TPU v7x, 128 devices: a whole 4x4x4 slice. The times are simulated.
128 devices in a mesh: req: 64 (over z, y, x), ctx: 2 (over core).
Axes of the slice: x: 4, y: 4, z: 4, core: 2. Of those that a mesh axis runs over, the one named last changes fastest.
Arguments:
- conv_input: bfloat16 [64, 512, 10240], P('req', 'ctx'), may hold values from -6 to 6
- gate_input: bfloat16 [64, 512, 8192], P('req', 'ctx'), may hold values from -6 to 6
- dt_raw: bfloat16 [64, 512, 128], P('req', 'ctx'), may hold values from -3 to 3
- conv_weight: float32 [4, 10240], replicated, may hold values from -3 to 3
- conv_bias: float32 [10240], replicated, may hold values from -3 to 3
- dt_bias: float32 [128], replicated
- a_log: float32 [128], replicated
- d_skip: float32 [128], replicated, may hold values from 0.5 to 2
- norm_weight: float32 [8192], replicated, may hold values from 0.5 to 1.5
- conv_cache: bfloat16 [64, 3, 10240], P('req'), may hold values from -6 to 6
- state_pool: float32 [16384, 64, 128], P(('req', 'ctx')), may hold values from -6 to 6
- page_owner: int32 [64, 128], replicated, may hold values from 0 to 127, as said below
- page_slot: int32 [64, 128], replicated, may hold values from 0 to 127, as said below
- prefix_len: int32 [64], replicated, may hold values from 0 to 32767, as said below
- new_count: int32 [64], replicated, may hold values from 64 to 512, as said below
Outputs:
- mixed: bfloat16 [64, 512, 8192], P('req', 'ctx')
- new_conv: bfloat16 [64, 3, 10240], P('req')
- new_pool: float32 [16384, 64, 128], P(('req', 'ctx'))
Inputs may be any that keep to these rules, and one draw needn't show every extreme that they name: `page_owner`: page j of request r holds rows j * 64 to (j + 1) * 64 - 1 of its state; devices are counted as req index times the ctx axis's size plus ctx index. The 64 pages j of one request with the same j // 64 lie on different devices, and every device holds exactly 64 pages of all requests together. `page_slot`: the pages held by one device lie in different slots; other slots hold nothing of these requests. `prefix_len`: some request has prefix length 0 in every draw. `new_count`: both ends are reached in every draw; the new tokens of a request fill its first slots.
All inputs are finite; a program needn't handle non-finite values.
Results may differ from a plain program's by a relative error of at most 0.0095.
Values may be sent and summed in bfloat16 or wider, within the bound.
No kernel may reach another device: no remote copies, remote signals or barrier semaphores. Data moves between devices by JAX's collectives and lax.ppermute only.
A program may use at most 192 MiB of HBM per device.

v0:
```python
import jax
import jax.numpy as jnp
from jax import lax
from jax.sharding import PartitionSpec as P

GROUPS = 8


def passed_along(value, axis, steps):
    count = lax.axis_size(axis)
    first, last = (max(0, -steps), min(count, count - steps))
    return lax.ppermute(value, axis, [(source, source + steps) for source in range(first, last)])


def prefix_2(x, axis, combine, identity):
    count, mine = (lax.axis_size(axis), lax.axis_index(axis))
    everything = jax.tree.map(lambda part: lax.all_gather(part, axis), x)
    start = jax.tree.map(
        lambda part, zero: jnp.broadcast_to(jnp.asarray(zero, part.dtype), part.shape), x, identity
    )

    def step(k, before):
        reached = k < mine
        new = combine(before, jax.tree.map(lambda part: part[k], everything))
        return jax.tree.map(lambda a, b: jnp.where(reached, a, b), new, before)

    return lax.fori_loop(0, count, step, start)


def conv_silu(extended, conv_weight, conv_bias, count_rows):
    accum = jnp.broadcast_to(conv_bias, (count_rows, conv_bias.shape[0]))
    for tap in range(conv_weight.shape[0]):
        accum = accum + conv_weight[tap] * extended[tap : tap + count_rows].astype(jnp.float32)
    return jax.nn.silu(accum).astype(jnp.bfloat16)


def local_block(inputs, b_proj, c_proj, step_size, log_decay):
    rows, heads, width = inputs.shape
    groups = b_proj.shape[1]
    per_group = heads // groups
    cumulative = jnp.cumsum(log_decay, axis=0)
    lower = jnp.arange(rows)[:, None] >= jnp.arange(rows)[None, :]
    grouped_x = jnp.moveaxis(inputs.reshape(rows, groups, per_group, width), 1, 0)
    grouped_cum = jnp.moveaxis(cumulative.reshape(rows, groups, per_group), 1, 0)
    grouped_dt = jnp.moveaxis(step_size.reshape(rows, groups, per_group), 1, 0)

    def per_head_group(items):
        x_grp, b_grp, c_grp, cum_grp, dt_grp = items
        scores = jnp.dot(c_grp, b_grp.T, preferred_element_type=jnp.float32)
        gap = cum_grp.T[:, :, None] - cum_grp.T[:, None, :]
        decay = jnp.where(lower, jnp.exp(jnp.where(lower, gap, 0.0)), 0.0)
        weights = (scores[None] * decay * dt_grp.T[:, None, :]).astype(jnp.bfloat16)
        intra = jnp.einsum("hts,shp->thp", weights, x_grp, preferred_element_type=jnp.float32)
        ending = jnp.exp(cum_grp[-1][None, :] - cum_grp) * dt_grp
        scaled = (x_grp.astype(jnp.float32) * ending[:, :, None]).astype(jnp.bfloat16)
        state = jnp.einsum("shp,sn->hpn", scaled, b_grp, preferred_element_type=jnp.float32)
        return (intra, state)

    intra, states = lax.map(
        per_head_group,
        (
            grouped_x,
            jnp.moveaxis(b_proj, 1, 0),
            jnp.moveaxis(c_proj, 1, 0),
            grouped_cum,
            grouped_dt,
        ),
    )
    intra = jnp.moveaxis(intra, 0, 1).reshape(rows, heads, width)
    return (intra, states.reshape(heads, width, -1), cumulative)


def state_part(c_proj, cumulative, state):
    rows, groups, _ = c_proj.shape
    heads = cumulative.shape[1]
    rounded = state.astype(jnp.bfloat16).reshape(groups, -1, state.shape[2])
    product = jnp.einsum("tgn,gkn->tgk", c_proj, rounded, preferred_element_type=jnp.float32)
    return product.reshape(rows, heads, -1) * jnp.exp(cumulative)[:, :, None]


def finish(mixer, inputs, gate_in, d_skip, norm_weight, live, groups):
    rows = mixer.shape[0]
    summed = mixer + d_skip[None, :, None] * inputs.astype(jnp.float32)
    gated = summed.reshape(rows, -1) * jax.nn.silu(gate_in.astype(jnp.float32))
    grouped = gated.reshape(rows, groups, -1)
    factor = lax.rsqrt(jnp.mean(grouped * grouped, axis=-1, keepdims=True) + 1e-05)
    normed = (grouped * factor).reshape(rows, -1) * norm_weight
    return jnp.where(live[:, None], normed, 0.0).astype(jnp.bfloat16)


def combine_pairs(earlier, later):
    return (earlier[0] * later[0], later[0][:, None, None] * earlier[1] + later[1])


def local(
    conv_input,
    gate_input,
    dt_raw,
    conv_weight,
    conv_bias,
    dt_bias,
    a_log,
    d_skip,
    norm_weight,
    conv_cache,
    state_pool,
    page_owner,
    page_slot,
    prefix_len,
    new_count,
):
    req_count = lax.axis_size("req")
    ctx_count = lax.axis_size("ctx")
    devices = req_count * ctx_count
    req_index = lax.axis_index("req")
    ctx_index = lax.axis_index("ctx")
    own_index = req_index * ctx_count + ctx_index
    tokens = conv_input[0]
    rows = tokens.shape[0]
    heads = dt_raw.shape[2]
    inner = gate_input.shape[2]
    width = inner // heads
    nstate = state_pool.shape[2]
    page_rows = state_pool.shape[1]
    pool_slots = state_pool.shape[0]
    head_share = heads // ctx_count
    device_pages = page_owner.shape[1] // ctx_count
    rim = conv_weight.shape[0] - 1
    prefix = prefix_len[req_index]
    count = new_count[req_index]
    owner_table = page_owner.reshape(devices, device_pages)
    slot_table = page_slot.reshape(devices, device_pages)
    matches = owner_table == own_index
    slot_for = jnp.sum(jnp.where(matches, slot_table, 0), axis=1)
    present = jnp.any(matches, axis=1)
    outgoing = jnp.where(present[:, None, None], state_pool[slot_for], 0.0)
    incoming = lax.all_to_all(outgoing, ("req", "ctx"), split_axis=0, concat_axis=0, tiled=True)
    my_owners = owner_table[own_index]
    initial_share = incoming[my_owners] * (prefix > 0).astype(jnp.float32)
    previous = passed_along(tokens[rows - rim :], "ctx", 1)
    keep_rows = jnp.arange(rim) >= rim - prefix
    cached = jnp.where(keep_rows[:, None], conv_cache[0], jnp.zeros_like(conv_cache[0]))
    rim_rows = jnp.where(ctx_index == 0, cached, previous)
    extended = jnp.concatenate([rim_rows, tokens], axis=0)
    active = conv_silu(extended, conv_weight, conv_bias, rows)
    groups = GROUPS
    inputs = active[:, :inner].reshape(rows, heads, width)
    b_proj = active[:, inner : inner + groups * nstate].reshape(rows, groups, nstate)
    c_proj = active[:, inner + groups * nstate :].reshape(rows, groups, nstate)
    positions = ctx_index * rows + jnp.arange(rows)
    live = positions < count
    step_size = jax.nn.softplus(dt_raw[0].astype(jnp.float32) + dt_bias) * live[:, None].astype(
        jnp.float32
    )
    log_decay = step_size * -jnp.exp(a_log)
    intra, states, cumulative = local_block(inputs, b_proj, c_proj, step_size, log_decay)
    decays = jnp.exp(cumulative[-1])
    all_decays = lax.all_gather(decays[None, :], "ctx", axis=0, tiled=True)
    block_ids = jnp.arange(ctx_count)
    initial = lax.all_gather(initial_share, "ctx", axis=0, tiled=True)
    before_decay, before_state = prefix_2(
        (decays, states), "ctx", combine_pairs, (jnp.ones_like(decays), jnp.zeros_like(states))
    )
    device_start = before_state + before_decay[:, None, None] * initial
    suffix = jnp.prod(jnp.where((block_ids > ctx_index)[:, None], all_decays, 1.0), axis=0)
    summed = lax.psum_scatter(
        (suffix[:, None, None] * states).astype(jnp.bfloat16),
        "ctx",
        scatter_dimension=0,
        tiled=True,
    ).astype(jnp.float32)
    whole_decay = lax.dynamic_slice_in_dim(
        jnp.prod(all_decays, axis=0), ctx_index * head_share, head_share, 0
    )
    final_share = summed + whole_decay[:, None, None] * initial_share
    carried = state_part(c_proj, cumulative, device_start)
    output = finish(intra + carried, inputs, gate_input[0], d_skip, norm_weight, live, groups)
    targets = count - rim + jnp.arange(rim)
    picks = (positions[None, :] == targets[:, None]).astype(jnp.bfloat16)
    tail_rows = jnp.dot(picks, tokens, preferred_element_type=jnp.float32)
    new_tail = lax.psum(tail_rows.astype(jnp.bfloat16), "ctx")
    outbound = jnp.zeros((devices, page_rows, nstate), jnp.float32).at[my_owners].set(final_share)
    returned = lax.all_to_all(
        outbound.astype(jnp.bfloat16), ("req", "ctx"), split_axis=0, concat_axis=0, tiled=True
    ).astype(outbound.dtype)
    target_slots = jnp.where(present, slot_for, pool_slots)
    new_pool = state_pool.at[target_slots].set(returned, mode="drop")
    return (output[None], new_tail[None], new_pool)


def solution(mesh):
    return jax.shard_map(
        local,
        mesh=mesh,
        in_specs=(
            P("req", "ctx", None),
            P("req", "ctx", None),
            P("req", "ctx", None),
            P(),
            P(),
            P(),
            P(),
            P(),
            P(),
            P("req", None, None),
            P(("req", "ctx"), None, None),
            P(),
            P(),
            P(),
            P(),
        ),
        out_specs=(P("req", "ctx", None), P("req", None, None), P(("req", "ctx"), None, None)),
        check_vma=False,
    )
```

profile of v0, /device:TPU:1, one launch (start us, length us, event | category | flops | bytes accessed | tf_op | source)
XLA Modules:
  0.0 305.4 jit_solution(7194455624240730033)
XLA Ops:
  7.2 4.8 %copy.85 = f32[128,64,128]{2,1,0:T(8,128)} copy(f32[128,64,128]{2,1,0:T(8,128)} %param.29) | data formatting | bytes 8388608
  12.0 1.0 slice_bitcast_fusion
  13.0 1.3 collective-permute-start
  14.3 8.0 %copy.44 = bf16[1,256,10240]{1,2,0:T(8,128)(2,1)} copy(bf16[1,256,10240]{2,1,0:T(8,128)(2,1)} %param.19) | data formatting | bytes 10485760 | tf_op args[0]
  22.6 0.6 dynamic_slice.44
  23.2 0.6 fusion.60
  24.6 0.6 dynamic_slice.45
  25.2 2.1 copy.42
  27.4 2.9 all-gather
  31.2 2.1 copy.43
  33.3 2.8 fusion.45
  36.1 0.9 slice-done.3
  37.0 15.6 %multiply_convert_fusion.7 = bf16[256,10240]{0,1:T(8,128)(2,1)S(1)} fusion(bf16[256,10240]{0,1:T(8,128)(2,1)S(1)} %bitcast.190, bf16[3,10240]{0,1:T(8,128)(2,1)S(1)} %fusion.45, f32[10240]{0:T(1024)S(1)} %bitcast.207, f32[10240]{0:T(1024)S(1)} %bitcast.208, f32[10240]{0:T(1024)S(1)} %bitcast.206, f32[10240]{0:T(1024)S(1)} %bitcast.205, f32[10240]{0:T(1024)S(1)} %copy-done.5), kind=kLoop, calls=%fused_computation.50 | loop fusion | flops 68157440 | bytes 10752000 | tf_op jit(solution)/shard_map/convert_element_type | solution.py:34
  52.8 2.5 slice.74
  55.3 1.1 copy-done
  56.3 0.3 copy.45
  56.6 50.0 %while.30 = (s32[]{:T(128)}, f32[8,256,16,64]{1,3,2,0:T(8,128)}, f32[8,16,64,128]{3,2,1,0:T(8,128)}, bf16[8,256,16,64]{1,3,2,0:T(8,128)(2,1)}, bf16[8,256,128]{1...) while((s32[]{:T(128)}, f32[8,256,16,64]{1,3,2,0:T(8,128)}, ...), condition=%wide.region_3.4_spmd.clone.clone, body=%wide.region_2.3_spmd.clone.clone.sunk | while | flops 225255424 | bytes 3657673 | solution.py:59
  56.6 0.2 fusion.82
  56.9 3.6 %fusion.83 = f32[8,256,16,64]{1,3,2,0:T(8,128)} fusion(f32[8,256,16,64]{1,3,2,0:T(8,128)} %get-tuple-element.405, s32[]{:T(128)} %get-tuple-element.404, f32[16,256]{1,0:T(8,128)S(1)} %get-tuple-element.383, f32[16,256]{1,0:T(8,128)S(1)} %get-tuple-element.384, f32[256,256]{1,0:T(8,128)S(1)} %fusion.82, ...), kind=kOutput, calls=%fused_computation.14.clone.1 | convolution fusion | flops 140509184 | bytes 1950720 | tf_op jit(solution)/shard_map/while/body/eval_jaxpr/hts,shp->thp/dot_general | solution.py:53
  60.7 2.2 fusion.84
  63.1 3.6 %fusion.83 = f32[8,256,16,64]{1,3,2,0:T(8,128)} fusion(f32[8,256,16,64]{1,3,2,0:T(8,128)} %get-tuple-element.405, s32[]{:T(128)} %get-tuple-element.404, f32[16,256]{1,0:T(8,128)S(1)} %get-tuple-element.383, f32[16,256]{1,0:T(8,128)S(1)} %get-tuple-element.384, f32[256,256]{1,0:T(8,128)S(1)} %fusion.82, ...), kind=kOutput, calls=%fused_computation.14.clone.1 | convolution fusion | flops 140509184 | bytes 1950720 | tf_op jit(solution)/shard_map/while/body/eval_jaxpr/hts,shp->thp/dot_general | solution.py:53
  66.9 2.2 fusion.84
  69.1 0.2 fusion.82
  69.4 3.6 %fusion.83 = f32[8,256,16,64]{1,3,2,0:T(8,128)} fusion(f32[8,256,16,64]{1,3,2,0:T(8,128)} %get-tuple-element.405, s32[]{:T(128)} %get-tuple-element.404, f32[16,256]{1,0:T(8,128)S(1)} %get-tuple-element.383, f32[16,256]{1,0:T(8,128)S(1)} %get-tuple-element.384, f32[256,256]{1,0:T(8,128)S(1)} %fusion.82, ...), kind=kOutput, calls=%fused_computation.14.clone.1 | convolution fusion | flops 140509184 | bytes 1950720 | tf_op jit(solution)/shard_map/while/body/eval_jaxpr/hts,shp->thp/dot_general | solution.py:53
  73.2 2.2 fusion.84
  75.4 0.2 fusion.82
  75.6 3.6 %fusion.83 = f32[8,256,16,64]{1,3,2,0:T(8,128)} fusion(f32[8,256,16,64]{1,3,2,0:T(8,128)} %get-tuple-element.405, s32[]{:T(128)} %get-tuple-element.404, f32[16,256]{1,0:T(8,128)S(1)} %get-tuple-element.383, f32[16,256]{1,0:T(8,128)S(1)} %get-tuple-element.384, f32[256,256]{1,0:T(8,128)S(1)} %fusion.82, ...), kind=kOutput, calls=%fused_computation.14.clone.1 | convolution fusion | flops 140509184 | bytes 1950720 | tf_op jit(solution)/shard_map/while/body/eval_jaxpr/hts,shp->thp/dot_general | solution.py:53
  79.4 2.1 fusion.84
  81.8 3.6 %fusion.83 = f32[8,256,16,64]{1,3,2,0:T(8,128)} fusion(f32[8,256,16,64]{1,3,2,0:T(8,128)} %get-tuple-element.405, s32[]{:T(128)} %get-tuple-element.404, f32[16,256]{1,0:T(8,128)S(1)} %get-tuple-element.383, f32[16,256]{1,0:T(8,128)S(1)} %get-tuple-element.384, f32[256,256]{1,0:T(8,128)S(1)} %fusion.82, ...), kind=kOutput, calls=%fused_computation.14.clone.1 | convolution fusion | flops 140509184 | bytes 1950720 | tf_op jit(solution)/shard_map/while/body/eval_jaxpr/hts,shp->thp/dot_general | solution.py:53
  85.7 2.2 fusion.84
  88.1 3.6 %fusion.83 = f32[8,256,16,64]{1,3,2,0:T(8,128)} fusion(f32[8,256,16,64]{1,3,2,0:T(8,128)} %get-tuple-element.405, s32[]{:T(128)} %get-tuple-element.404, f32[16,256]{1,0:T(8,128)S(1)} %get-tuple-element.383, f32[16,256]{1,0:T(8,128)S(1)} %get-tuple-element.384, f32[256,256]{1,0:T(8,128)S(1)} %fusion.82, ...), kind=kOutput, calls=%fused_computation.14.clone.1 | convolution fusion | flops 140509184 | bytes 1950720 | tf_op jit(solution)/shard_map/while/body/eval_jaxpr/hts,shp->thp/dot_general | solution.py:53
  91.9 2.2 fusion.84
  94.3 3.6 %fusion.83 = f32[8,256,16,64]{1,3,2,0:T(8,128)} fusion(f32[8,256,16,64]{1,3,2,0:T(8,128)} %get-tuple-element.405, s32[]{:T(128)} %get-tuple-element.404, f32[16,256]{1,0:T(8,128)S(1)} %get-tuple-element.383, f32[16,256]{1,0:T(8,128)S(1)} %get-tuple-element.384, f32[256,256]{1,0:T(8,128)S(1)} %fusion.82, ...), kind=kOutput, calls=%fused_computation.14.clone.1 | convolution fusion | flops 140509184 | bytes 1950720 | tf_op jit(solution)/shard_map/while/body/eval_jaxpr/hts,shp->thp/dot_general | solution.py:53
  98.2 2.2 fusion.84
  100.6 3.6 %fusion.83 = f32[8,256,16,64]{1,3,2,0:T(8,128)} fusion(f32[8,256,16,64]{1,3,2,0:T(8,128)} %get-tuple-element.405, s32[]{:T(128)} %get-tuple-element.404, f32[16,256]{1,0:T(8,128)S(1)} %get-tuple-element.383, f32[16,256]{1,0:T(8,128)S(1)} %get-tuple-element.384, f32[256,256]{1,0:T(8,128)S(1)} %fusion.82, ...), kind=kOutput, calls=%fused_computation.14.clone.1 | convolution fusion | flops 140509184 | bytes 1950720 | tf_op jit(solution)/shard_map/while/body/eval_jaxpr/hts,shp->thp/dot_general | solution.py:53
  104.4 2.2 fusion.84
  106.6 3.9 %fusion.44 = bf16[128,64,128]{2,1,0:T(8,128)(2,1)} fusion(f32[8,16,64,128]{3,2,1,0:T(8,128)} %get-tuple-element.165, f32[128]{0:T(128)S(1)} %select_reduce_fusion.1), kind=kLoop, calls=%fused_computation.72 | loop fusion | flops 2097152 | bytes 6291968 | tf_op jit(solution)/shard_map/convert_element_type | solution.py:167
  110.6 0.7 all-gather.4.cloned.1.call-update
  111.7 5.0 %gather_fusion = f32[128,64,128]{2,1,0:T(8,128)} fusion(f32[128,64,128]{2,1,0:T(8,128)} %copy.85, s32[1024]{0:T(1024)S(1)} %pad_clamp_fusion.1), kind=kCustom, calls=%fused_computation | custom fusion | bytes 8389120 | tf_op jit(solution)/shard_map/gather | solution.py:136
  116.7 4.6 %broadcast_select_fusion.2 = f32[128,64,128]{2,1,0:T(8,128)} fusion(f32[128,64,128]{2,1,0:T(8,128)} %gather_fusion, pred[128]{0:T(512)(128)(4,1)S(1)} %get-tuple-element.285), kind=kLoop, calls=%fused_computation.77 | loop fusion | flops 1048576 | bytes 8388736 | tf_op jit(solution)/shard_map/jit(_where)/select_n | solution.py:136
  121.3 11.2 %all-to-all-start = ((f32[128,64,128]{2,1,0:T(8,128)}), f32[128,64,128]{2,1,0:T(8,128)}, u32[]{:S(2)}, u32[]{:S(2)}) async-start(f32[128,64,128]{2,1,0:T(8,128)} %broadcast_select_fusion.2), calls=%async_computation | async-start | bytes 8388608 | tf_op jit(solution)/shard_map/all_to_all | solution.py:137
  133.3 51.8 %all-to-all-done = f32[128,64,128]{2,1,0:T(8,128)} async-done(((f32[128,64,128]{2,1,0:T(8,128)}), f32[128,64,128]{2,1,0:T(8,128)}, u32[]{:S(2)}, u32[]{:S(2)}) %all-to-all-start) | async-done | bytes 4194336 | tf_op jit(solution)/shard_map/all_to_all | solution.py:137
  185.1 4.2 %gather_fusion.1 = f32[64,64,128]{2,1,0:T(8,128)} fusion(f32[128,64,128]{2,1,0:T(8,128)} %all-to-all-done, s32[1024]{0:T(1024)S(1)} %pad_clamp_fusion), kind=kCustom, calls=%fused_computation.1 | custom fusion | bytes 4194560 | tf_op jit(solution)/shard_map/gather | solution.py:139
  189.3 3.6 %multiply_add_fusion = (f32[64,64,128]{2,1,0:T(8,128)S(1)}, f32[64,64,128]{2,1,0:T(8,128)}) fusion(bf16[64,64,128]{2,1,0:T(8,128)(2,1)} %reduce-scatter.2.cloned.1.call-done, f32[64]{0:T(128)S(1)} %dynamic_slice.47, f32[64,64,128]{2,1,0:T(8,128)} %gather_fusion.1, f32[]{:T(128)} %bitcast.34), kind=kLoop, calls=%fused_computation.76 | loop fusion | flops 2097152 | bytes 7340292 | tf_op jit(solution)/shard_map/add | solution.py:175
  192.9 2.5 broadcast.145
  195.4 8.8 %scatter_fusion = f32[128,64,128]{2,1,0:T(8,128)} fusion(f32[128,64,128]{2,1,0:T(8,128)} %broadcast.145, s32[64]{0:T(128)S(1)} %fusion.55, f32[64,64,128]{2,1,0:T(8,128)S(1)} %get-tuple-element.281), kind=kCustom, calls=%fused_computation.2 | custom fusion | bytes 6291712 | tf_op jit(solution)/shard_map/scatter | solution.py:182
  204.2 4.0 %convert_element_type.106 = bf16[128,64,128]{2,1,0:T(8,128)(2,1)} convert(f32[128,64,128]{2,1,0:T(8,128)} %scatter_fusion) | non-fusion elementwise | flops 1048576 | bytes 6291456 | tf_op jit(solution)/shard_map/convert_element_type | solution.py:184
  208.2 4.5 %all-to-all-start.1 = ((bf16[128,64,128]{2,1,0:T(8,128)(2,1)}), bf16[128,64,128]{2,1,0:T(8,128)(2,1)S(1)}, u32[]{:S(2)}, u32[]{:S(2)}) async-start(bf16[128,64,128]{2,1,0:T(8,128)(2,1)} %convert_element_type.106), calls=%async_computation.2 | async-start | bytes 4194304 | tf_op jit(solution)/shard_map/all_to_all | solution.py:183
  212.9 6.4 %copy.54 = bf16[1,256,8192]{1,2,0:T(8,128)(2,1)} copy(bf16[1,256,8192]{2,1,0:T(8,128)(2,1)} %param.20) | data formatting | bytes 8388608 | tf_op args[1]
  220.1 3.3 %fusion.31 = bf16[1,3,10240]{2,1,0:T(4,128)(2,1)S(1)} fusion(bf16[1,256,10240]{2,1,0:T(8,128)(2,1)} %param.19, s32[256]{0:T(256)S(1)} %iota_add_fusion, s32[3]{0:T(128)S(1)} %iota_add_fusion.1), kind=kOutput, calls=%fused_computation.47 | convolution fusion | flops 15760128 | bytes 5305356 | tf_op jit(solution)/shard_map/dot_general | solution.py:180
  223.4 5.4 %psum.7 = bf16[1,3,10240]{2,1,0:T(4,128)(2,1)} all-reduce(bf16[1,3,10240]{2,1,0:T(4,128)(2,1)S(1)} %fusion.31), channel_id=1, replica_groups=mesh['req'=64,'ctx'=2] {'ctx'}, use_global_device_ids=true, to_apply=%region_9.10 | all-reduce | flops 30720 | bytes 122880 | tf_op jit(solution)/shard_map/psum | solution.py:181
  228.7 14.6 %all-to-all-done.1 = bf16[128,64,128]{2,1,0:T(8,128)(2,1)S(1)} async-done(((bf16[128,64,128]{2,1,0:T(8,128)(2,1)}), bf16[128,64,128]{2,1,0:T(8,128)(2,1)S(1)}, u32[]{:S(2)}, u32[]{:S(2)}) %all-to-all-start.1) | async-done | bytes 2097184 | tf_op jit(solution)/shard_map/all_to_all | solution.py:183
  243.4 2.5 convert_element_type.107
  245.9 19.0 %scatter_fusion.1 = f32[128,64,128]{2,1,0:T(8,128)} fusion(f32[128,64,128]{2,1,0:T(8,128)} %copy.85, s32[128]{0:T(128)S(1)} %get-tuple-element.297, f32[128,64,128]{2,1,0:T(8,128)} %convert_element_type.107), kind=kCustom, calls=%fused_computation.3 | custom fusion | bytes 12583424 | tf_op jit(solution)/shard_map/scatter | solution.py:187
  264.9 10.8 %while.31 = (s32[]{:T(128)}, f32[128]{0:T(128)S(1)}, f32[128,64,128]{2,1,0:T(8,128)}, s32[]{:T(128)}, f32[2,128]{1,0:T(2,128)S(1)}, /*index=5*/f32[2,128,64,128]{3,2,1,0:T(8,128)}, s32[]{:T(128)}, s32[]{:T(128)}) while((s32[]{:T(128)}, f32[128]{0:T(128)S(1)}, f32[128,64,128]{2,1,0:T(8,128)}, s32[]{:T(128)}, ...), condition=%wide.region_5.6_spmd.clone, body=%wide.region_4.5_spmd.clone.sunk | while | flops 4194692 | bytes 12585587 | solution.py:27
  265.0 4.7 %fusion.85 = f32[128,64,128]{2,1,0:T(8,128)} fusion(f32[2,128,64,128]{3,2,1,0:T(8,128)} %get-tuple-element.447, s32[]{:T(128)} %get-tuple-element.434, f32[128,64,128]{2,1,0:T(8,128)} %get-tuple-element.436, f32[128]{0:T(128)S(1)} %get-tuple-element.392, pred[]{:T(512)S(6)} %compare.3, pred[]{:T(512)S(6)} %lt.103), kind=kLoop, calls=%fused_computation.42.clone.1 | loop fusion | flops 4194304 | bytes 12583430 | tf_op jit(solution)/shard_map/while/body/eval_jaxpr/jit(_where)/select_n | solution.py:25
  269.7 6.0 %fusion.85 = f32[128,64,128]{2,1,0:T(8,128)} fusion(f32[2,128,64,128]{3,2,1,0:T(8,128)} %get-tuple-element.447, s32[]{:T(128)} %get-tuple-element.434, f32[128,64,128]{2,1,0:T(8,128)} %get-tuple-element.436, f32[128]{0:T(128)S(1)} %get-tuple-element.392, pred[]{:T(512)S(6)} %compare.3, pred[]{:T(512)S(6)} %lt.103), kind=kLoop, calls=%fused_computation.42.clone.1 | loop fusion | flops 4194304 | bytes 12583430 | tf_op jit(solution)/shard_map/while/body/eval_jaxpr/jit(_where)/select_n | solution.py:25
  275.7 4.1 %add_convert_fusion = bf16[128,64,128]{2,1,0:T(8,128)(2,1)S(1)} fusion(f32[128,64,128]{2,1,0:T(8,128)} %get-tuple-element.166, f32[128,64,128]{2,1,0:T(8,128)} %all-gather.6.cloned.1.call-done, f32[128]{0:T(128)S(1)} %get-tuple-element.167), kind=kLoop, calls=%fused_computation.73 | loop fusion | flops 3145728 | bytes 10486272 | tf_op jit(solution)/shard_map/convert_element_type | solution.py:76
  279.8 1.2 fusion.64
  281.1 0.9 slice-done.1
  282.0 1.3 copy-done.1
  283.3 6.7 %bitcast_reduce_fusion = (f32[256,8]{0,1:T(8,128)S(1)}, f32[256,8192]{0,1:T(8,128)S(1)}) fusion(bf16[1,256,8192]{1,2,0:T(8,128)(2,1)S(1)} %copy-done.1, bf16[256,10240]{0,1:T(8,128)(2,1)S(1)} %bitcast.187, f32[8192]{0:T(1024)S(1)} %mul.250, f32[256,128]{0,1:T(8,128)S(1)} %copy.53, f32[8,1024,256]{2,1,0:T(8,128)S(1)} %fusion.64, ...), kind=kLoop, calls=%fused_computation.64 | loop fusion | flops 27260928 | bytes 33726464 | tf_op jit(solution)/shard_map/reduce_sum | solution.py:86
  290.0 2.6 fusion.40
  292.6 6.3 %copy.55 = bf16[1,256,8192]{2,1,0:T(8,128)(2,1)} copy(bf16[1,256,8192]{1,2,0:T(8,128)(2,1)} %bitcast.192) | data formatting | bytes 8388608
  (132 shorter events, 5.5 us)
Async XLA Ops:
  7.2 182.1 %reduce-scatter.2.cloned.1.call-start = ((), (), s32[]{:S(2)}) async-start(), calls=%async_computation.5 | async-start | bytes 3145728 | tf_op jit(solution)/shard_map/reduce_scatter | solution.py:166
  13.0 18.2 %collective-permute-start = (bf16[3,10240]{1,0:T(4,128)(2,1)S(1)}, bf16[3,10240]{1,0:T(4,128)(2,1)S(1)}, u32[]{:S(2)}, u32[]{:S(2)}) collective-permute-start(bf16[3,10240]{1,0:T(4,128)(2,1)S(1)} %slice_bitcast_fusion), channel_id=1, source_target_pairs={{0,1},{2,3},{4,5},{6,7},{8,9},{10,11},{12,13},{14,15},{16,17},{18,... | collective-permute-start | bytes 184328 | tf_op jit(solution)/shard_map/ppermute | solution.py:12
  14.3 8.1 %copy-start.4 = (bf16[1,256,128]{2,1,0:T(8,128)(2,1)S(1)}, bf16[1,256,128]{2,1,0:T(8,128)(2,1)}, u32[]{:S(2)}) copy-start(bf16[1,256,128]{2,1,0:T(8,128)(2,1)} %param.21) | copy-start | bytes 196612
  14.3 8.2 %copy-start.11 = (f32[128]{0:T(128)S(1)}, f32[128]{0:T(128)}, u32[]{:S(2)}) copy-start(f32[128]{0:T(128)} %param.25) | copy-start | bytes 1540
  14.3 8.2 %copy-start.9 = (f32[128]{0:T(128)S(1)}, f32[128]{0:T(128)}, u32[]{:S(2)}) copy-start(f32[128]{0:T(128)} %param.24) | copy-start | bytes 1540
  14.3 8.3 %copy-start.12 = (s32[64]{0:T(128)S(1)}, s32[64]{0:T(128)}, u32[]{:S(2)}) copy-start(s32[64]{0:T(128)} %param.33) | copy-start | bytes 772
  14.3 10.2 %copy-start.13 = (s32[64]{0:T(128)S(1)}, s32[64]{0:T(128)}, u32[]{:S(2)}) copy-start(s32[64]{0:T(128)} %param.32) | copy-start | bytes 772
  14.3 10.8 %copy-start.3 = (bf16[1,3,10240]{2,1,0:T(4,128)(2,1)S(1)}, bf16[1,3,10240]{2,1,0:T(4,128)(2,1)}, u32[]{:S(2)}) copy-start(bf16[1,3,10240]{2,1,0:T(4,128)(2,1)} %param.28) | copy-start | bytes 184324
  22.3 4.9 %copy-start.2 = (f32[4,10240]{1,0:T(4,128)S(1)}, f32[4,10240]{1,0:T(4,128)}, u32[]{:S(2)}) copy-start(f32[4,10240]{1,0:T(4,128)} %param.22) | copy-start | bytes 491524
  31.2 4.9 %slice-start.2 = ((s8[5242880]{0:T(1024)(128)(4,1)}), s8[1048576]{0:T(1024)(128)(4,1)S(1)}, s32[]{:S(2)}) async-start(s8[5242880]{0:T(1024)(128)(4,1)} %bitcast.188), calls=%async_computation.8 | async-start | bytes 2097152
  33.3 3.8 %slice-start.3 = ((s8[5242880]{0:T(1024)(128)(4,1)}), s8[4194304]{0:T(1024)(128)(4,1)S(1)}, s32[]{:S(2)}) async-start(s8[5242880]{0:T(1024)(128)(4,1)} %bitcast.188), calls=%async_computation.9 | async-start | bytes 8388608
  33.3 3.8 %copy-start.5 = (f32[10240]{0:T(1024)S(1)}, f32[10240]{0:T(1024)}, u32[]{:S(2)}) copy-start(f32[10240]{0:T(1024)} %param.23) | copy-start | bytes 122884
  52.7 3.7 %copy-start = (bf16[256,10240]{0,1:T(8,128)(2,1)}, bf16[256,10240]{0,1:T(8,128)(2,1)S(1)}, u32[]{:S(2)}) copy-start(bf16[256,10240]{0,1:T(8,128)(2,1)S(1)} %multiply_convert_fusion.7) | copy-start | bytes 15728644
  110.5 0.8 copy-start.7
  110.5 0.9 copy-start.8
  110.5 154.4 %all-gather.4.cloned.1.call-start = ((), (), s32[]{:S(2)}) async-start(), calls=%async_computation.3 | async-start | bytes 12582912 | tf_op jit(solution)/shard_map/all_gather | solution.py:17
  121.3 63.8 %all-to-all-start = ((f32[128,64,128]{2,1,0:T(8,128)}), f32[128,64,128]{2,1,0:T(8,128)}, u32[]{:S(2)}, u32[]{:S(2)}) async-start(f32[128,64,128]{2,1,0:T(8,128)} %broadcast_select_fusion.2), calls=%async_computation | async-start | bytes 8388608 | tf_op jit(solution)/shard_map/all_to_all | solution.py:137
  132.4 143.3 %all-gather.6.cloned.1.call-start = ((), (), s32[]{:S(2)}) async-start(), calls=%async_computation.4 | async-start | bytes 6291456 | tf_op jit(solution)/shard_map/all_gather | solution.py:160
  208.2 35.2 %all-to-all-start.1 = ((bf16[128,64,128]{2,1,0:T(8,128)(2,1)}), bf16[128,64,128]{2,1,0:T(8,128)(2,1)S(1)}, u32[]{:S(2)}, u32[]{:S(2)}) async-start(bf16[128,64,128]{2,1,0:T(8,128)(2,1)} %convert_element_type.106), calls=%async_computation.2 | async-start | bytes 4194304 | tf_op jit(solution)/shard_map/all_to_all | solution.py:183
  212.9 6.4 %copy-start.10 = (f32[128]{0:T(128)S(1)}, f32[128]{0:T(128)}, u32[]{:S(2)}) copy-start(f32[128]{0:T(128)} %param.26) | copy-start | bytes 1540
  275.7 5.4 %slice-start = ((s8[5242880]{0:T(1024)(128)(4,1)}), s8[1048576]{0:T(1024)(128)(4,1)S(1)}, s32[]{:S(2)}) async-start(s8[5242880]{0:T(1024)(128)(4,1)} %bitcast.186), calls=%async_computation.6 | async-start | bytes 2097152
  279.8 2.2 slice-start.1
  279.8 3.5 %copy-start.1 = (bf16[1,256,8192]{1,2,0:T(8,128)(2,1)S(1)}, bf16[1,256,8192]{1,2,0:T(8,128)(2,1)}, u32[]{:S(2)}) copy-start(bf16[1,256,8192]{1,2,0:T(8,128)(2,1)} %copy.54) | copy-start | bytes 12582916
  283.3 6.7 %copy-start.6 = (f32[8192]{0:T(1024)S(1)}, f32[8192]{0:T(1024)}, u32[]{:S(2)}) copy-start(f32[8192]{0:T(1024)} %param.27) | copy-start | bytes 98308
Sparse Core Ops, SparseCore 0:
  110.6 15.1 reduce-scatter.1
  127.5 23.8 all-gather.3
  193.0 12.3 all-gather.5
where the time goes:
time: 308 us; the launch traced here: 305 us
  local copies, waits for them, and re-layouts  80.8 us (26%)
  waiting for transfers between devices  67.2 us (22%)
  other arithmetic  63.5 us (21%)
  matrix products  52.2 us (17%)
  starting transfers between devices  17.1 us (6%)
  between operations  16.1 us (5%)
  blocking collectives  8.26 us (3%)
    all_to_all x1, waiting for transfers between devices, local(): lax.all_to_all(outgoing, ('req', 'ctx'), split_axis=0, concat_axis=0, til...  51.8 us
    unnamed x44, local copies, waits for them, and re-layouts  31.9 us
    dot_general x8, matrix products, per_head_group(): jnp.einsum('hts,shp->thp', weights, x_grp, preferred_element_type=jnp.flo...  28.7 us
    scatter x1, local copies, waits for them, and re-layouts, local(): new_pool = state_pool.at[target_slots].set(returned, mode='drop')  19 us
    dot_general x8, matrix products, per_head_group(): jnp.einsum('shp,sn->hpn', scaled, b_grp, preferred_element_type=jnp.float32)  17.3 us
    convert_element_type x1, other arithmetic, conv_silu(): return jax.nn.silu(accum).astype(jnp.bfloat16)  15.6 us
    all_to_all x1, waiting for transfers between devices, local(): lax.all_to_all(outbound.astype(jnp.bfloat16), ('req', 'ctx'), split_axis=...  14.6 us
    all_to_all x1, starting transfers between devices, local(): lax.all_to_all(outgoing, ('req', 'ctx'), split_axis=0, concat_axis=0, til...  11.2 us
  transfers between devices with their start and end apart: 6, of which 2 were waited for; matrix products, arithmetic and copies ran while one was open for 29% of the time, Pallas kernels for 0%

commit v1 on v0

v1 whole, which is shorter than its diff:
```python
import jax
import jax.numpy as jnp
from jax import lax
from jax.experimental import pallas as pl
from jax.experimental.pallas import tpu as pltpu
from jax.sharding import PartitionSpec as P

GROUPS = 8
LANES = 128
TOP = 88.72
F32 = jnp.float32
BF16 = jnp.bfloat16


def swapped(value):
    return lax.ppermute(value, "ctx", [(0, 1), (1, 0)])


def silu(value):
    half = 0.5 * value
    return half + half * jnp.tanh(half)


def cost(flops, nbytes, trans=0):
    return pl.CostEstimate(flops=flops, bytes_accessed=nbytes, transcendentals=trans)


def gather_body(dev_ref, pool_ref, out_ref):
    step = pl.program_id(0)
    for k in range(pool_ref.shape[0]):
        device = dev_ref[step * pool_ref.shape[0] + k]

        @pl.when(device >= 0)
        def _():
            out_ref[device] = pool_ref[k].astype(BF16)


def gather_pages(dev_of_slot, pool, devices):
    slots, rows, width = pool.shape
    chunk = min(32, slots)
    return pl.pallas_call(
        gather_body,
        out_shape=jax.ShapeDtypeStruct((devices, rows, width), BF16),
        grid_spec=pltpu.PrefetchScalarGridSpec(
            num_scalar_prefetch=1,
            grid=(slots // chunk,),
            in_specs=[pl.BlockSpec((chunk, rows, width), lambda i, d: (i, 0, 0))],
            out_specs=pl.BlockSpec((devices, rows, width), lambda i, d: (0, 0, 0)),
        ),
        cost_estimate=cost(slots * rows * width, slots * rows * width * 6),
        name="gather_pages",
    )(dev_of_slot, pool)


def steps_body(at_ref, raw_ref, bias_ref, alog_ref, cum_ref, shift_ref, ending_ref, decay_ref):
    rows, heads = cum_ref.shape
    pos = at_ref[0] + lax.broadcasted_iota(jnp.int32, (rows, heads), 0)
    live = pos < at_ref[1]
    value = raw_ref[0].astype(F32) + bias_ref[...]
    soft = jnp.maximum(value, 0.0) + jnp.log1p(jnp.exp(-jnp.abs(value)))
    dt = jnp.where(live, soft, 0.0)
    la = -jnp.exp(alog_ref[...]) * dt
    tri = (
        lax.broadcasted_iota(jnp.int32, (rows, rows), 0)
        >= lax.broadcasted_iota(jnp.int32, (rows, rows), 1)
    )
    tri = jnp.where(tri, 1.0, 0.0).astype(BF16)
    high = la.astype(BF16)
    rest = la - high.astype(F32)
    mid = rest.astype(BF16)
    low = (rest - mid.astype(F32)).astype(BF16)
    cum = (
        jnp.dot(tri, low, preferred_element_type=F32)
        + jnp.dot(tri, mid, preferred_element_type=F32)
        + jnp.dot(tri, high, preferred_element_type=F32)
    )
    last = cum[rows - 1 :, :]
    cum_ref[...] = cum
    some = dt > 0.0
    log_dt = jnp.where(some, jnp.log(jnp.where(some, dt, 1.0)), -1e30)
    shift_ref[...] = (cum - log_dt).T
    ending_ref[...] = jnp.exp(last - cum) * dt
    decay_ref[...] = jnp.broadcast_to(jnp.exp(last), decay_ref.shape)


def step_tables(at, dt_raw, dt_bias, a_log):
    _, rows, heads = dt_raw.shape
    whole = lambda *shape: pl.BlockSpec(shape, lambda i, a: (0,) * len(shape))
    return pl.pallas_call(
        steps_body,
        out_shape=(
            jax.ShapeDtypeStruct((rows, heads), F32),
            jax.ShapeDtypeStruct((heads, rows), F32),
            jax.ShapeDtypeStruct((rows, heads), F32),
            jax.ShapeDtypeStruct((8, heads), F32),
        ),
        grid_spec=pltpu.PrefetchScalarGridSpec(
            num_scalar_prefetch=1,
            grid=(1,),
            in_specs=[whole(1, rows, heads), whole(1, heads), whole(1, heads)],
            out_specs=[whole(rows, heads), whole(heads, rows), whole(rows, heads), whole(8, heads)],
        ),
        cost_estimate=cost(rows * rows * heads * 6, rows * heads * 16, rows * heads * 4),
        name="step_tables",
    )(at, dt_raw, dt_bias[None], a_log[None])


def pair_columns(table, p, first):
    rows = table.shape[0]
    left = jnp.broadcast_to(table[:, 2 * p : 2 * p + 1], (rows, LANES))
    right = jnp.broadcast_to(table[:, 2 * p + 1 : 2 * p + 2], (rows, LANES))
    return left, right, jnp.where(first, left, right)


def group_heads(ref, group, per_group):
    heads = ref.shape[1]
    return pltpu.roll(ref[...], lax.rem(heads - group * per_group, heads), 1)


def conv_body(
    at_ref, x_ref, b_ref, c_ref, rx_ref, rb_ref, rc_ref, wx_ref, wb_ref, wc_ref,
    bx_ref, bb_ref, bc_ref, ending_ref, xa_ref, ba_ref, ca_ref, state_ref, rows_ref, cols_ref,
):
    group = at_ref[0] + pl.program_id(0)
    rows = x_ref.shape[1]
    pairs = x_ref.shape[2] // LANES
    taps = wx_ref.shape[0]
    first = lax.broadcasted_iota(jnp.int32, (rows, LANES), 1) < LANES // 2
    cols_ref[...] = group_heads(ending_ref, group, 2 * pairs)

    def conv(slot, src, rim, weight, bias, at):
        lanes = slice(at, at + LANES)
        rows_ref[slot, 0:8] = rim[:, lanes]
        rows_ref[slot, 8 : 8 + rows] = src[0, :, lanes].astype(F32)
        total = bias[:, lanes]
        for k in range(taps):
            begin = 9 - taps + k
            total = total + weight[k : k + 1, lanes] * rows_ref[slot, begin : begin + rows]
        return silu(total).astype(BF16)

    b_act = conv(0, b_ref, rb_ref, wb_ref, bb_ref, 0)
    ba_ref[...] = b_act
    ca_ref[...] = conv(1, c_ref, rc_ref, wc_ref, bc_ref, 0)
    for p in range(pairs):
        act = conv(p % 2, x_ref, rx_ref, wx_ref, bx_ref, p * LANES)
        xa_ref[:, p * LANES : (p + 1) * LANES] = act
        _, _, ending = pair_columns(cols_ref, p, first)
        scaled = (act.astype(F32) * ending).astype(BF16)
        state = lax.dot_general(
            scaled, ba_ref[...], (((0,), (0,)), ((), ())), preferred_element_type=F32
        )
        state_ref[p * LANES : (p + 1) * LANES, :] = state.astype(BF16)


def conv_half(at, tokens, rim, weight, bias, ending, inner, nstate):
    _, rows, channels = tokens.shape
    heads = ending.shape[1]
    width = inner // GROUPS
    half = GROUPS // 2
    b_at, c_at = inner // nstate, inner // nstate + GROUPS
    taps = weight.shape[0]

    def three(lead):
        pre = (0,) * len(lead)
        return [
            pl.BlockSpec(lead + (width,), lambda i, a: pre + (a[0] + i,)),
            pl.BlockSpec(lead + (nstate,), lambda i, a: pre + (b_at + a[0] + i,)),
            pl.BlockSpec(lead + (nstate,), lambda i, a: pre + (c_at + a[0] + i,)),
        ]

    return pl.pallas_call(
        conv_body,
        out_shape=(
            jax.ShapeDtypeStruct((rows, half * width), BF16),
            jax.ShapeDtypeStruct((rows, half * nstate), BF16),
            jax.ShapeDtypeStruct((rows, half * nstate), BF16),
            jax.ShapeDtypeStruct((half * width, nstate), BF16),
        ),
        grid_spec=pltpu.PrefetchScalarGridSpec(
            num_scalar_prefetch=1,
            grid=(half,),
            in_specs=three((1, rows))
            + three((8,))
            + three((taps,))
            + three((1,))
            + [pl.BlockSpec((rows, heads), lambda i, a: (0, 0))],
            out_specs=[
                pl.BlockSpec((rows, width), lambda i, a: (0, i)),
                pl.BlockSpec((rows, nstate), lambda i, a: (0, i)),
                pl.BlockSpec((rows, nstate), lambda i, a: (0, i)),
                pl.BlockSpec((width, nstate), lambda i, a: (i, 0)),
            ],
            scratch_shapes=[pltpu.VMEM((2, rows + 8, LANES), F32), pltpu.VMEM((rows, heads), F32)],
        ),
        cost_estimate=cost(rows * channels * 40, rows * channels * 2, rows * channels // 2),
        name="conv_half",
    )(at, tokens, tokens, tokens, rim, rim, rim, weight, weight, weight, bias, bias, bias, ending)


def outbound_body(owner_ref, own_w_ref, recv_w_ref, own_ref, recv_ref, out_ref):
    step = pl.program_id(0)
    chunk = own_ref.shape[0]
    for k in range(chunk):
        page = step * chunk + k
        total = own_w_ref[page] * own_ref[k].astype(F32) + recv_w_ref[page] * recv_ref[k].astype(F32)
        out_ref[owner_ref[page]] = total.astype(BF16)


def outbound_pages(owners, own_w, recv_w, own, recv, devices):
    pages, rows, width = own.shape
    chunk = min(16, pages)
    return pl.pallas_call(
        outbound_body,
        out_shape=jax.ShapeDtypeStruct((devices, rows, width), BF16),
        grid_spec=pltpu.PrefetchScalarGridSpec(
            num_scalar_prefetch=3,
            grid=(pages // chunk,),
            in_specs=[pl.BlockSpec((chunk, rows, width), lambda i, *s: (i, 0, 0))] * 2,
            out_specs=pl.BlockSpec((devices, rows, width), lambda i, *s: (0, 0, 0)),
        ),
        cost_estimate=cost(pages * rows * width * 3, pages * rows * width * 8),
        name="outbound_pages",
    )(owners, own_w, recv_w, own, recv)


def start_body(owner_ref, decay_ref, at_ref, keep_ref, in_ref, own_ref, recv_ref, start_ref, send_ref):
    step = pl.program_id(0)
    chunk = own_ref.shape[0]
    keep = keep_ref[0]

    @pl.when(at_ref[0] == 0)
    def _():
        for k in range(chunk):
            page = step * chunk + k
            held = in_ref[owner_ref[page]].astype(F32) * keep
            start_ref[k] = held.astype(BF16)
            send_ref[k] = (decay_ref[page] * held + own_ref[k].astype(F32)).astype(BF16)

    @pl.when(at_ref[0] != 0)
    def _():
        for k in range(chunk):
            page = step * chunk + k
            held = in_ref[owner_ref[page]].astype(F32) * keep
            send_ref[k] = held.astype(BF16)
            start_ref[k] = (decay_ref[page] * held + recv_ref[k].astype(F32)).astype(BF16)


def start_states(owners, decay, ctx, keep, incoming, own, recv):
    pages, rows, width = own.shape
    chunk = min(16, pages)
    block = pl.BlockSpec((chunk, rows, width), lambda i, *s: (i, 0, 0))
    return pl.pallas_call(
        start_body,
        out_shape=(jax.ShapeDtypeStruct(own.shape, BF16),) * 2,
        grid_spec=pltpu.PrefetchScalarGridSpec(
            num_scalar_prefetch=4,
            grid=(pages // chunk,),
            in_specs=[pl.BlockSpec(incoming.shape, lambda i, *s: (0, 0, 0)), block, block],
            out_specs=[block, block],
        ),
        cost_estimate=cost(pages * rows * width * 4, pages * rows * width * 12),
        name="start_states",
    )(owners, decay, ctx, keep, incoming, own, recv)


def mixer_body(
    at_ref, x_ref, b_ref, c_ref, cum_ref, shift_ref, start_ref, gate_ref, skip_ref, norm_ref, *rest
):
    out_ref, cols_ref, score_ref, gated_ref = rest[-4:]
    group = at_ref[0] + pl.program_id(0)
    rows, width = x_ref.shape
    pairs = width // LANES
    half = rows // 2
    first = lax.broadcasted_iota(jnp.int32, (rows, LANES), 1) < LANES // 2
    cols_ref[...] = group_heads(cum_ref, group, 2 * pairs)
    b_val, c_val = b_ref[...], c_ref[...]
    nt = (((1,), (1,)), ((), ()))
    scores = lax.dot_general(c_val, b_val, nt, preferred_element_type=F32)
    lower = (
        lax.broadcasted_iota(jnp.int32, (rows, rows), 0)
        >= lax.broadcasted_iota(jnp.int32, (rows, rows), 1)
    )
    score_ref[...] = jnp.where(lower, scores, 0.0)
    squares = jnp.zeros((rows, LANES), F32)
    for p in range(pairs):
        lanes = slice(p * LANES, (p + 1) * LANES)
        x_val = x_ref[:, lanes]
        left, right, both = pair_columns(cols_ref, p, first)
        ys = []
        for cum, h in ((left, 2 * p), (right, 2 * p + 1)):
            early = shift_ref[h : h + 1, :half]
            late = shift_ref[h : h + 1, half:]
            w00 = score_ref[:half, :half] * jnp.exp(jnp.minimum(cum[:half] - early, TOP))
            w10 = score_ref[half:, :half] * jnp.exp(cum[half:] - early)
            w11 = score_ref[half:, half:] * jnp.exp(jnp.minimum(cum[half:] - late, TOP))
            y0 = jnp.dot(w00.astype(BF16), x_val[:half], preferred_element_type=F32)
            w1 = jnp.concatenate([w10.astype(BF16), w11.astype(BF16)], axis=1)
            y1 = jnp.dot(w1, x_val, preferred_element_type=F32)
            ys.append(jnp.concatenate([y0, y1], axis=0))
        carried = lax.dot_general(c_val, start_ref[lanes, :], nt, preferred_element_type=F32)
        y = jnp.where(first, ys[0], ys[1]) + jnp.exp(both) * carried
        y = y + skip_ref[:, lanes] * x_val.astype(F32)
        gated = y * silu(gate_ref[0, :, lanes].astype(F32))
        gated_ref[p] = gated
        squares = squares + gated * gated
    mean = jnp.sum(squares, axis=1, keepdims=True) * (1.0 / width)
    live = at_ref[1] + lax.broadcasted_iota(jnp.int32, (rows, 1), 0) < at_ref[2]
    factor = jnp.where(live, lax.rsqrt(mean + 1e-05), 0.0)
    factor = jnp.broadcast_to(factor, (rows, LANES))
    for p in range(pairs):
        lanes = slice(p * LANES, (p + 1) * LANES)
        out_ref[0, :, lanes] = (gated_ref[p] * factor * norm_ref[:, lanes]).astype(BF16)


def mixer_half(at, x, b, c, cum, shift, start, gate, skip, norm, so_far):
    rows, half_width = x.shape
    heads = cum.shape[1]
    half = GROUPS // 2
    width = half_width // half
    nstate = start.shape[1]
    per_group = heads // GROUPS
    in_specs = [
        pl.BlockSpec((rows, width), lambda i, a: (0, i)),
        pl.BlockSpec((rows, nstate), lambda i, a: (0, i)),
        pl.BlockSpec((rows, nstate), lambda i, a: (0, i)),
        pl.BlockSpec((rows, heads), lambda i, a: (0, 0)),
        pl.BlockSpec((per_group, rows), lambda i, a: (a[0] + i, 0)),
        pl.BlockSpec((width, nstate), lambda i, a: (i, 0)),
        pl.BlockSpec((1, rows, width), lambda i, a: (0, 0, a[0] + i)),
        pl.BlockSpec((1, width), lambda i, a: (0, a[0] + i)),
        pl.BlockSpec((1, width), lambda i, a: (0, a[0] + i)),
    ]
    args = [at, x, b, c, cum, shift, start, gate, skip, norm]
    aliases = {}
    if so_far is not None:
        in_specs.append(pl.BlockSpec(memory_space=pl.ANY))
        aliases = {len(args): 0}
        args.append(so_far)
    return pl.pallas_call(
        mixer_body,
        out_shape=jax.ShapeDtypeStruct(gate.shape, BF16),
        grid_spec=pltpu.PrefetchScalarGridSpec(
            num_scalar_prefetch=1,
            grid=(half,),
            in_specs=in_specs,
            out_specs=pl.BlockSpec((1, rows, width), lambda i, a: (0, 0, a[0] + i)),
            scratch_shapes=[
                pltpu.VMEM((rows, heads), F32),
                pltpu.VMEM((rows, rows), F32),
                pltpu.VMEM((width // LANES, rows, LANES), F32),
            ],
        ),
        input_output_aliases=aliases,
        cost_estimate=cost(
            rows * half_width * (2 * rows + 2 * nstate), rows * half_width * 8, rows * rows * heads // 2
        ),
        name="mixer_half",
    )(*args)


def pool_body(dev_ref, decay_ref, pool_ref, in_ref, out_ref):
    step = pl.program_id(0)
    chunk = pool_ref.shape[0]
    for k in range(chunk):
        slot = step * chunk + k
        device = dev_ref[slot]

        @pl.when(device >= 0)
        def _():
            out_ref[k] = decay_ref[slot] * pool_ref[k] + in_ref[device].astype(F32)

        @pl.when(device < 0)
        def _():
            out_ref[k] = pool_ref[k]


def updated_pool(dev_of_slot, decay, pool, returned):
    slots, rows, width = pool.shape
    chunk = min(32, slots)
    block = pl.BlockSpec((chunk, rows, width), lambda i, *s: (i, 0, 0))
    return pl.pallas_call(
        pool_body,
        out_shape=jax.ShapeDtypeStruct(pool.shape, F32),
        grid_spec=pltpu.PrefetchScalarGridSpec(
            num_scalar_prefetch=2,
            grid=(slots // chunk,),
            in_specs=[block, pl.BlockSpec(returned.shape, lambda i, *s: (0, 0, 0))],
            out_specs=block,
        ),
        cost_estimate=cost(slots * rows * width * 2, slots * rows * width * 10),
        name="updated_pool",
    )(dev_of_slot, decay, pool, returned)


def local(
    conv_input,
    gate_input,
    dt_raw,
    conv_weight,
    conv_bias,
    dt_bias,
    a_log,
    d_skip,
    norm_weight,
    conv_cache,
    state_pool,
    page_owner,
    page_slot,
    prefix_len,
    new_count,
):
    ctx_count = lax.axis_size("ctx")
    devices = lax.axis_size("req") * ctx_count
    req_index = lax.axis_index("req")
    ctx_index = lax.axis_index("ctx")
    own_index = req_index * ctx_count + ctx_index
    rows = conv_input.shape[1]
    heads = dt_raw.shape[2]
    inner = gate_input.shape[2]
    width = inner // heads
    slots, page_rows, nstate = state_pool.shape
    pages = page_owner.shape[1] // ctx_count
    rim = conv_weight.shape[0] - 1
    half_groups = GROUPS // 2

    owner_table = page_owner.reshape(devices, pages)
    slot_table = page_slot.reshape(devices, pages)
    matches = owner_table == own_index
    slot_for = jnp.max(jnp.where(matches, slot_table, -1), axis=1)
    dev_ids = jnp.arange(devices, dtype=jnp.int32)
    slot_hits = slot_for[None, :] == jnp.arange(slots, dtype=jnp.int32)[:, None]
    dev_of_slot = jnp.max(jnp.where(slot_hits, dev_ids[None, :], -1), axis=1)
    outgoing = gather_pages(dev_of_slot, state_pool, devices)
    incoming = lax.all_to_all(outgoing, ("req", "ctx"), split_axis=0, concat_axis=0, tiled=True)

    prefix = prefix_len[req_index]
    count = new_count[req_index]
    owners = owner_table[own_index]
    base = (ctx_index * rows).astype(jnp.int32)
    at = jnp.stack([base, count])
    cum, shift, ending, decay_rows = step_tables(at, dt_raw, dt_bias, a_log)
    decay = decay_rows[0:1]
    other_decay = swapped(decay)

    previous = lax.ppermute(conv_input[0, rows - rim :], "ctx", [(0, 1)])
    keep_rows = jnp.arange(rim) >= rim - prefix
    cached = jnp.where(keep_rows[:, None], conv_cache[0], jnp.zeros_like(conv_cache[0]))
    rim_rows = jnp.where(ctx_index == 0, cached, previous).astype(F32)
    rim_rows = jnp.concatenate([jnp.zeros((8 - rim, rim_rows.shape[1]), F32), rim_rows], axis=0)

    own_at = jnp.stack([ctx_index * half_groups, base, count]).astype(jnp.int32)
    other_at = jnp.stack([(1 - ctx_index) * half_groups, base, count]).astype(jnp.int32)
    conv_args = (conv_input, rim_rows, conv_weight, conv_bias[None], ending, inner, nstate)
    x_other, b_other, c_other, state_other = conv_half(other_at, *conv_args)
    received = swapped(state_other)
    x_own, b_own, c_own, state_own = conv_half(own_at, *conv_args)

    ctx_first = ctx_index == 0
    mine = jnp.where(ctx_first, decay[0, : heads // 2], decay[0, heads // 2 :])
    theirs = jnp.where(ctx_first, other_decay[0, : heads // 2], other_decay[0, heads // 2 :])
    decay_early = jnp.where(ctx_first, mine, theirs)
    decay_late = jnp.where(ctx_first, theirs, mine)
    ones = jnp.ones_like(mine)
    own_w = jnp.where(ctx_first, decay_late, ones)
    recv_w = jnp.where(ctx_first, ones, decay_late)
    as_pages = lambda value: value.reshape(pages, page_rows, nstate)
    own_pages, recv_pages = as_pages(state_own), as_pages(received)
    outbound = outbound_pages(owners, own_w, recv_w, own_pages, recv_pages, devices)
    returned = lax.all_to_all(outbound, ("req", "ctx"), split_axis=0, concat_axis=0, tiled=True)
    all_decays = lax.all_gather((mine * theirs)[None], ("req", "ctx"), axis=0, tiled=True)

    keep = (prefix > 0).astype(F32)[None]
    start, send = start_states(
        owners, decay_early, ctx_index[None].astype(jnp.int32), keep, incoming, own_pages, recv_pages
    )
    start_other = swapped(send)
    skip = jnp.repeat(d_skip, width)[None]
    norm = norm_weight[None]
    as_rows = lambda value: value.reshape(pages * page_rows, nstate)
    mixed = mixer_half(
        own_at, x_own, b_own, c_own, cum, shift, as_rows(start), gate_input, skip, norm, None
    )
    mixed = mixer_half(
        other_at, x_other, b_other, c_other, cum, shift, as_rows(start_other), gate_input, skip, norm, mixed
    )

    targets = count - rim + jnp.arange(rim)
    positions = base + jnp.arange(rows)
    picks = (positions[None, :] == targets[:, None]).astype(BF16)
    tail_rows = jnp.dot(picks, conv_input[0], preferred_element_type=F32).astype(BF16)
    new_tail = tail_rows + swapped(tail_rows)

    request_kept = jnp.repeat((prefix_len > 0).astype(F32), ctx_count)
    page_decay = jnp.sum(jnp.where(matches, all_decays, 0.0), axis=1) * request_kept
    slot_decay = jnp.sum(jnp.where(slot_hits, page_decay[None, :], 0.0), axis=1)
    new_pool = updated_pool(dev_of_slot, slot_decay, state_pool, returned)
    return (mixed, new_tail[None], new_pool)


def solution(mesh):
    return jax.shard_map(
        local,
        mesh=mesh,
        in_specs=(
            P("req", "ctx", None),
            P("req", "ctx", None),
            P("req", "ctx", None),
            P(),
            P(),
            P(),
            P(),
            P(),
            P(),
            P("req", None, None),
            P(("req", "ctx"), None, None),
            P(),
            P(),
            P(),
            P(),
        ),
        out_specs=(P("req", "ctx", None), P("req", None, None), P(("req", "ctx"), None, None)),
        check_vma=False,
    )
```

time: 308 us -> 145 us (0.47)
  local copies, waits for them, and re-layouts: 80.8 us -> 9.28 us
  waiting for transfers between devices: 67.2 us -> 1.59 us
  Pallas kernels: 0 us -> 64.7 us
  other arithmetic: 63.5 us -> 7.74 us
  matrix products: 52.2 us -> 3.31 us
  blocking collectives: 8.26 us -> 33.4 us
  between operations: 16.1 us -> 2.6 us
  starting transfers between devices: 17.1 us -> 21.4 us
    pallas_call x0 -> x9, Pallas kernels: none -> 64.7 us  [the longest x2 20.4 us: mixer_half(): pl.pallas_call(mixer_body, out_shape=jax.ShapeDtypeStruct(gate.shape, BF1...]
    all_to_all x1, waiting for transfers between devices: 51.8 us -> 0.01 us  [local(): lax.all_to_all(outgoing, ('req', 'ctx'), split_axis=0, concat_axis=0, til...]
    dot_general x26 -> x1, matrix products: 52.2 us -> 3.31 us  [local(): jnp.dot(picks, conv_input[0], preferred_element_type=F32).astype(BF16)]
    convert_element_type x7 -> x1, other arithmetic: 33.4 us -> 0.01 us  [local(): request_kept = jnp.repeat((prefix_len > 0).astype(F32), ctx_count)]
    all_gather x1, blocking collectives: 2.89 us -> 33.4 us  [local(): lax.all_gather((mine * theirs)[None], ('req', 'ctx'), axis=0, tiled=True)]
    unnamed x44 -> x12, local copies, waits for them, and re-layouts: 31.9 us -> 1.99 us
    scatter x2 -> x0, local copies, waits for them, and re-layouts: 27.8 us -> none  [the longest x1 19 us: local(): new_pool = state_pool.at[target_slots].set(returned, mode='drop')]
    select_n x8 -> x3, other arithmetic: 18.1 us -> 2.08 us  [the longest x1 1.38 us: local(): recv_w = jnp.where(ctx_first, ones, decay_late)]
  transfers between devices with their start and end apart: 6 -> 7, of which waited for: 2 -> 1; matrix products, arithmetic and copies ran while one was open for 29% -> 12% of each run, Pallas kernels for 0% -> 40%
where the time goes in v1:
time: 145 us; the launch traced here: 144 us
  Pallas kernels  64.7 us (45%)
  blocking collectives  33.4 us (23%)
  starting transfers between devices  21.4 us (15%)
  local copies, waits for them, and re-layouts  9.28 us (6%)
  other arithmetic  7.74 us (5%)
  matrix products  3.31 us (2%)
  between operations  2.6 us (2%)
  waiting for transfers between devices  1.59 us (1%)
    all_gather x1, blocking collectives, local(): lax.all_gather((mine * theirs)[None], ('req', 'ctx'), axis=0, tiled=True)  33.4 us
    pallas_call x2, Pallas kernels, mixer_half(): pl.pallas_call(mixer_body, out_shape=jax.ShapeDtypeStruct(gate.shape, BF1...  20.4 us
    pallas_call x2, Pallas kernels, conv_half(): pl.pallas_call(conv_body, out_shape=(jax.ShapeDtypeStruct((rows, half * w...  19.3 us
    all_to_all x1, starting transfers between devices, local(): lax.all_to_all(outbound, ('req', 'ctx'), split_axis=0, concat_axis=0, til...  9.63 us
    pallas_call x1, Pallas kernels, updated_pool(): pl.pallas_call(pool_body, out_shape=jax.ShapeDtypeStruct(pool.shape, F32)...  7 us
    all_to_all x1, starting transfers between devices, local(): lax.all_to_all(outgoing, ('req', 'ctx'), split_axis=0, concat_axis=0, til...  6.73 us
    pallas_call x1, Pallas kernels, gather_pages(): pl.pallas_call(gather_body, out_shape=jax.ShapeDtypeStruct((devices, rows...  5.47 us
    pallas_call x1, Pallas kernels, start_states(): pl.pallas_call(start_body, out_shape=(jax.ShapeDtypeStruct(own.shape, BF1...  5.37 us
  transfers between devices with their start and end apart: 7, of which 1 were waited for; matrix products, arithmetic and copies ran while one was open for 12% of the time, Pallas kernels for 40%

profile of v1, /device:TPU:1, one launch (start us, length us, event | category | flops | bytes accessed | tf_op | source)
XLA Modules:
  0.0 144.0 jit_solution(9403591702152072316)
XLA Ops:
  0.6 1.0 slice_bitcast_fusion
  1.6 1.3 collective-permute-start
  2.9 1.2 dynamic_slice.9
  4.1 1.2 pad_add_fusion.at_ref
  5.4 2.6 %step_tables.1 = (f32[256,128]{1,0:T(8,128)}, f32[128,256]{1,0:T(8,128)}, f32[256,128]{1,0:T(8,128)}, f32[8,128]{1,0:T(8,128)}) custom-call(s32[2]{0:T(128)} %pad_add_fusion.at_ref, bf16[1,256,128]{2,1,0:T(8,128)(2,1)} %raw_ref.1, f32[1,128]{1,0:T(1,128)} %bitcast.51, f32[1,128]{1,0:T(1,128)} %bitcast.52), custom_call_target="tpu_custom_call" | custom-call | flops 50331648 | bytes 524288 | tf_op jit(solution)/shard_map/step_tables/pallas_call | solution.py:89
  8.0 0.7 slice.23
  8.7 1.4 collective-permute-start.1
  10.1 1.2 dynamic_slice.10
  11.9 1.3 add_add_fusion
  13.2 0.8 reshape.69
  14.1 0.8 reshape.70
  15.5 0.0 collective-permute-done.1
  15.6 1.4 fusion.7
  16.9 0.6 fusion.6
  17.5 33.4 %all-gather = f32[128,1,64]{2,1,0:T(1,128)S(1)} all-gather(f32[1,1,64]{2,1,0:T(1,128)S(1)} %get-tuple-element.37), channel_id=1, replica_groups=mesh['req'=64,'ctx'=2] {'req','ctx'}, dimensions={0}, use_global_device_ids=true | all-gather | bytes 33024 | tf_op jit(solution)/shard_map/all_gather | solution.py:470
  50.9 0.1 select_reduce_fusion.1
  51.0 0.1 select_reduce_fusion.3
  51.1 0.7 select_reduce_fusion.2.dev_ref
  51.8 0.0 copy-start.3
  51.8 5.5 %gather_pages.1 = bf16[128,64,128]{2,1,0:T(8,128)(2,1)} custom-call(s32[128]{0:T(128)} %select_reduce_fusion.2.dev_ref, f32[128,64,128]{2,1,0:T(8,128)} %pool_ref.3), custom_call_target="tpu_custom_call" | custom-call | flops 1048576 | bytes 6291456 | tf_op jit(solution)/shard_map/gather_pages/pallas_call | solution.py:41
  57.3 6.7 %all-to-all-start = ((bf16[128,64,128]{2,1,0:T(8,128)(2,1)}), bf16[128,64,128]{2,1,0:T(8,128)(2,1)S(1)}, u32[]{:S(2)}, u32[]{:S(2)}) async-start(bf16[128,64,128]{2,1,0:T(8,128)(2,1)} %gather_pages.1), calls=%async_computation | async-start | bytes 4194304 | tf_op jit(solution)/shard_map/all_to_all | solution.py:434
  64.0 0.0 collective-permute-done
  64.1 0.0 copy-done.3
  64.1 0.1 fusion.1
  64.2 0.8 pad_convert_fusion.rx_ref.rb_ref.rc_ref
  65.0 9.7 %conv_half.2 = (bf16[256,4096]{1,0:T(8,128)(2,1)}, bf16[256,512]{1,0:T(8,128)(2,1)}, bf16[256,512]{1,0:T(8,128)(2,1)}, bf16[4096,128]{1,0:T(8,128)(2,1)}) custom-call(s32[3]{0:T(128)} %get-tuple-element.39.at_ref, bf16[1,256,10240]{2,1,0:T(8,128)(2,1)} %c_ref.3, bf16[1,256,10240]{2,1,0:T(8,128)(2,1)} %c_ref.3, bf16[1,256,10240]{2,1,0:T(8,128)(2,1)} %c_ref.3, ...), custom_call_target="tpu_custom_call" | custom-call | flops 104857600 | bytes 5242880 | tf_op jit(solution)/shard_map/conv_half/pallas_call | solution.py:171
  74.6 0.0 copy-start.4
  74.6 0.0 copy-start.5
  74.7 1.1 collective-permute-start.2
  75.8 3.3 %convolution_convert_fusion = bf16[3,10240]{1,0:T(4,128)(2,1)S(1)} fusion(bf16[1,256,10240]{2,1,0:T(8,128)(2,1)} %c_ref.3, s32[256]{0:T(256)S(1)} %iota_add_fusion, s32[3]{0:T(128)S(1)} %iota_add_fusion.1), kind=kOutput, calls=%fused_computation | convolution fusion | flops 15760128 | bytes 5305356 | tf_op jit(solution)/shard_map/dot_general | solution.py:490
  79.1 0.1 collective-permute-start.4
  79.8 0.0 copy-done.4
  79.8 0.1 broadcast_in_dim.89
  79.8 0.7 broadcast_in_dim_reshape.3.skip_ref
  80.6 0.0 copy-done.5
  80.6 0.1 broadcast_in_dim.93
  80.6 0.1 reshape.75
  80.8 0.5 dynamic-slice_bitcast_fusion.owner_ref
  81.3 0.7 select_reduce_fusion.decay_ref
  82.0 9.7 %conv_half.3 = (bf16[256,4096]{1,0:T(8,128)(2,1)}, bf16[256,512]{1,0:T(8,128)(2,1)}, bf16[256,512]{1,0:T(8,128)(2,1)}, bf16[4096,128]{1,0:T(8,128)(2,1)}) custom-call(s32[3]{0:T(128)} %get-tuple-element.40.at_ref, bf16[1,256,10240]{2,1,0:T(8,128)(2,1)} %c_ref.3, bf16[1,256,10240]{2,1,0:T(8,128)(2,1)} %c_ref.3, bf16[1,256,10240]{2,1,0:T(8,128)(2,1)} %c_ref.3, ...), custom_call_target="tpu_custom_call" | custom-call | flops 104857600 | bytes 5242880 | tf_op jit(solution)/shard_map/conv_half/pallas_call | solution.py:171
  91.7 0.0 collective-permute-done.2
  91.7 0.0 copy-start.1
  91.7 1.0 copy-done.1
  92.7 4.5 %outbound_pages.1 = bf16[128,64,128]{2,1,0:T(8,128)(2,1)} custom-call(s32[64]{0:T(128)} %dynamic-slice_bitcast_fusion.owner_ref, f32[64]{0:T(128)} %get-tuple-element.36.own_w_ref, f32[64]{0:T(128)} %get-tuple-element.31.recv_w_ref, bf16[64,64,128]{2,1,0:T(8,128)(2,1)} %bitcast.38, bf16[64,64,128]{2,1,0:T(8,128)(2,1)} %bitcast.36), custom_call_target="tpu_custom_call" | custom-call | flops 1572864 | bytes 4194304 | tf_op jit(solution)/shard_map/outbound_pages/pallas_call | solution.py:212
  97.2 0.0 all-to-all-done.in_ref
  97.2 0.0 copy-start
  97.2 9.6 %all-to-all-start.1 = ((bf16[128,64,128]{2,1,0:T(8,128)(2,1)}), bf16[128,64,128]{2,1,0:T(8,128)(2,1)}, u32[]{:S(2)}, u32[]{:S(2)}) async-start(bf16[128,64,128]{2,1,0:T(8,128)(2,1)} %outbound_pages.1), calls=%async_computation.1 | async-start | bytes 4194304 | tf_op jit(solution)/shard_map/all_to_all | solution.py:469
  106.8 0.0 copy-done
  106.9 5.4 %start_states.1 = (bf16[64,64,128]{2,1,0:T(8,128)(2,1)}, bf16[64,64,128]{2,1,0:T(8,128)(2,1)}) custom-call(s32[64]{0:T(128)} %dynamic-slice_bitcast_fusion.owner_ref, f32[64]{0:T(128)} %get-tuple-element.38.decay_ref, s32[1]{0:T(128)} %bitcast.10.at_ref, f32[1]{0:T(128)S(6)} %convert_element_type.12.keep_ref, bf16[128,64,128]{2,1,0:T(8,128)(2,1)} %copy-done, ...), custom_call_target="tpu_custom_call" | custom-call | flops 2097152 | bytes 6291456 | tf_op jit(solution)/shard_map/start_states/pallas_call | solution.py:252
  112.2 1.2 collective-permute-start.3
  113.4 0.0 collective-permute-done.4
  113.4 0.7 add_bitcast_fusion
  114.1 10.2 %mixer_half.2.rest_0_ = bf16[1,256,8192]{2,1,0:T(8,128)(2,1)} custom-call(s32[3]{0:T(128)} %get-tuple-element.40.at_ref, bf16[256,4096]{1,0:T(8,128)(2,1)} %get-tuple-element.27.x_ref, bf16[256,512]{1,0:T(8,128)(2,1)} %get-tuple-element.28.b_ref, bf16[256,512]{1,0:T(8,128)(2,1)} %get-tuple-element.29.c_ref, f32[256,128]{1,0:T(8,128)} %get-tuple-element.21.cum_ref, ...), custom_call_target="tpu_custom_call" | custom-call | flops 805306368 | bytes 8388608 | tf_op jit(solution)/shard_map/mixer_half/pallas_call | solution.py:339
  124.3 0.0 collective-permute-done.3
  124.3 0.0 copy-start.2
  124.3 1.0 copy-done.2
  125.2 10.2 %mixer_half.3 = bf16[1,256,8192]{2,1,0:T(8,128)(2,1)} custom-call(s32[3]{0:T(128)} %get-tuple-element.39.at_ref, bf16[256,4096]{1,0:T(8,128)(2,1)} %get-tuple-element.18.x_ref, bf16[256,512]{1,0:T(8,128)(2,1)} %get-tuple-element.19.b_ref, bf16[256,512]{1,0:T(8,128)(2,1)} %get-tuple-element.20.c_ref, ...), custom_call_target="tpu_custom_call", output_to_operand_aliasing={{}: (10, {})} | custom-call | flops 805306368 | bytes 8388608 | tf_op jit(solution)/shard_map/mixer_half/pallas_call | solution.py:339
  135.4 1.6 %all-to-all-done.1.in_ref = bf16[128,64,128]{2,1,0:T(8,128)(2,1)} async-done(((bf16[128,64,128]{2,1,0:T(8,128)(2,1)}), bf16[128,64,128]{2,1,0:T(8,128)(2,1)}, u32[]{:S(2)}, u32[]{:S(2)}) %all-to-all-start.1) | async-done | bytes 2097184 | tf_op jit(solution)/shard_map/all_to_all | solution.py:469
  137.0 7.0 %updated_pool.1 = f32[128,64,128]{2,1,0:T(8,128)} custom-call(s32[128]{0:T(128)} %select_reduce_fusion.2.dev_ref, f32[128]{0:T(128)} %select_reduce_fusion.decay_ref, f32[128,64,128]{2,1,0:T(8,128)} %pool_ref.3, bf16[128,64,128]{2,1,0:T(8,128)(2,1)} %all-to-all-done.1.in_ref), custom_call_target="tpu_custom_call" | custom-call | flops 2097152 | bytes 10485760 | tf_op jit(solution)/shard_map/updated_pool/pallas_call | solution.py:381
  (5 shorter events, 0.0 us)
Async XLA Ops:
  1.6 62.5 %collective-permute-start = (bf16[3,10240]{1,0:T(4,128)(2,1)S(1)}, bf16[3,10240]{1,0:T(4,128)(2,1)S(1)}, u32[]{:S(2)}, u32[]{:S(2)}) collective-permute-start(bf16[3,10240]{1,0:T(4,128)(2,1)S(1)} %slice_bitcast_fusion), channel_id=1, source_target_pairs={{0,1},{2,3},{4,5},{6,7},{8,9},{10,11},{12,13},{14,15},{16,17},{18,... | collective-permute-start | bytes 184328 | tf_op jit(solution)/shard_map/ppermute | solution.py:445
  8.7 6.9 %collective-permute-start.1 = (f32[1,128]{1,0:T(1,128)S(1)}, f32[1,128]{1,0:T(1,128)S(1)}, u32[]{:S(2)}, u32[]{:S(2)}) collective-permute-start(f32[1,128]{1,0:T(1,128)S(1)} %slice.23), channel_id=1, source_target_pairs={{0,1},{1,0},{2,3},{3,2},{4,5},{5,4},{6,7},{7,6},{8,9},{9,8},{10,11... | collective-permute-start | bytes 1544 | tf_op jit(solution)/shard_map/ppermute | solution.py:16
  51.8 12.2 %copy-start.3 = (bf16[1,3,10240]{2,1,0:T(4,128)(2,1)S(1)}, bf16[1,3,10240]{2,1,0:T(4,128)(2,1)}, u32[]{:S(2)}) copy-start(bf16[1,3,10240]{2,1,0:T(4,128)(2,1)} %param.24) | copy-start | bytes 184324
  57.3 39.9 %all-to-all-start = ((bf16[128,64,128]{2,1,0:T(8,128)(2,1)}), bf16[128,64,128]{2,1,0:T(8,128)(2,1)S(1)}, u32[]{:S(2)}, u32[]{:S(2)}) async-start(bf16[128,64,128]{2,1,0:T(8,128)(2,1)} %gather_pages.1), calls=%async_computation | async-start | bytes 4194304 | tf_op jit(solution)/shard_map/all_to_all | solution.py:434
  74.6 5.1 %copy-start.4 = (f32[128]{0:T(128)S(1)}, f32[128]{0:T(128)}, u32[]{:S(2)}) copy-start(f32[128]{0:T(128)} %param.22) | copy-start | bytes 1540
  74.6 5.9 %copy-start.5 = (s32[64]{0:T(128)S(1)}, s32[64]{0:T(128)}, u32[]{:S(2)}) copy-start(s32[64]{0:T(128)} %param.28) | copy-start | bytes 772
  74.7 17.0 %collective-permute-start.2 = (bf16[4096,128]{1,0:T(8,128)(2,1)}, bf16[4096,128]{1,0:T(8,128)(2,1)S(1)}, u32[]{:S(2)}, u32[]{:S(2)}) collective-permute-start(bf16[4096,128]{1,0:T(8,128)(2,1)} %get-tuple-element.25), channel_id=1, source_target_pairs={{0,1},{1,0},{2,3},{3,2},{4,5},{5,4},{6,7},{7,6},{8,9},{9,8},{10,11... | collective-permute-start | bytes 3145736 | tf_op jit(solution)/shard_map/ppermute | solution.py:16
  79.1 34.3 %collective-permute-start.4 = (bf16[3,10240]{1,0:T(4,128)(2,1)S(1)}, bf16[3,10240]{1,0:T(4,128)(2,1)S(1)}, u32[]{:S(2)}, u32[]{:S(2)}) collective-permute-start(bf16[3,10240]{1,0:T(4,128)(2,1)S(1)} %convolution_convert_fusion), channel_id=1, source_target_pairs={{0,1},{1,0},{2,3},{3,2},{4,5},{5,4},{6,7},{7,6},{8,9},{9,8},{10,11... | collective-permute-start | bytes 184328 | tf_op jit(solution)/shard_map/ppermute | solution.py:16
  91.7 1.0 copy-start.1
  97.2 9.6 %copy-start = (bf16[128,64,128]{2,1,0:T(8,128)(2,1)}, bf16[128,64,128]{2,1,0:T(8,128)(2,1)S(1)}, u32[]{:S(2)}) copy-start(bf16[128,64,128]{2,1,0:T(8,128)(2,1)S(1)} %all-to-all-done.in_ref) | copy-start | bytes 6291460
  97.2 39.8 %all-to-all-start.1 = ((bf16[128,64,128]{2,1,0:T(8,128)(2,1)}), bf16[128,64,128]{2,1,0:T(8,128)(2,1)}, u32[]{:S(2)}, u32[]{:S(2)}) async-start(bf16[128,64,128]{2,1,0:T(8,128)(2,1)} %outbound_pages.1), calls=%async_computation.1 | async-start | bytes 4194304 | tf_op jit(solution)/shard_map/all_to_all | solution.py:469
  112.2 12.0 %collective-permute-start.3 = (bf16[64,64,128]{2,1,0:T(8,128)(2,1)}, bf16[64,64,128]{2,1,0:T(8,128)(2,1)S(1)}, u32[]{:S(2)}, u32[]{:S(2)}) collective-permute-start(bf16[64,64,128]{2,1,0:T(8,128)(2,1)} %get-tuple-element.26), channel_id=1, source_target_pairs={{0,1},{1,0},{2,3},{3,2},{4,5},{5,4},{6,7},{7,6},{8,9},{9,8},{10,11... | collective-permute-start | bytes 3145736 | tf_op jit(solution)/shard_map/ppermute | solution.py:16
  124.3 1.0 copy-start.2

commit v2 on v1

v2 whole, which is shorter than its diff:
```python
import functools

import jax
import jax.numpy as jnp
from jax import lax
from jax.experimental import pallas as pl
from jax.experimental.pallas import tpu as pltpu
from jax.sharding import PartitionSpec as P

GROUPS = 8
LANES = 128
TAIL = 8
TOP = 88.72
F32 = jnp.float32
BF16 = jnp.bfloat16


def swapped(value):
    return lax.ppermute(value, "ctx", [(0, 1), (1, 0)])


def silu(value):
    half = 0.5 * value
    return half + half * jnp.tanh(half)


def cost(flops, nbytes, trans=0):
    return pl.CostEstimate(flops=flops, bytes_accessed=nbytes, transcendentals=trans)


def gather_body(dev_ref, pool_ref, out_ref):
    step = pl.program_id(0)
    for k in range(pool_ref.shape[0]):
        device = dev_ref[step * pool_ref.shape[0] + k]

        @pl.when(device >= 0)
        def _():
            out_ref[device] = pool_ref[k].astype(BF16)


def gather_pages(dev_of_slot, pool, devices):
    slots, rows, width = pool.shape
    chunk = min(32, slots)
    return pl.pallas_call(
        gather_body,
        out_shape=jax.ShapeDtypeStruct((devices, rows, width), BF16),
        grid_spec=pltpu.PrefetchScalarGridSpec(
            num_scalar_prefetch=1,
            grid=(slots // chunk,),
            in_specs=[pl.BlockSpec((chunk, rows, width), lambda i, d: (i, 0, 0))],
            out_specs=pl.BlockSpec((devices, rows, width), lambda i, d: (0, 0, 0)),
        ),
        cost_estimate=cost(slots * rows * width, slots * rows * width * 6),
        name="gather_pages",
    )(dev_of_slot, pool)


def steps_body(id_ref, count_ref, raw_ref, bias_ref, alog_ref, cum_ref, shift_ref, ending_ref, decay_ref):
    rows, heads = cum_ref.shape
    pos = id_ref[1] * rows + lax.broadcasted_iota(jnp.int32, (rows, heads), 0)
    live = pos < count_ref[id_ref[0]]
    value = raw_ref[0].astype(F32) + bias_ref[...]
    soft = jnp.maximum(value, 0.0) + jnp.log1p(jnp.exp(-jnp.abs(value)))
    dt = jnp.where(live, soft, 0.0)
    la = -jnp.exp(alog_ref[...]) * dt
    tri = (
        lax.broadcasted_iota(jnp.int32, (rows, rows), 0)
        >= lax.broadcasted_iota(jnp.int32, (rows, rows), 1)
    )
    tri = jnp.where(tri, 1.0, 0.0).astype(BF16)
    high = la.astype(BF16)
    rest = la - high.astype(F32)
    mid = rest.astype(BF16)
    low = (rest - mid.astype(F32)).astype(BF16)
    cum = (
        jnp.dot(tri, low, preferred_element_type=F32)
        + jnp.dot(tri, mid, preferred_element_type=F32)
        + jnp.dot(tri, high, preferred_element_type=F32)
    )
    last = cum[rows - 1 :, :]
    cum_ref[...] = cum
    some = dt > 0.0
    log_dt = jnp.where(some, jnp.log(jnp.where(some, dt, 1.0)), -1e30)
    shift_ref[...] = (cum - log_dt).T
    ending_ref[...] = jnp.exp(last - cum) * dt
    decay_ref[...] = jnp.broadcast_to(jnp.exp(last), decay_ref.shape)


def step_tables(ids, counts, dt_raw, dt_bias, a_log):
    _, rows, heads = dt_raw.shape
    whole = lambda *shape: pl.BlockSpec(shape, lambda i, *s: (0,) * len(shape))
    return pl.pallas_call(
        steps_body,
        out_shape=(
            jax.ShapeDtypeStruct((rows, heads), F32),
            jax.ShapeDtypeStruct((heads, rows), F32),
            jax.ShapeDtypeStruct((rows, heads), F32),
            jax.ShapeDtypeStruct((8, heads), F32),
        ),
        grid_spec=pltpu.PrefetchScalarGridSpec(
            num_scalar_prefetch=2,
            grid=(1,),
            in_specs=[whole(1, rows, heads), whole(1, heads), whole(1, heads)],
            out_specs=[whole(rows, heads), whole(heads, rows), whole(rows, heads), whole(8, heads)],
        ),
        cost_estimate=cost(rows * rows * heads * 6, rows * heads * 16, rows * heads * 4),
        name="step_tables",
    )(ids, counts, dt_raw, dt_bias[None], a_log[None])


def pair_columns(table, p, first):
    rows = table.shape[0]
    left = jnp.broadcast_to(table[:, 2 * p : 2 * p + 1], (rows, LANES))
    right = jnp.broadcast_to(table[:, 2 * p + 1 : 2 * p + 2], (rows, LANES))
    return left, right, jnp.where(first, left, right)


def first_group(id_ref, own):
    ctx = id_ref[1]
    return (ctx if own else 1 - ctx) * (GROUPS // 2)


def group_heads(ref, group, per_group):
    heads = ref.shape[1]
    return pltpu.roll(ref[...], lax.rem(heads - group * per_group, heads), 1)


def conv_body(
    own, id_ref, prefix_ref, x_ref, b_ref, c_ref, kx_ref, kb_ref, kc_ref, px_ref, pb_ref, pc_ref,
    wx_ref, wb_ref, wc_ref, bx_ref, bb_ref, bc_ref, ending_ref, xa_ref, ba_ref, ca_ref, state_ref, rows_ref, cols_ref,
):
    group = first_group(id_ref, own) + pl.program_id(0)
    rows = x_ref.shape[1]
    pairs = x_ref.shape[2] // LANES
    taps = wx_ref.shape[0]
    first = lax.broadcasted_iota(jnp.int32, (rows, LANES), 1) < LANES // 2
    cols_ref[...] = group_heads(ending_ref, group, 2 * pairs)

    held = lax.broadcasted_iota(jnp.int32, (taps - 1, LANES), 0) >= taps - 1 - prefix_ref[id_ref[0]]
    lead = id_ref[1] == 0

    def conv(slot, src, kept, before, weight, bias, at):
        lanes = slice(at, at + LANES)
        cached = jnp.where(held, kept[0, :, lanes].astype(F32), 0.0)
        rim = jnp.where(lead, cached, before[:, lanes].astype(F32))
        rows_ref[slot, 9 - taps : 8] = rim
        rows_ref[slot, 8 : 8 + rows] = src[0, :, lanes].astype(F32)
        total = bias[:, lanes]
        for k in range(taps):
            begin = 9 - taps + k
            total = total + weight[k : k + 1, lanes] * rows_ref[slot, begin : begin + rows]
        return silu(total).astype(BF16)

    b_act = conv(0, b_ref, kb_ref, pb_ref, wb_ref, bb_ref, 0)
    ba_ref[...] = b_act
    ca_ref[...] = conv(1, c_ref, kc_ref, pc_ref, wc_ref, bc_ref, 0)
    for p in range(pairs):
        act = conv(p % 2, x_ref, kx_ref, px_ref, wx_ref, bx_ref, p * LANES)
        xa_ref[:, p * LANES : (p + 1) * LANES] = act
        _, _, ending = pair_columns(cols_ref, p, first)
        scaled = (act.astype(F32) * ending).astype(BF16)
        state = lax.dot_general(
            scaled, ba_ref[...], (((0,), (0,)), ((), ())), preferred_element_type=F32
        )
        state_ref[p * LANES : (p + 1) * LANES, :] = state.astype(BF16)


def conv_half(own, ids, prefix, tokens, cache, before, weight, bias, ending, inner, nstate):
    _, rows, channels = tokens.shape
    heads = ending.shape[1]
    width = inner // GROUPS
    half = GROUPS // 2
    b_at, c_at = inner // nstate, inner // nstate + GROUPS
    taps = weight.shape[0]

    def three(lead):
        pre = (0,) * len(lead)
        return [
            pl.BlockSpec(lead + (width,), lambda i, a, b: pre + (first_group(a, own) + i,)),
            pl.BlockSpec(lead + (nstate,), lambda i, a, b: pre + (b_at + first_group(a, own) + i,)),
            pl.BlockSpec(lead + (nstate,), lambda i, a, b: pre + (c_at + first_group(a, own) + i,)),
        ]

    return pl.pallas_call(
        functools.partial(conv_body, own),
        out_shape=(
            jax.ShapeDtypeStruct((rows, half * width), BF16),
            jax.ShapeDtypeStruct((rows, half * nstate), BF16),
            jax.ShapeDtypeStruct((rows, half * nstate), BF16),
            jax.ShapeDtypeStruct((half * width, nstate), BF16),
        ),
        grid_spec=pltpu.PrefetchScalarGridSpec(
            num_scalar_prefetch=2,
            grid=(half,),
            in_specs=three((1, rows))
            + three((1, taps - 1))
            + three((taps - 1,))
            + three((taps,))
            + three((1,))
            + [pl.BlockSpec((rows, heads), lambda i, a, b: (0, 0))],
            out_specs=[
                pl.BlockSpec((rows, width), lambda i, a, b: (0, i)),
                pl.BlockSpec((rows, nstate), lambda i, a, b: (0, i)),
                pl.BlockSpec((rows, nstate), lambda i, a, b: (0, i)),
                pl.BlockSpec((width, nstate), lambda i, a, b: (i, 0)),
            ],
            scratch_shapes=[pltpu.VMEM((2, rows + 8, LANES), F32), pltpu.VMEM((rows, heads), F32)],
        ),
        cost_estimate=cost(rows * channels * 40, rows * channels * 2, rows * channels // 2),
        name="conv_half",
    )(ids, prefix, tokens, tokens, tokens, cache, cache, cache, before, before, before, weight, weight, weight, bias, bias, bias, ending)


def outbound_body(
    owner_ref, early_ref, late_ref, id_ref, prefix_ref, own_ref, recv_ref, out_ref
):
    step = pl.program_id(0)
    chunk, rows, width = own_ref.shape
    lead = id_ref[1] == 0
    keep = jnp.where(prefix_ref[id_ref[0]] > 0, 1.0, 0.0)
    top = lax.broadcasted_iota(jnp.int32, (TAIL, width), 0) == 0
    for k in range(chunk):
        page = step * chunk + k
        late = late_ref[page]
        own_w = jnp.where(lead, late, 1.0)
        recv_w = jnp.where(lead, 1.0, late)
        total = own_w * own_ref[k].astype(F32) + recv_w * recv_ref[k].astype(F32)
        whole = jnp.full((TAIL, width), early_ref[page] * late * keep, F32)
        high = whole.astype(BF16).astype(F32)
        owner = owner_ref[page]
        out_ref[owner, :rows] = total.astype(BF16)
        out_ref[owner, rows:] = jnp.where(top, high, whole - high).astype(BF16)


def outbound_pages(owners, early, late, ids, prefix, own, recv, devices):
    pages, rows, width = own.shape
    chunk = min(16, pages)
    return pl.pallas_call(
        outbound_body,
        out_shape=jax.ShapeDtypeStruct((devices, rows + TAIL, width), BF16),
        grid_spec=pltpu.PrefetchScalarGridSpec(
            num_scalar_prefetch=5,
            grid=(pages // chunk,),
            in_specs=[pl.BlockSpec((chunk, rows, width), lambda i, *s: (i, 0, 0))] * 2,
            out_specs=pl.BlockSpec((devices, rows + TAIL, width), lambda i, *s: (0, 0, 0)),
        ),
        cost_estimate=cost(pages * rows * width * 3, pages * rows * width * 8),
        name="outbound_pages",
    )(owners, early, late, ids, prefix, own, recv)


def start_body(owner_ref, decay_ref, id_ref, prefix_ref, in_ref, own_ref, recv_ref, start_ref, send_ref):
    step = pl.program_id(0)
    chunk = own_ref.shape[0]
    keep = jnp.where(prefix_ref[id_ref[0]] > 0, 1.0, 0.0)

    @pl.when(id_ref[1] == 0)
    def _():
        for k in range(chunk):
            page = step * chunk + k
            held = in_ref[owner_ref[page]].astype(F32) * keep
            start_ref[k] = held.astype(BF16)
            send_ref[k] = (decay_ref[page] * held + own_ref[k].astype(F32)).astype(BF16)

    @pl.when(id_ref[1] != 0)
    def _():
        for k in range(chunk):
            page = step * chunk + k
            held = in_ref[owner_ref[page]].astype(F32) * keep
            send_ref[k] = held.astype(BF16)
            start_ref[k] = (decay_ref[page] * held + recv_ref[k].astype(F32)).astype(BF16)


def start_states(owners, decay, ids, prefix, incoming, own, recv):
    pages, rows, width = own.shape
    chunk = min(16, pages)
    block = pl.BlockSpec((chunk, rows, width), lambda i, *s: (i, 0, 0))
    return pl.pallas_call(
        start_body,
        out_shape=(jax.ShapeDtypeStruct(own.shape, BF16),) * 2,
        grid_spec=pltpu.PrefetchScalarGridSpec(
            num_scalar_prefetch=4,
            grid=(pages // chunk,),
            in_specs=[pl.BlockSpec(incoming.shape, lambda i, *s: (0, 0, 0)), block, block],
            out_specs=[block, block],
        ),
        cost_estimate=cost(pages * rows * width * 4, pages * rows * width * 12),
        name="start_states",
    )(owners, decay, ids, prefix, incoming, own, recv)


def mixer_body(
    own, id_ref, count_ref, skip_ref, x_ref, b_ref, c_ref, cum_ref, shift_ref, start_ref, gate_ref,
    norm_ref, *rest
):
    out_ref, cols_ref, score_ref, gated_ref = rest[-4:]
    group = first_group(id_ref, own) + pl.program_id(0)
    rows, width = x_ref.shape
    pairs = width // LANES
    half = rows // 2
    first = lax.broadcasted_iota(jnp.int32, (rows, LANES), 1) < LANES // 2
    cols_ref[...] = group_heads(cum_ref, group, 2 * pairs)
    b_val, c_val = b_ref[...], c_ref[...]
    nt = (((1,), (1,)), ((), ()))
    scores = lax.dot_general(c_val, b_val, nt, preferred_element_type=F32)
    lower = (
        lax.broadcasted_iota(jnp.int32, (rows, rows), 0)
        >= lax.broadcasted_iota(jnp.int32, (rows, rows), 1)
    )
    score_ref[...] = jnp.where(lower, scores, 0.0)
    squares = jnp.zeros((rows, LANES), F32)
    for p in range(pairs):
        lanes = slice(p * LANES, (p + 1) * LANES)
        x_val = x_ref[:, lanes]
        left, right, both = pair_columns(cols_ref, p, first)
        ys = []
        for cum, h in ((left, 2 * p), (right, 2 * p + 1)):
            early = shift_ref[h : h + 1, :half]
            late = shift_ref[h : h + 1, half:]
            w00 = score_ref[:half, :half] * jnp.exp(jnp.minimum(cum[:half] - early, TOP))
            w10 = score_ref[half:, :half] * jnp.exp(cum[half:] - early)
            w11 = score_ref[half:, half:] * jnp.exp(jnp.minimum(cum[half:] - late, TOP))
            y0 = jnp.dot(w00.astype(BF16), x_val[:half], preferred_element_type=F32)
            w1 = jnp.concatenate([w10.astype(BF16), w11.astype(BF16)], axis=1)
            y1 = jnp.dot(w1, x_val, preferred_element_type=F32)
            ys.append(jnp.concatenate([y0, y1], axis=0))
        carried = lax.dot_general(c_val, start_ref[lanes, :], nt, preferred_element_type=F32)
        y = jnp.where(first, ys[0], ys[1]) + jnp.exp(both) * carried
        head = group * 2 * pairs + 2 * p
        skip = jnp.where(first, skip_ref[head], skip_ref[head + 1])
        y = y + skip * x_val.astype(F32)
        gated = y * silu(gate_ref[0, :, lanes].astype(F32))
        gated_ref[p] = gated
        squares = squares + gated * gated
    mean = jnp.sum(squares, axis=1, keepdims=True) * (1.0 / width)
    pos = id_ref[1] * rows + lax.broadcasted_iota(jnp.int32, (rows, 1), 0)
    live = pos < count_ref[id_ref[0]]
    factor = jnp.where(live, lax.rsqrt(mean + 1e-05), 0.0)
    factor = jnp.broadcast_to(factor, (rows, LANES))
    for p in range(pairs):
        lanes = slice(p * LANES, (p + 1) * LANES)
        out_ref[0, :, lanes] = (gated_ref[p] * factor * norm_ref[:, lanes]).astype(BF16)


def mixer_half(own, ids, counts, skip, x, b, c, cum, shift, start, gate, norm, so_far):
    rows, half_width = x.shape
    heads = cum.shape[1]
    half = GROUPS // 2
    width = half_width // half
    nstate = start.shape[1]
    per_group = heads // GROUPS
    in_specs = [
        pl.BlockSpec((rows, width), lambda i, a, *s: (0, i)),
        pl.BlockSpec((rows, nstate), lambda i, a, *s: (0, i)),
        pl.BlockSpec((rows, nstate), lambda i, a, *s: (0, i)),
        pl.BlockSpec((rows, heads), lambda i, a, *s: (0, 0)),
        pl.BlockSpec((per_group, rows), lambda i, a, *s: (first_group(a, own) + i, 0)),
        pl.BlockSpec((width, nstate), lambda i, a, *s: (i, 0)),
        pl.BlockSpec((1, rows, width), lambda i, a, *s: (0, 0, first_group(a, own) + i)),
        pl.BlockSpec((1, width), lambda i, a, *s: (0, first_group(a, own) + i)),
    ]
    args = [ids, counts, skip, x, b, c, cum, shift, start, gate, norm]
    aliases = {}
    if so_far is not None:
        in_specs.append(pl.BlockSpec(memory_space=pl.ANY))
        aliases = {len(args): 0}
        args.append(so_far)
    return pl.pallas_call(
        functools.partial(mixer_body, own),
        out_shape=jax.ShapeDtypeStruct(gate.shape, BF16),
        grid_spec=pltpu.PrefetchScalarGridSpec(
            num_scalar_prefetch=3,
            grid=(half,),
            in_specs=in_specs,
            out_specs=pl.BlockSpec((1, rows, width), lambda i, a, *s: (0, 0, first_group(a, own) + i)),
            scratch_shapes=[
                pltpu.VMEM((rows, heads), F32),
                pltpu.VMEM((rows, rows), F32),
                pltpu.VMEM((width // LANES, rows, LANES), F32),
            ],
        ),
        input_output_aliases=aliases,
        cost_estimate=cost(
            rows * half_width * (2 * rows + 2 * nstate), rows * half_width * 8, rows * rows * heads // 2
        ),
        name="mixer_half",
    )(*args)


def pool_body(dev_ref, pool_ref, in_ref, out_ref):
    step = pl.program_id(0)
    chunk, rows, _ = pool_ref.shape
    for k in range(chunk):
        slot = step * chunk + k
        device = dev_ref[slot]

        @pl.when(device >= 0)
        def _():
            tail = in_ref[device, rows:].astype(F32)
            whole = tail[0:1] + tail[1:2]
            out_ref[k] = whole * pool_ref[k] + in_ref[device, :rows].astype(F32)

        @pl.when(device < 0)
        def _():
            out_ref[k] = pool_ref[k]


def updated_pool(dev_of_slot, pool, returned):
    slots, rows, width = pool.shape
    chunk = min(32, slots)
    block = pl.BlockSpec((chunk, rows, width), lambda i, *s: (i, 0, 0))
    return pl.pallas_call(
        pool_body,
        out_shape=jax.ShapeDtypeStruct(pool.shape, F32),
        grid_spec=pltpu.PrefetchScalarGridSpec(
            num_scalar_prefetch=1,
            grid=(slots // chunk,),
            in_specs=[block, pl.BlockSpec(returned.shape, lambda i, *s: (0, 0, 0))],
            out_specs=block,
        ),
        cost_estimate=cost(slots * rows * width * 2, slots * rows * width * 10),
        name="updated_pool",
    )(dev_of_slot, pool, returned)


def local(
    conv_input,
    gate_input,
    dt_raw,
    conv_weight,
    conv_bias,
    dt_bias,
    a_log,
    d_skip,
    norm_weight,
    conv_cache,
    state_pool,
    page_owner,
    page_slot,
    prefix_len,
    new_count,
):
    ctx_count = lax.axis_size("ctx")
    devices = lax.axis_size("req") * ctx_count
    req_index = lax.axis_index("req")
    ctx_index = lax.axis_index("ctx")
    own_index = req_index * ctx_count + ctx_index
    rows = conv_input.shape[1]
    heads = dt_raw.shape[2]
    inner = gate_input.shape[2]
    slots, page_rows, nstate = state_pool.shape
    pages = page_owner.shape[1] // ctx_count
    rim = conv_weight.shape[0] - 1
    requests = page_owner.shape[0]

    matches = page_owner == own_index
    early = jnp.arange(2 * pages)[None, :] < pages
    slot_0 = jnp.max(jnp.where(matches & early, page_slot, -1), axis=1)
    slot_1 = jnp.max(jnp.where(matches & ~early, page_slot, -1), axis=1)
    slot_ids = jnp.arange(slots, dtype=jnp.int32)[:, None]
    request_ids = jnp.arange(requests, dtype=jnp.int32)[None, :]
    hits_0, hits_1 = slot_0[None, :] == slot_ids, slot_1[None, :] == slot_ids
    dev_of_slot = jnp.max(
        jnp.maximum(
            jnp.where(hits_0, 2 * request_ids, -1), jnp.where(hits_1, 2 * request_ids + 1, -1)
        ),
        axis=1,
    )
    outgoing = gather_pages(dev_of_slot, state_pool, devices)
    outgoing, conv_input, dt_raw, new_count, prefix_len, page_owner = lax.optimization_barrier(
        (outgoing, conv_input, dt_raw, new_count, prefix_len, page_owner)
    )
    incoming = lax.all_to_all(outgoing, ("req", "ctx"), split_axis=0, concat_axis=0, tiled=True)

    ids = jnp.stack([req_index, ctx_index]).astype(jnp.int32)
    owners = lax.dynamic_slice(page_owner, (req_index, ctx_index * pages), (1, pages))[0]
    previous = lax.ppermute(conv_input[0, rows - rim :], "ctx", [(0, 1)])
    cum, shift, ending, decay_rows = step_tables(ids, new_count, dt_raw, dt_bias, a_log)
    decay = decay_rows[0:1]
    other_decay = swapped(decay)

    conv_args = (
        ids, prefix_len, conv_input, conv_cache, previous, conv_weight, conv_bias[None], ending, inner, nstate
    )
    x_other, b_other, c_other, state_other = conv_half(False, *conv_args)
    received = swapped(state_other)
    x_own, b_own, c_own, state_own = conv_half(True, *conv_args)

    ctx_first = ctx_index == 0
    mine = jnp.where(ctx_first, decay[0, : heads // 2], decay[0, heads // 2 :])
    theirs = jnp.where(ctx_first, other_decay[0, : heads // 2], other_decay[0, heads // 2 :])
    decay_early = jnp.where(ctx_first, mine, theirs)
    decay_late = jnp.where(ctx_first, theirs, mine)
    as_pages = lambda value: value.reshape(pages, page_rows, nstate)
    own_pages, recv_pages = as_pages(state_own), as_pages(received)
    outbound = outbound_pages(
        owners, decay_early, decay_late, ids, prefix_len, own_pages, recv_pages, devices
    )
    returned = lax.all_to_all(outbound, ("req", "ctx"), split_axis=0, concat_axis=0, tiled=True)

    start, send = start_states(
        owners, decay_early, ids, prefix_len, incoming, own_pages, recv_pages
    )
    start_other = swapped(send)
    as_rows = lambda value: value.reshape(pages * page_rows, nstate)
    mixed = mixer_half(
        True, ids, new_count, d_skip, x_own, b_own, c_own, cum, shift, as_rows(start), gate_input,
        norm_weight[None], None,
    )
    mixed = mixer_half(
        False, ids, new_count, d_skip, x_other, b_other, c_other, cum, shift, as_rows(start_other),
        gate_input, norm_weight[None], mixed,
    )

    targets = new_count[req_index] - rim + jnp.arange(rim)
    positions = ctx_index * rows + jnp.arange(rows)
    picks = (positions[None, :] == targets[:, None]).astype(BF16)
    tail_rows = jnp.dot(picks, conv_input[0], preferred_element_type=F32).astype(BF16)
    new_tail = tail_rows + swapped(tail_rows)

    new_pool = updated_pool(dev_of_slot, state_pool, returned)
    return (mixed, new_tail[None], new_pool)


def solution(mesh):
    return jax.shard_map(
        local,
        mesh=mesh,
        in_specs=(
            P("req", "ctx", None),
            P("req", "ctx", None),
            P("req", "ctx", None),
            P(),
            P(),
            P(),
            P(),
            P(),
            P(),
            P("req", None, None),
            P(("req", "ctx"), None, None),
            P(),
            P(),
            P(),
            P(),
        ),
        out_specs=(P("req", "ctx", None), P("req", None, None), P(("req", "ctx"), None, None)),
        check_vma=False,
    )
```

time: 145 us -> 114 us (0.79)
  blocking collectives: 33.4 us -> 0 us
  starting transfers between devices: 21.4 us -> 25.1 us
  waiting for transfers between devices: 1.59 us -> 4.2 us
  other arithmetic: 7.74 us -> 5.21 us
    all_gather x1 -> x0, blocking collectives: 33.4 us -> none  [local(): lax.all_gather((mine * theirs)[None], ('req', 'ctx'), axis=0, tiled=True)]
    all_to_all x1, starting transfers between devices: 6.73 us -> 11.5 us  [local(): lax.all_to_all(outgoing, ('req', 'ctx'), split_axis=0, concat_axis=0, til...]
    unnamed x12, local copies, waits for them, and re-layouts: 1.99 us -> 5.35 us
    all_to_all x1, waiting for transfers between devices: 1.58 us -> 4.19 us  [local(): lax.all_to_all(outbound, ('req', 'ctx'), split_axis=0, concat_axis=0, til...]
    another operation x2 -> x1, other arithmetic: 2.55 us -> 0.65 us  [local(): ids = jnp.stack([req_index, ctx_index]).astype(jnp.int32)]
    dynamic_slice x2 -> x1, local copies, waits for them, and re-layouts: 2.45 us -> 0.62 us  [local(): targets = new_count[req_index] - rim + jnp.arange(rim)]
    reshape x3 -> x0, local copies, waits for them, and re-layouts: 1.81 us -> none  [the longest x1 0.83 us: local(): slot_table = page_slot.reshape(devices, pages)]
  transfers between devices with their start and end apart: 7 -> 7, of which waited for: 1 -> 1; matrix products, arithmetic and copies ran while one was open for 12% -> 9% of each run, Pallas kernels for 40% -> 46%
where the time goes in v2:
time: 114 us; the launch traced here: 113 us
  Pallas kernels  65.1 us (57%)
  starting transfers between devices  25.1 us (22%)
  local copies, waits for them, and re-layouts  8.88 us (8%)
  other arithmetic  5.21 us (5%)
  waiting for transfers between devices  4.2 us (4%)
  matrix products  3.31 us (3%)
  between operations  1.39 us (1%)
    pallas_call x2, Pallas kernels, mixer_half(): pl.pallas_call(functools.partial(mixer_body, own), out_shape=jax.ShapeDty...  20 us
    pallas_call x2, Pallas kernels, conv_half(): pl.pallas_call(functools.partial(conv_body, own), out_shape=(jax.ShapeDty...  19.9 us
    all_to_all x1, starting transfers between devices, local(): lax.all_to_all(outgoing, ('req', 'ctx'), split_axis=0, concat_axis=0, til...  11.5 us
    all_to_all x1, starting transfers between devices, local(): lax.all_to_all(outbound, ('req', 'ctx'), split_axis=0, concat_axis=0, til...  9.52 us
    pallas_call x1, Pallas kernels, updated_pool(): pl.pallas_call(pool_body, out_shape=jax.ShapeDtypeStruct(pool.shape, F32)...  7.14 us
    pallas_call x1, Pallas kernels, start_states(): pl.pallas_call(start_body, out_shape=(jax.ShapeDtypeStruct(own.shape, BF1...  5.43 us
    unnamed x12, local copies, waits for them, and re-layouts  5.35 us
    pallas_call x1, Pallas kernels, gather_pages(): pl.pallas_call(gather_body, out_shape=jax.ShapeDtypeStruct((devices, rows...  5.33 us
  transfers between devices with their start and end apart: 7, of which 1 were waited for; matrix products, arithmetic and copies ran while one was open for 9% of the time, Pallas kernels for 46%

profile of v2, /device:TPU:1, one launch (start us, length us, event | category | flops | bytes accessed | tf_op | source)
XLA Modules:
  0.0 113.2 jit_solution(16238240293059653972)
XLA Ops:
  0.7 0.9 select_reduce_fusion.1
  1.6 0.7 maximum_reduce_fusion.dev_ref
  2.3 5.3 %gather_pages.1 = bf16[128,64,128]{2,1,0:T(8,128)(2,1)} custom-call(s32[128]{0:T(128)} %maximum_reduce_fusion.dev_ref, f32[128,64,128]{2,1,0:T(8,128)} %pool_ref.3), custom_call_target="tpu_custom_call" | custom-call | flops 1048576 | bytes 6291456 | tf_op jit(solution)/shard_map/gather_pages/pallas_call | solution.py:44
  7.6 11.5 %all-to-all-start = ((bf16[128,64,128]{2,1,0:T(8,128)(2,1)}), bf16[128,64,128]{2,1,0:T(8,128)(2,1)S(1)}, u32[]{:S(2)}, u32[]{:S(2)}) async-start(bf16[128,64,128]{2,1,0:T(8,128)(2,1)} %gather_pages.1), calls=%async_computation | async-start | bytes 4194304 | tf_op jit(solution)/shard_map/all_to_all | solution.py:473
  19.1 1.0 slice_bitcast_fusion
  20.1 1.3 %collective-permute-start = (bf16[3,10240]{1,0:T(4,128)(2,1)S(1)}, bf16[3,10240]{1,0:T(4,128)(2,1)S(1)}, u32[]{:S(2)}, u32[]{:S(2)}) collective-permute-start(bf16[3,10240]{1,0:T(4,128)(2,1)S(1)} %slice_bitcast_fusion), channel_id=1, source_target_pairs={{0,1},{2,3},{4,5},{6,7},{8,9},{10,11},{12,13},{14,15},{16,17},{18,... | collective-permute-start | bytes 184328 | tf_op jit(solution)/shard_map/ppermute | solution.py:477
  21.4 0.7 pad_add_fusion.id_ref
  22.0 2.7 %step_tables.1 = (f32[256,128]{1,0:T(8,128)}, f32[128,256]{1,0:T(8,128)}, f32[256,128]{1,0:T(8,128)}, f32[8,128]{1,0:T(8,128)}) custom-call(s32[2]{0:T(128)} %pad_add_fusion.id_ref, s32[64]{0:T(128)} %count_ref.2, bf16[1,256,128]{2,1,0:T(8,128)(2,1)} %raw_ref, f32[1,128]{1,0:T(1,128)} %bitcast.38, f32[1,128]{1,0:T(1,128)} %bitcast.39), custom_call_target="tpu_custom_call" | custom-call | flops 50331648 | bytes 524288 | tf_op jit(solution)/shard_map/step_tables/pallas_call | solution.py:92
  24.7 0.0 collective-permute-done.px_ref.pb_ref.pc_ref
  24.7 0.0 copy-start.3
  24.7 0.6 copy-done.3
  25.3 0.0 copy-start.5
  25.3 10.0 %conv_half.2 = (bf16[256,4096]{1,0:T(8,128)(2,1)}, bf16[256,512]{1,0:T(8,128)(2,1)}, bf16[256,512]{1,0:T(8,128)(2,1)}, bf16[4096,128]{1,0:T(8,128)(2,1)}) custom-call(s32[2]{0:T(128)} %pad_add_fusion.id_ref, s32[64]{0:T(128)} %prefix_ref.3, bf16[1,256,10240]{2,1,0:T(8,128)(2,1)} %c_ref.1, bf16[1,256,10240]{2,1,0:T(8,128)(2,1)} %c_ref.1, ...), custom_call_target="tpu_custom_call" | custom-call | flops 104857600 | bytes 5242880 | tf_op jit(solution)/shard_map/conv_half/pallas_call | solution.py:184
  35.3 1.2 %collective-permute-start.2 = (bf16[4096,128]{1,0:T(8,128)(2,1)}, bf16[4096,128]{1,0:T(8,128)(2,1)S(1)}, u32[]{:S(2)}, u32[]{:S(2)}) collective-permute-start(bf16[4096,128]{1,0:T(8,128)(2,1)} %get-tuple-element.37), channel_id=1, source_target_pairs={{0,1},{1,0},{2,3},{3,2},{4,5},{5,4},{6,7},{7,6},{8,9},{9,8},{10,11... | collective-permute-start | bytes 3145736 | tf_op jit(solution)/shard_map/ppermute | solution.py:19
  36.6 0.7 slice.23
  37.2 0.0 collective-permute-start.1
  37.2 0.0 copy-done.5
  37.3 0.6 dynamic_slice.7
  38.5 3.3 %convolution_convert_fusion = bf16[3,10240]{1,0:T(4,128)(2,1)S(1)} fusion(bf16[1,256,10240]{2,1,0:T(8,128)(2,1)} %c_ref.1, s32[256]{0:T(256)S(1)} %iota_add_fusion, s32[3]{0:T(128)S(1)} %iota_add_fusion.1), kind=kOutput, calls=%fused_computation | convolution fusion | flops 15760128 | bytes 5305356 | tf_op jit(solution)/shard_map/dot_general | solution.py:518
  41.8 0.5 collective-permute-start.4
  42.4 1.3 %dynamic-slice_bitcast_fusion.owner_ref = s32[64]{0:T(128)} fusion(s32[64,128]{1,0:T(8,128)} %param.26, s32[]{:T(128)S(6)} %select_n.51, s32[]{:T(128)S(6)} %select_n.52), kind=kLoop, calls=%fused_computation.22 | loop fusion | bytes 520 | tf_op jit(solution)/shard_map/squeeze | solution.py:476
  43.6 0.0 collective-permute-done.1
  43.6 1.4 %fusion.5 = (f32[64]{0:T(128)}, f32[64]{0:T(128)}) fusion(pred[]{:T(512)S(6)} %eq.56, f32[8,128]{1,0:T(8,128)} %get-tuple-element.34, f32[1,128]{1,0:T(1,128)S(1)} %collective-permute-done.1), kind=kLoop, calls=%fused_computation.19 | loop fusion | flops 256 | bytes 1537 | tf_op jit(solution)/shard_map/jit(_where)/select_n | solution.py:493
  45.0 9.9 %conv_half.3 = (bf16[256,4096]{1,0:T(8,128)(2,1)}, bf16[256,512]{1,0:T(8,128)(2,1)}, bf16[256,512]{1,0:T(8,128)(2,1)}, bf16[4096,128]{1,0:T(8,128)(2,1)}) custom-call(s32[2]{0:T(128)} %pad_add_fusion.id_ref, s32[64]{0:T(128)} %prefix_ref.3, bf16[1,256,10240]{2,1,0:T(8,128)(2,1)} %c_ref.1, bf16[1,256,10240]{2,1,0:T(8,128)(2,1)} %c_ref.1, ...), custom_call_target="tpu_custom_call" | custom-call | flops 104857600 | bytes 5242880 | tf_op jit(solution)/shard_map/conv_half/pallas_call | solution.py:184
  54.9 0.0 collective-permute-done.2
  54.9 0.0 copy-start.2
  54.9 1.0 copy-done.2
  55.9 4.6 %outbound_pages.1 = bf16[128,72,128]{2,1,0:T(8,128)(2,1)} custom-call(s32[64]{0:T(128)} %dynamic-slice_bitcast_fusion.owner_ref, f32[64]{0:T(128)} %get-tuple-element.46.decay_ref.early_ref, f32[64]{0:T(128)} %get-tuple-element.45.late_ref, s32[2]{0:T(128)} %pad_add_fusion.id_ref, s32[64]{0:T(128)} %prefix_ref.3, bf16[64,64,128]{2,1,0:T(8,128)(2,1)} %bitcast.26, ...), custom_call_target="tpu_custom_call" | custom-call | flops 1572864 | bytes 4194304 | tf_op jit(solution)/shard_map/outbound_pages/pallas_call | solution.py:238
  60.5 0.0 all-to-all-done.in_ref
  60.5 0.0 copy-start.1
  60.5 1.3 %copy-done.1 = bf16[128,64,128]{2,1,0:T(8,128)(2,1)} copy-done((bf16[128,64,128]{2,1,0:T(8,128)(2,1)}, bf16[128,64,128]{2,1,0:T(8,128)(2,1)S(1)}, u32[]{:S(2)}) %copy-start.1) | copy-done | bytes 2097176
  61.9 9.5 %all-to-all-start.1 = ((bf16[128,72,128]{2,1,0:T(8,128)(2,1)}), bf16[128,72,128]{2,1,0:T(8,128)(2,1)S(1)}, u32[]{:S(2)}, u32[]{:S(2)}) async-start(bf16[128,72,128]{2,1,0:T(8,128)(2,1)} %outbound_pages.1), calls=%async_computation.1 | async-start | bytes 4718592 | tf_op jit(solution)/shard_map/all_to_all | solution.py:499
  71.4 5.4 %start_states.1 = (bf16[64,64,128]{2,1,0:T(8,128)(2,1)}, bf16[64,64,128]{2,1,0:T(8,128)(2,1)}) custom-call(s32[64]{0:T(128)} %dynamic-slice_bitcast_fusion.owner_ref, f32[64]{0:T(128)} %get-tuple-element.46.decay_ref.early_ref, s32[2]{0:T(128)} %pad_add_fusion.id_ref, s32[64]{0:T(128)} %prefix_ref.3, bf16[128,64,128]{2,1,0:T(8,128)(2,1)} %copy-done.1, ...), custom_call_target="tpu_custom_call" | custom-call | flops 2097152 | bytes 6291456 | tf_op jit(solution)/shard_map/start_states/pallas_call | solution.py:278
  76.8 1.1 collective-permute-start.3
  77.9 0.0 collective-permute-done.4
  77.9 1.6 %add_bitcast_fusion = bf16[1,3,10240]{2,1,0:T(4,128)(2,1)} fusion(bf16[3,10240]{1,0:T(4,128)(2,1)S(1)} %convolution_convert_fusion, bf16[3,10240]{1,0:T(4,128)(2,1)} %collective-permute-done.4), kind=kLoop, calls=%fused_computation.2 | loop fusion | flops 30720 | bytes 184320 | tf_op jit(solution)/shard_map/broadcast_in_dim | solution.py:522
  79.5 9.9 %mixer_half.2.rest_0_ = bf16[1,256,8192]{2,1,0:T(8,128)(2,1)} custom-call(s32[2]{0:T(128)} %pad_add_fusion.id_ref, s32[64]{0:T(128)} %count_ref.2, f32[128]{0:T(128)} %skip_ref.3, bf16[256,4096]{1,0:T(8,128)(2,1)} %get-tuple-element.39.x_ref, bf16[256,512]{1,0:T(8,128)(2,1)} %get-tuple-element.40.b_ref, bf16[256,512]{1,0:T(8,128)(2,1)} %get-tuple-element.41.c_ref, ...), custom_call_target="tpu_custom_call" | custom-call | flops 805306368 | bytes 8388608 | tf_op jit(solution)/shard_map/mixer_half/pallas_call | solution.py:368
  89.4 0.0 collective-permute-done.3
  89.4 0.0 copy-start.4
  89.4 1.0 copy-done.4
  90.4 10.1 %mixer_half.3 = bf16[1,256,8192]{2,1,0:T(8,128)(2,1)} custom-call(s32[2]{0:T(128)} %pad_add_fusion.id_ref, s32[64]{0:T(128)} %count_ref.2, f32[128]{0:T(128)} %skip_ref.3, bf16[256,4096]{1,0:T(8,128)(2,1)} %get-tuple-element.28.x_ref, bf16[256,512]{1,0:T(8,128)(2,1)} %get-tuple-element.29.b_ref, ...), custom_call_target="tpu_custom_call", output_to_operand_aliasing={{}: (11, {})} | custom-call | flops 805306368 | bytes 8388608 | tf_op jit(solution)/shard_map/mixer_half/pallas_call | solution.py:368
  100.5 4.2 %all-to-all-done.1.in_ref = bf16[128,72,128]{2,1,0:T(8,128)(2,1)S(1)} async-done(((bf16[128,72,128]{2,1,0:T(8,128)(2,1)}), bf16[128,72,128]{2,1,0:T(8,128)(2,1)S(1)}, u32[]{:S(2)}, u32[]{:S(2)}) %all-to-all-start.1) | async-done | bytes 2359328 | tf_op jit(solution)/shard_map/all_to_all | solution.py:499
  104.6 0.0 copy-start
  104.6 1.4 %copy-done = bf16[128,72,128]{2,1,0:T(8,128)(2,1)} copy-done((bf16[128,72,128]{2,1,0:T(8,128)(2,1)}, bf16[128,72,128]{2,1,0:T(8,128)(2,1)S(1)}, u32[]{:S(2)}) %copy-start) | copy-done | bytes 2359320
  106.1 7.1 %updated_pool.1 = f32[128,64,128]{2,1,0:T(8,128)} custom-call(s32[128]{0:T(128)} %maximum_reduce_fusion.dev_ref, f32[128,64,128]{2,1,0:T(8,128)} %pool_ref.3, bf16[128,72,128]{2,1,0:T(8,128)(2,1)} %copy-done), custom_call_target="tpu_custom_call" | custom-call | flops 2097152 | bytes 10485760 | tf_op jit(solution)/shard_map/updated_pool/pallas_call | solution.py:412
  (4 shorter events, 0.0 us)
Async XLA Ops:
  7.6 53.0 %all-to-all-start = ((bf16[128,64,128]{2,1,0:T(8,128)(2,1)}), bf16[128,64,128]{2,1,0:T(8,128)(2,1)S(1)}, u32[]{:S(2)}, u32[]{:S(2)}) async-start(bf16[128,64,128]{2,1,0:T(8,128)(2,1)} %gather_pages.1), calls=%async_computation | async-start | bytes 4194304 | tf_op jit(solution)/shard_map/all_to_all | solution.py:473
  20.1 4.6 %collective-permute-start = (bf16[3,10240]{1,0:T(4,128)(2,1)S(1)}, bf16[3,10240]{1,0:T(4,128)(2,1)S(1)}, u32[]{:S(2)}, u32[]{:S(2)}) collective-permute-start(bf16[3,10240]{1,0:T(4,128)(2,1)S(1)} %slice_bitcast_fusion), channel_id=1, source_target_pairs={{0,1},{2,3},{4,5},{6,7},{8,9},{10,11},{12,13},{14,15},{16,17},{18,... | collective-permute-start | bytes 184328 | tf_op jit(solution)/shard_map/ppermute | solution.py:477
  24.7 0.6 copy-start.3
  25.3 11.9 %copy-start.5 = (s32[64]{0:T(128)S(1)}, s32[64]{0:T(128)}, u32[]{:S(2)}) copy-start(s32[64]{0:T(128)} %count_ref.2) | copy-start | bytes 772
  35.3 19.5 %collective-permute-start.2 = (bf16[4096,128]{1,0:T(8,128)(2,1)}, bf16[4096,128]{1,0:T(8,128)(2,1)S(1)}, u32[]{:S(2)}, u32[]{:S(2)}) collective-permute-start(bf16[4096,128]{1,0:T(8,128)(2,1)} %get-tuple-element.37), channel_id=1, source_target_pairs={{0,1},{1,0},{2,3},{3,2},{4,5},{5,4},{6,7},{7,6},{8,9},{9,8},{10,11... | collective-permute-start | bytes 3145736 | tf_op jit(solution)/shard_map/ppermute | solution.py:19
  37.2 6.4 %collective-permute-start.1 = (f32[1,128]{1,0:T(1,128)S(1)}, f32[1,128]{1,0:T(1,128)S(1)}, u32[]{:S(2)}, u32[]{:S(2)}) collective-permute-start(f32[1,128]{1,0:T(1,128)S(1)} %slice.23), channel_id=1, source_target_pairs={{0,1},{1,0},{2,3},{3,2},{4,5},{5,4},{6,7},{7,6},{8,9},{9,8},{10,11... | collective-permute-start | bytes 1544 | tf_op jit(solution)/shard_map/ppermute | solution.py:19
  41.8 36.1 %collective-permute-start.4 = (bf16[3,10240]{1,0:T(4,128)(2,1)S(1)}, bf16[3,10240]{1,0:T(4,128)(2,1)}, u32[]{:S(2)}, u32[]{:S(2)}) collective-permute-start(bf16[3,10240]{1,0:T(4,128)(2,1)S(1)} %convolution_convert_fusion), channel_id=1, source_target_pairs={{0,1},{1,0},{2,3},{3,2},{4,5},{5,4},{6,7},{7,6},{8,9},{9,8},{10,11... | collective-permute-start | bytes 184328 | tf_op jit(solution)/shard_map/ppermute | solution.py:19
  54.9 1.0 copy-start.2
  60.5 1.3 %copy-start.1 = (bf16[128,64,128]{2,1,0:T(8,128)(2,1)}, bf16[128,64,128]{2,1,0:T(8,128)(2,1)S(1)}, u32[]{:S(2)}) copy-start(bf16[128,64,128]{2,1,0:T(8,128)(2,1)S(1)} %all-to-all-done.in_ref) | copy-start | bytes 6291460
  61.9 42.8 %all-to-all-start.1 = ((bf16[128,72,128]{2,1,0:T(8,128)(2,1)}), bf16[128,72,128]{2,1,0:T(8,128)(2,1)S(1)}, u32[]{:S(2)}, u32[]{:S(2)}) async-start(bf16[128,72,128]{2,1,0:T(8,128)(2,1)} %outbound_pages.1), calls=%async_computation.1 | async-start | bytes 4718592 | tf_op jit(solution)/shard_map/all_to_all | solution.py:499
  76.8 12.6 %collective-permute-start.3 = (bf16[64,64,128]{2,1,0:T(8,128)(2,1)}, bf16[64,64,128]{2,1,0:T(8,128)(2,1)S(1)}, u32[]{:S(2)}, u32[]{:S(2)}) collective-permute-start(bf16[64,64,128]{2,1,0:T(8,128)(2,1)} %get-tuple-element.38), channel_id=1, source_target_pairs={{0,1},{1,0},{2,3},{3,2},{4,5},{5,4},{6,7},{7,6},{8,9},{9,8},{10,11... | collective-permute-start | bytes 3145736 | tf_op jit(solution)/shard_map/ppermute | solution.py:19
  89.4 1.0 copy-start.4
  104.6 1.4 %copy-start = (bf16[128,72,128]{2,1,0:T(8,128)(2,1)}, bf16[128,72,128]{2,1,0:T(8,128)(2,1)S(1)}, u32[]{:S(2)}) copy-start(bf16[128,72,128]{2,1,0:T(8,128)(2,1)S(1)} %all-to-all-done.1.in_ref) | copy-start | bytes 7077892

commit v3 on v2

v3 whole, which is shorter than its diff:
```python
import functools

import jax
import jax.numpy as jnp
from jax import lax
from jax.experimental import pallas as pl
from jax.experimental.pallas import tpu as pltpu
from jax.sharding import PartitionSpec as P

GROUPS = 8
LANES = 128
TAIL = 8
PARTS = 4
GRANT = 64 << 20
TOP = 88.72
F32 = jnp.float32
IN_HBM = pl.BlockSpec(memory_space=pltpu.HBM)
BF16 = jnp.bfloat16


def swapped(value):
    return lax.ppermute(value, "ctx", [(0, 1), (1, 0)])


def silu(value):
    half = 0.5 * value
    return half + half * jnp.tanh(half)


def cost(flops, nbytes, trans=0):
    return pl.CostEstimate(flops=flops, bytes_accessed=nbytes, transcendentals=trans)


def part_copies(source, target, sems, parts):
    size = source.shape[0] // parts
    return [
        pltpu.make_async_copy(
            source.at[pl.ds(c * size, size)], target.at[pl.ds(c * size, size)], sems.at[c]
        )
        for c in range(parts)
    ]


def gather_body(early_ref, late_ref, pool_ref, out_ref, page_ref, round_ref, in_sem, out_sem):
    devices = round_ref.shape[0]
    ins = part_copies(pool_ref, page_ref, in_sem, PARTS)
    outs = part_copies(round_ref, out_ref, out_sem, PARTS)
    for copy in ins:
        copy.start()
    for copy in ins:
        copy.wait()
    for c in range(PARTS):
        for k in range(devices // PARTS):
            device = c * (devices // PARTS) + k
            slot = (early_ref, late_ref)[device % 2][device // 2]
            round_ref[device] = page_ref[jnp.maximum(slot, 0)].astype(BF16)
        outs[c].start()
    for copy in outs:
        copy.wait()


def gather_pages(slot_early, slot_late, pool, devices):
    slots, rows, width = pool.shape
    return pl.pallas_call(
        gather_body,
        out_shape=jax.ShapeDtypeStruct((devices, rows, width), BF16),
        grid_spec=pltpu.PrefetchScalarGridSpec(
            num_scalar_prefetch=2,
            grid=(1,),
            in_specs=[IN_HBM],
            out_specs=IN_HBM,
            scratch_shapes=[
                pltpu.VMEM((slots, rows, width), F32),
                pltpu.VMEM((devices, rows, width), BF16),
                pltpu.SemaphoreType.DMA((PARTS,)),
                pltpu.SemaphoreType.DMA((PARTS,)),
            ],
        ),
        compiler_params=pltpu.CompilerParams(vmem_limit_bytes=GRANT),
        cost_estimate=cost(slots * rows * width, slots * rows * width * 6),
        name="gather_pages",
    )(slot_early, slot_late, pool)


def steps_body(id_ref, count_ref, raw_ref, bias_ref, alog_ref, cum_ref, shift_ref, ending_ref, decay_ref):
    rows, heads = cum_ref.shape
    pos = id_ref[1] * rows + lax.broadcasted_iota(jnp.int32, (rows, heads), 0)
    live = pos < count_ref[id_ref[0]]
    value = raw_ref[0].astype(F32) + bias_ref[...]
    soft = jnp.maximum(value, 0.0) + jnp.log1p(jnp.exp(-jnp.abs(value)))
    dt = jnp.where(live, soft, 0.0)
    la = -jnp.exp(alog_ref[...]) * dt
    tri = (
        lax.broadcasted_iota(jnp.int32, (rows, rows), 0)
        >= lax.broadcasted_iota(jnp.int32, (rows, rows), 1)
    )
    tri = jnp.where(tri, 1.0, 0.0).astype(BF16)
    high = la.astype(BF16)
    rest = la - high.astype(F32)
    mid = rest.astype(BF16)
    low = (rest - mid.astype(F32)).astype(BF16)
    cum = (
        jnp.dot(tri, low, preferred_element_type=F32)
        + jnp.dot(tri, mid, preferred_element_type=F32)
        + jnp.dot(tri, high, preferred_element_type=F32)
    )
    last = cum[rows - 1 :, :]
    cum_ref[...] = cum
    some = dt > 0.0
    log_dt = jnp.where(some, jnp.log(jnp.where(some, dt, 1.0)), -1e30)
    shift_ref[...] = (cum - log_dt).T
    ending_ref[...] = jnp.exp(last - cum) * dt
    decay_ref[...] = jnp.broadcast_to(jnp.exp(last), decay_ref.shape)


def step_tables(ids, counts, dt_raw, dt_bias, a_log):
    _, rows, heads = dt_raw.shape
    whole = lambda *shape: pl.BlockSpec(shape, lambda i, *s: (0,) * len(shape))
    return pl.pallas_call(
        steps_body,
        out_shape=(
            jax.ShapeDtypeStruct((rows, heads), F32),
            jax.ShapeDtypeStruct((heads, rows), F32),
            jax.ShapeDtypeStruct((rows, heads), F32),
            jax.ShapeDtypeStruct((8, heads), F32),
        ),
        grid_spec=pltpu.PrefetchScalarGridSpec(
            num_scalar_prefetch=2,
            grid=(1,),
            in_specs=[whole(1, rows, heads), whole(1, heads), whole(1, heads)],
            out_specs=[whole(rows, heads), whole(heads, rows), whole(rows, heads), whole(8, heads)],
        ),
        compiler_params=pltpu.CompilerParams(vmem_limit_bytes=GRANT),
        cost_estimate=cost(rows * rows * heads * 6, rows * heads * 16, rows * heads * 4),
        name="step_tables",
    )(ids, counts, dt_raw, dt_bias[None], a_log[None])


def pair_columns(table, p, first):
    rows = table.shape[0]
    left = jnp.broadcast_to(table[:, 2 * p : 2 * p + 1], (rows, LANES))
    right = jnp.broadcast_to(table[:, 2 * p + 1 : 2 * p + 2], (rows, LANES))
    return left, right, jnp.where(first, left, right)


def first_group(id_ref, own):
    ctx = id_ref[1]
    return (ctx if own else 1 - ctx) * (GROUPS // 2)


def group_heads(ref, group, per_group):
    heads = ref.shape[1]
    return pltpu.roll(ref[...], lax.rem(heads - group * per_group, heads), 1)


def conv_body(
    own, channels, id_ref, prefix_ref, count_ref, x_ref, b_ref, c_ref, cache_ref, before_ref, weight_ref, bias_ref,
    ending_ref, *rest
):
    xa_ref, bc_ref, state_ref, tail_ref, rows_ref, cols_ref = rest[-6:]
    group = first_group(id_ref, own) + pl.program_id(0)
    rows = x_ref.shape[1]
    width = x_ref.shape[2]
    nstate = b_ref.shape[2]
    pairs = width // LANES
    taps = weight_ref.shape[0]
    b_at, c_at = channels
    first = lax.broadcasted_iota(jnp.int32, (rows, LANES), 1) < LANES // 2
    cols_ref[...] = group_heads(ending_ref, group, 2 * pairs)
    held = lax.broadcasted_iota(jnp.int32, (taps - 1, LANES), 0) >= taps - 1 - prefix_ref[id_ref[0]]
    lead = id_ref[1] == 0
    last = count_ref[id_ref[0]] - id_ref[1] * rows
    newest = 9 - taps + jnp.clip(last, 0, rows)
    if own:

        @pl.when(pl.program_id(0) == 0)
        def _():
            tail_ref[...] = rest[0][...]

    def conv(slot, src, at, begin):
        lanes = pl.ds(pl.multiple_of(begin, LANES), LANES)
        cached = jnp.where(held, cache_ref[0, :, lanes].astype(F32), 0.0)
        rim = jnp.where(lead, cached, before_ref[:, lanes].astype(F32))
        rows_ref[slot, 9 - taps : 8] = rim
        rows_ref[slot, 8 : 8 + rows] = src[0, :, at : at + LANES].astype(F32)
        tail_ref[:, lanes] = rows_ref[slot, pl.ds(newest, 8)].astype(BF16)
        total = bias_ref[:, lanes]
        weight = weight_ref[:, lanes]
        for k in range(taps):
            start = 9 - taps + k
            total = total + weight[k : k + 1] * rows_ref[slot, start : start + rows]
        return silu(total).astype(BF16)

    bc_ref[:, :nstate] = conv(0, b_ref, 0, b_at + group * nstate)
    bc_ref[:, nstate:] = conv(1, c_ref, 0, c_at + group * nstate)
    b_turned = bc_ref[:, :nstate].T
    nt = (((1,), (1,)), ((), ()))
    down = lax.broadcasted_iota(jnp.int32, (LANES, LANES), 0)
    across = lax.broadcasted_iota(jnp.int32, (LANES, LANES), 1)
    same = jnp.where(down == across, 1.0, 0.0).astype(BF16)
    for p in range(pairs):
        act = conv(p % 2, x_ref, p * LANES, group * width + p * LANES)
        xa_ref[:, p * LANES : (p + 1) * LANES] = act
        _, _, ending = pair_columns(cols_ref, p, first)
        scaled = (act.astype(F32) * ending).astype(BF16)
        turned = jnp.dot(b_turned, scaled, preferred_element_type=F32).astype(BF16)
        state = lax.dot_general(same, turned, nt, preferred_element_type=F32)
        state_ref[p * LANES : (p + 1) * LANES, :] = state.astype(BF16)


def conv_half(own, ids, prefix, counts, tail, tokens, cache, before, weight, bias, ending, inner, nstate):
    _, rows, channels = tokens.shape
    heads = ending.shape[1]
    width = inner // GROUPS
    half = GROUPS // 2
    b_at, c_at = inner, inner + GROUPS * nstate

    def channel_block(wide, begin):
        return pl.BlockSpec(
            (1, rows, wide), lambda i, a, *s: (0, 0, begin // wide + first_group(a, own) + i)
        )

    def whole(value):
        return pl.BlockSpec(value.shape, lambda i, *s: (0,) * value.ndim)

    tails = [] if tail is None else [tail]
    return pl.pallas_call(
        functools.partial(conv_body, own, (b_at, c_at)),
        out_shape=(
            jax.ShapeDtypeStruct((rows, half * width), BF16),
            jax.ShapeDtypeStruct((rows, half * 2 * nstate), BF16),
            jax.ShapeDtypeStruct((half * width, nstate), BF16),
            jax.ShapeDtypeStruct((8, channels), BF16),
        ),
        grid_spec=pltpu.PrefetchScalarGridSpec(
            num_scalar_prefetch=3,
            grid=(half,),
            in_specs=[
                channel_block(width, 0),
                channel_block(nstate, b_at),
                channel_block(nstate, c_at),
                whole(cache),
                whole(before),
                whole(weight),
                whole(bias),
                whole(ending),
            ]
            + [whole(value) for value in tails],
            out_specs=[
                pl.BlockSpec((rows, width), lambda i, *s: (0, i)),
                pl.BlockSpec((rows, 2 * nstate), lambda i, *s: (0, i)),
                pl.BlockSpec((width, nstate), lambda i, *s: (i, 0)),
                pl.BlockSpec((8, channels), lambda i, *s: (0, 0)),
            ],
            scratch_shapes=[pltpu.VMEM((2, rows + 16, LANES), F32), pltpu.VMEM((rows, heads), F32)],
        ),
        compiler_params=pltpu.CompilerParams(vmem_limit_bytes=GRANT),
        cost_estimate=cost(rows * channels * 40, rows * channels * 2, rows * channels // 2),
        name="conv_half",
    )(ids, prefix, counts, tokens, tokens, tokens, cache, before, weight, bias, ending, *tails)


def owner_of(owner_ref, id_ref, page, pages):
    return owner_ref[lax.rem(id_ref[0], owner_ref.shape[0]), id_ref[1] * pages + page]


def owner_block(owners):
    deep = min(8, owners.shape[0])
    return pl.BlockSpec(
        (deep, owners.shape[1]), lambda i, d, *s: (d[0] // deep, 0), memory_space=pltpu.SMEM
    )


def decay_block(decay):
    return pl.BlockSpec(decay.shape, lambda i, *s: (0, 0), memory_space=pltpu.SMEM)


def outbound_body(
    id_ref, prefix_ref, owner_ref, mine_ref, theirs_ref, own_hbm, recv_hbm, out_ref, own_ref, recv_ref,
    page_ref, own_sem, recv_sem, sem,
):
    pages, rows, width = own_ref.shape
    lead = id_ref[1] == 0
    keep = jnp.where(prefix_ref[id_ref[0]] > 0, 1.0, 0.0)
    top = lax.broadcasted_iota(jnp.int32, (TAIL, width), 0) == 0
    own_in = part_copies(own_hbm, own_ref, own_sem, PARTS)
    recv_in = part_copies(recv_hbm, recv_ref, recv_sem, PARTS)
    for c in range(PARTS):
        own_in[c].start()
        recv_in[c].start()
    outs = []
    for c in range(PARTS):
        own_in[c].wait()
        recv_in[c].wait()
        for k in range(pages // PARTS):
            page = c * (pages // PARTS) + k
            head = id_ref[1] * pages + page
            mine, theirs = mine_ref[0, head], theirs_ref[0, head]
            own_w = jnp.where(lead, theirs, 1.0)
            recv_w = jnp.where(lead, 1.0, mine)
            total = own_w * own_ref[page].astype(F32) + recv_w * recv_ref[page].astype(F32)
            whole = jnp.full((TAIL, width), mine * theirs * keep, F32)
            high = whole.astype(BF16).astype(F32)
            page_ref[page, :rows] = total.astype(BF16)
            page_ref[page, rows:] = jnp.where(top, high, whole - high).astype(BF16)
        for k in range(pages // PARTS):
            page = c * (pages // PARTS) + k
            owner = owner_of(owner_ref, id_ref, page, pages)
            copy = pltpu.make_async_copy(page_ref.at[page], out_ref.at[owner], sem.at[page])
            copy.start()
            outs.append(copy)
    for copy in outs:
        copy.wait()


def outbound_pages(ids, prefix, owners, mine, theirs, own, recv, devices):
    pages, rows, width = own.shape
    return pl.pallas_call(
        outbound_body,
        out_shape=jax.ShapeDtypeStruct((devices, rows + TAIL, width), BF16),
        grid_spec=pltpu.PrefetchScalarGridSpec(
            num_scalar_prefetch=2,
            grid=(1,),
            in_specs=[owner_block(owners), decay_block(mine), decay_block(theirs), IN_HBM, IN_HBM],
            out_specs=IN_HBM,
            scratch_shapes=[
                pltpu.VMEM(own.shape, BF16),
                pltpu.VMEM(own.shape, BF16),
                pltpu.VMEM((pages, rows + TAIL, width), BF16),
                pltpu.SemaphoreType.DMA((PARTS,)),
                pltpu.SemaphoreType.DMA((PARTS,)),
                pltpu.SemaphoreType.DMA((pages,)),
            ],
        ),
        compiler_params=pltpu.CompilerParams(vmem_limit_bytes=GRANT),
        cost_estimate=cost(pages * rows * width * 3, pages * rows * width * 6),
        name="outbound_pages",
    )(ids, prefix, owners, mine, theirs, own, recv)


def start_body(
    id_ref, prefix_ref, owner_ref, mine_ref, theirs_ref, in_ref, own_hbm, recv_hbm, start_hbm, send_hbm,
    page_ref, state_ref, held_ref, moved_ref, sem, state_sem, held_sem, moved_sem,
):
    pages = page_ref.shape[0]
    keep = jnp.where(prefix_ref[id_ref[0]] > 0, 1.0, 0.0)

    def run(decay_ref, state_hbm, held_hbm, moved_hbm):
        states = part_copies(state_hbm, state_ref, state_sem, PARTS)
        held_out = part_copies(held_ref, held_hbm, held_sem, PARTS)
        moved_out = part_copies(moved_ref, moved_hbm, moved_sem, PARTS)
        fetches = []
        for page in range(pages):
            owner = owner_of(owner_ref, id_ref, page, pages)
            fetches.append(pltpu.make_async_copy(in_ref.at[owner], page_ref.at[page], sem.at[page]))
        for c in range(PARTS):
            states[c].start()
            for k in range(pages // PARTS):
                fetches[c * (pages // PARTS) + k].start()
        for c in range(PARTS):
            states[c].wait()
            for k in range(pages // PARTS):
                fetches[c * (pages // PARTS) + k].wait()
            for k in range(pages // PARTS):
                page = c * (pages // PARTS) + k
                held = page_ref[page].astype(F32) * keep
                decay = decay_ref[0, id_ref[1] * pages + page]
                held_ref[page] = held.astype(BF16)
                moved_ref[page] = (decay * held + state_ref[page].astype(F32)).astype(BF16)
            held_out[c].start()
            moved_out[c].start()
        for copy in held_out + moved_out:
            copy.wait()

    @pl.when(id_ref[1] == 0)
    def _():
        run(mine_ref, own_hbm, start_hbm, send_hbm)

    @pl.when(id_ref[1] != 0)
    def _():
        run(theirs_ref, recv_hbm, send_hbm, start_hbm)


def start_states(ids, prefix, owners, mine, theirs, incoming, own, recv):
    pages, rows, width = own.shape
    return pl.pallas_call(
        start_body,
        out_shape=(jax.ShapeDtypeStruct(own.shape, BF16),) * 2,
        grid_spec=pltpu.PrefetchScalarGridSpec(
            num_scalar_prefetch=2,
            grid=(1,),
            in_specs=[owner_block(owners), decay_block(mine), decay_block(theirs)] + [IN_HBM] * 3,
            out_specs=[IN_HBM, IN_HBM],
            scratch_shapes=[pltpu.VMEM(own.shape, BF16)] * 4
            + [pltpu.SemaphoreType.DMA((pages,))]
            + [pltpu.SemaphoreType.DMA((PARTS,))] * 3,
        ),
        compiler_params=pltpu.CompilerParams(vmem_limit_bytes=GRANT),
        cost_estimate=cost(pages * rows * width * 4, pages * rows * width * 8),
        name="start_states",
    )(ids, prefix, owners, mine, theirs, incoming, own, recv)


def mixer_body(
    own, id_ref, count_ref, skip_ref, x_ref, bc_ref, cum_ref, shift_ref, start_ref, gate_ref,
    norm_ref, *rest
):
    out_ref, cols_ref, score_ref, gated_ref = rest[-4:]
    group = first_group(id_ref, own) + pl.program_id(0)
    rows, width = x_ref.shape
    pairs = width // LANES
    half = rows // 2
    first = lax.broadcasted_iota(jnp.int32, (rows, LANES), 1) < LANES // 2
    cols_ref[...] = group_heads(cum_ref, group, 2 * pairs)
    nstate = start_ref.shape[1]
    b_val, c_val = bc_ref[:, :nstate], bc_ref[:, nstate:]
    nt = (((1,), (1,)), ((), ()))
    scores = lax.dot_general(c_val, b_val, nt, preferred_element_type=F32)
    lower = (
        lax.broadcasted_iota(jnp.int32, (rows, rows), 0)
        >= lax.broadcasted_iota(jnp.int32, (rows, rows), 1)
    )
    score_ref[...] = jnp.where(lower, scores, 0.0)
    squares = jnp.zeros((rows, LANES), F32)
    for p in range(pairs):
        lanes = slice(p * LANES, (p + 1) * LANES)
        x_val = x_ref[:, lanes]
        left, right, both = pair_columns(cols_ref, p, first)
        ys = []
        for cum, h in ((left, 2 * p), (right, 2 * p + 1)):
            early = shift_ref[h : h + 1, :half]
            late = shift_ref[h : h + 1, half:]
            w00 = score_ref[:half, :half] * jnp.exp(jnp.minimum(cum[:half] - early, TOP))
            w10 = score_ref[half:, :half] * jnp.exp(cum[half:] - early)
            w11 = score_ref[half:, half:] * jnp.exp(jnp.minimum(cum[half:] - late, TOP))
            y0 = jnp.dot(w00.astype(BF16), x_val[:half], preferred_element_type=F32)
            w1 = jnp.concatenate([w10.astype(BF16), w11.astype(BF16)], axis=1)
            y1 = jnp.dot(w1, x_val, preferred_element_type=F32)
            ys.append(jnp.concatenate([y0, y1], axis=0))
        carried = lax.dot_general(c_val, start_ref[lanes, :], nt, preferred_element_type=F32)
        y = jnp.where(first, ys[0], ys[1]) + jnp.exp(both) * carried
        head = group * 2 * pairs + 2 * p
        skip = jnp.where(first, skip_ref[head], skip_ref[head + 1])
        y = y + skip * x_val.astype(F32)
        gated = y * silu(gate_ref[0, :, lanes].astype(F32))
        gated_ref[p] = gated
        squares = squares + gated * gated
    mean = jnp.sum(squares, axis=1, keepdims=True) * (1.0 / width)
    pos = id_ref[1] * rows + lax.broadcasted_iota(jnp.int32, (rows, 1), 0)
    live = pos < count_ref[id_ref[0]]
    factor = jnp.where(live, lax.rsqrt(mean + 1e-05), 0.0)
    factor = jnp.broadcast_to(factor, (rows, LANES))
    for p in range(pairs):
        lanes = slice(p * LANES, (p + 1) * LANES)
        at = pl.ds(pl.multiple_of(group * width + p * LANES, LANES), LANES)
        out_ref[0, :, lanes] = (gated_ref[p] * factor * norm_ref[:, at]).astype(BF16)


def mixer_half(own, ids, counts, skip, x, bc, cum, shift, start, gate, norm, so_far):
    rows, half_width = x.shape
    heads = cum.shape[1]
    half = GROUPS // 2
    width = half_width // half
    nstate = start.shape[1]
    per_group = heads // GROUPS
    in_specs = [
        pl.BlockSpec((rows, width), lambda i, a, *s: (0, i)),
        pl.BlockSpec((rows, 2 * nstate), lambda i, a, *s: (0, i)),
        pl.BlockSpec((rows, heads), lambda i, a, *s: (0, 0)),
        pl.BlockSpec((per_group, rows), lambda i, a, *s: (first_group(a, own) + i, 0)),
        pl.BlockSpec((width, nstate), lambda i, a, *s: (i, 0)),
        pl.BlockSpec((1, rows, width), lambda i, a, *s: (0, 0, first_group(a, own) + i)),
        pl.BlockSpec(norm.shape, lambda i, a, *s: (0, 0)),
    ]
    args = [ids, counts, skip, x, bc, cum, shift, start, gate, norm]
    aliases = {}
    if so_far is not None:
        in_specs.append(pl.BlockSpec(memory_space=pl.ANY))
        aliases = {len(args): 0}
        args.append(so_far)
    return pl.pallas_call(
        functools.partial(mixer_body, own),
        out_shape=jax.ShapeDtypeStruct(gate.shape, BF16),
        grid_spec=pltpu.PrefetchScalarGridSpec(
            num_scalar_prefetch=3,
            grid=(half,),
            in_specs=in_specs,
            out_specs=pl.BlockSpec((1, rows, width), lambda i, a, *s: (0, 0, first_group(a, own) + i)),
            scratch_shapes=[
                pltpu.VMEM((rows, heads), F32),
                pltpu.VMEM((rows, rows), F32),
                pltpu.VMEM((width // LANES, rows, LANES), F32),
            ],
        ),
        input_output_aliases=aliases,
        compiler_params=pltpu.CompilerParams(vmem_limit_bytes=GRANT),
        cost_estimate=cost(
            rows * half_width * (2 * rows + 2 * nstate), rows * half_width * 8, rows * rows * heads // 2
        ),
        name="mixer_half",
    )(*args)


def pool_body(dev_ref, pool_hbm, in_hbm, out_hbm, in_ref, pool_ref, new_ref, in_sem, pool_sem, out_sem):
    slots, rows, _ = pool_ref.shape
    parts = 2 * PARTS
    size = slots // parts
    pages = part_copies(in_hbm, in_ref, in_sem, PARTS)
    pools = part_copies(pool_hbm, pool_ref, pool_sem, parts)
    outs = part_copies(new_ref, out_hbm, out_sem, parts)
    for copy in pages + pools:
        copy.start()
    for copy in pages:
        copy.wait()
    for c in range(parts):
        pools[c].wait()
        for k in range(size):
            slot = c * size + k
            device = dev_ref[slot]
            at = jnp.maximum(device, 0)
            tail = in_ref[at, rows:].astype(F32)
            whole = tail[0:1] + tail[1:2]
            old = pool_ref[slot]
            new = whole * old + in_ref[at, :rows].astype(F32)
            new_ref[slot] = jnp.where(device >= 0, new, old)
        outs[c].start()
    for copy in outs:
        copy.wait()


def updated_pool(dev_of_slot, pool, returned):
    slots, rows, width = pool.shape
    return pl.pallas_call(
        pool_body,
        out_shape=jax.ShapeDtypeStruct(pool.shape, F32),
        grid_spec=pltpu.PrefetchScalarGridSpec(
            num_scalar_prefetch=1,
            grid=(1,),
            in_specs=[IN_HBM, IN_HBM],
            out_specs=IN_HBM,
            scratch_shapes=[
                pltpu.VMEM(returned.shape, BF16),
                pltpu.VMEM(pool.shape, F32),
                pltpu.VMEM(pool.shape, F32),
                pltpu.SemaphoreType.DMA((PARTS,)),
                pltpu.SemaphoreType.DMA((2 * PARTS,)),
                pltpu.SemaphoreType.DMA((2 * PARTS,)),
            ],
        ),
        compiler_params=pltpu.CompilerParams(vmem_limit_bytes=GRANT),
        cost_estimate=cost(slots * rows * width * 2, slots * rows * width * 10),
        name="updated_pool",
    )(dev_of_slot, pool, returned)


def local(
    conv_input,
    gate_input,
    dt_raw,
    conv_weight,
    conv_bias,
    dt_bias,
    a_log,
    d_skip,
    norm_weight,
    conv_cache,
    state_pool,
    page_owner,
    page_slot,
    prefix_len,
    new_count,
):
    ctx_count = lax.axis_size("ctx")
    devices = lax.axis_size("req") * ctx_count
    req_index = lax.axis_index("req")
    ctx_index = lax.axis_index("ctx")
    own_index = req_index * ctx_count + ctx_index
    rows = conv_input.shape[1]
    heads = dt_raw.shape[2]
    inner = gate_input.shape[2]
    slots, page_rows, nstate = state_pool.shape
    pages = page_owner.shape[1] // ctx_count
    rim = conv_weight.shape[0] - 1
    requests = page_owner.shape[0]

    matches = page_owner == own_index
    early = jnp.arange(2 * pages)[None, :] < pages
    slot_0 = jnp.max(jnp.where(matches & early, page_slot, -1), axis=1)
    slot_1 = jnp.max(jnp.where(matches & ~early, page_slot, -1), axis=1)
    outgoing = gather_pages(slot_0, slot_1, state_pool, devices)
    outgoing, conv_input, dt_raw, new_count, prefix_len, page_owner = lax.optimization_barrier(
        (outgoing, conv_input, dt_raw, new_count, prefix_len, page_owner)
    )
    incoming = lax.all_to_all(outgoing, ("req", "ctx"), split_axis=0, concat_axis=0, tiled=True)

    ids = jnp.stack([req_index, ctx_index]).astype(jnp.int32)
    previous = lax.ppermute(conv_input[0, rows - rim :], "ctx", [(0, 1)])
    cum, shift, ending, decay_rows = step_tables(ids, new_count, dt_raw, dt_bias, a_log)
    other_decay = swapped(decay_rows)

    conv_args = (
        conv_input, conv_cache, previous, conv_weight, conv_bias[None], ending, inner, nstate
    )
    x_other, bc_other, state_other, tail = conv_half(False, ids, prefix_len, new_count, None, *conv_args)
    received = swapped(state_other)
    x_own, bc_own, state_own, tail = conv_half(True, ids, prefix_len, new_count, tail, *conv_args)
    as_pages = lambda value: value.reshape(pages, page_rows, nstate)
    own_pages, recv_pages = as_pages(state_own), as_pages(received)
    page_args = (ids, prefix_len, page_owner, decay_rows, other_decay)
    outbound = outbound_pages(*page_args, own_pages, recv_pages, devices)
    returned = lax.all_to_all(outbound, ("req", "ctx"), split_axis=0, concat_axis=0, tiled=True)

    start, send = start_states(*page_args, incoming, own_pages, recv_pages)
    start, slot_0, slot_1, late_count, tail = lax.optimization_barrier(
        (start, slot_0, slot_1, new_count, tail)
    )
    start_other = swapped(send)
    as_rows = lambda value: value.reshape(pages * page_rows, nstate)
    mixed = mixer_half(
        True, ids, new_count, d_skip, x_own, bc_own, cum, shift, as_rows(start), gate_input,
        norm_weight[None], None,
    )
    mixed = mixer_half(
        False, ids, new_count, d_skip, x_other, bc_other, cum, shift, as_rows(start_other),
        gate_input, norm_weight[None], mixed,
    )

    other_tail = swapped(tail)
    mine = (late_count[req_index] > rows) == (ctx_index == 1)
    new_tail = jnp.where(mine, tail, other_tail)[:rim]
    slot_ids = jnp.arange(slots, dtype=jnp.int32)[:, None]
    request_ids = jnp.arange(requests, dtype=jnp.int32)[None, :]
    hits_0, hits_1 = slot_0[None, :] == slot_ids, slot_1[None, :] == slot_ids
    dev_of_slot = jnp.max(
        jnp.maximum(
            jnp.where(hits_0, 2 * request_ids, -1), jnp.where(hits_1, 2 * request_ids + 1, -1)
        ),
        axis=1,
    )
    new_pool = updated_pool(dev_of_slot, state_pool, returned)
    return (mixed, new_tail[None], new_pool)


def solution(mesh):
    return jax.shard_map(
        local,
        mesh=mesh,
        in_specs=(
            P("req", "ctx", None),
            P("req", "ctx", None),
            P("req", "ctx", None),
            P(),
            P(),
            P(),
            P(),
            P(),
            P(),
            P("req", None, None),
            P(("req", "ctx"), None, None),
            P(),
            P(),
            P(),
            P(),
        ),
        out_specs=(P("req", "ctx", None), P("req", None, None), P(("req", "ctx"), None, None)),
        check_vma=False,
    )
```

time: 114 us -> 99.2 us (0.87)
  local copies, waits for them, and re-layouts: 8.88 us -> 2.84 us
  Pallas kernels: 65.1 us -> 59.6 us
  matrix products: 3.31 us -> 0 us
  waiting for transfers between devices: 4.2 us -> 1.73 us
  starting transfers between devices: 25.1 us -> 26.9 us
    unnamed x12 -> x0, local copies, waits for them, and re-layouts: 5.35 us -> none
    dot_general x1 -> x0, matrix products: 3.31 us -> none  [local(): jnp.dot(picks, conv_input[0], preferred_element_type=F32).astype(BF16)]
    all_to_all x1, waiting for transfers between devices: 4.19 us -> 1.71 us  [local(): lax.all_to_all(outbound, ('req', 'ctx'), split_axis=0, concat_axis=0, til...]
    pallas_call x2, Pallas kernels: 19.9 us -> 17.8 us  [conv_half(): pl.pallas_call(functools.partial(conv_body, own, (b_at, c_at)), out_shape...]
    pallas_call x1, Pallas kernels: 7.14 us -> 5.63 us  [updated_pool(): pl.pallas_call(pool_body, out_shape=jax.ShapeDtypeStruct(pool.shape, F32)...]
    select_n x1 -> x0, other arithmetic: 1.37 us -> none  [local(): decay_late = jnp.where(ctx_first, theirs, mine)]
    squeeze x1 -> x0, local copies, waits for them, and re-layouts: 1.27 us -> none  [local(): lax.dynamic_slice(page_owner, (req_index, ctx_index * pages), (1, pages))[0]]
  transfers between devices with their start and end apart: 7 -> 7, of which waited for: 1 -> 1; matrix products, arithmetic and copies ran while one was open for 9% -> 7% of each run, Pallas kernels for 46% -> 51%
where the time goes in v3:
time: 99.2 us; the launch traced here: 98.4 us
  Pallas kernels  59.6 us (60%)
  starting transfers between devices  26.9 us (27%)
  other arithmetic  5.77 us (6%)
  local copies, waits for them, and re-layouts  2.84 us (3%)
  waiting for transfers between devices  1.73 us (2%)
  between operations  1.55 us (2%)
    pallas_call x2, Pallas kernels, mixer_half(): pl.pallas_call(functools.partial(mixer_body, own), out_shape=jax.ShapeDty...  19.7 us
    pallas_call x2, Pallas kernels, conv_half(): pl.pallas_call(functools.partial(conv_body, own, (b_at, c_at)), out_shape...  17.8 us
    all_to_all x1, starting transfers between devices, local(): lax.all_to_all(outgoing, ('req', 'ctx'), split_axis=0, concat_axis=0, til...  12 us
    all_to_all x1, starting transfers between devices, local(): lax.all_to_all(outbound, ('req', 'ctx'), split_axis=0, concat_axis=0, til...  10.2 us
    pallas_call x1, Pallas kernels, updated_pool(): pl.pallas_call(pool_body, out_shape=jax.ShapeDtypeStruct(pool.shape, F32)...  5.63 us
    pallas_call x1, Pallas kernels, start_states(): pl.pallas_call(start_body, out_shape=(jax.ShapeDtypeStruct(own.shape, BF1...  5.1 us
    pallas_call x1, Pallas kernels, outbound_pages(): pl.pallas_call(outbound_body, out_shape=jax.ShapeDtypeStruct((devices, ro...  4.48 us
    pallas_call x1, Pallas kernels, gather_pages(): pl.pallas_call(gather_body, out_shape=jax.ShapeDtypeStruct((devices, rows...  4.27 us
  transfers between devices with their start and end apart: 7, of which 1 were waited for; matrix products, arithmetic and copies ran while one was open for 7% of the time, Pallas kernels for 51%

profile of v3, /device:TPU:1, one launch (start us, length us, event | category | flops | bytes accessed | tf_op | source)
XLA Modules:
  0.0 98.4 jit_solution(12498080699397541538)
XLA Ops:
  0.7 1.5 %select_reduce_fusion = (s32[64]{0:T(128)}, s32[64]{0:T(128)}) fusion(s32[64,128]{1,0:T(8,128)} %param.27, pred[128]{0:T(512)(128)(4,1)S(1)} %get-tuple-element.56, pred[128]{0:T(512)(128)(4,1)S(1)} %get-tuple-element.55, s32[64,128]{1,0:T(8,128)} %owner_ref.1, s32[]{:T(128)S(6)} %add.17), kind=kLoop, calls=%fused_computation.6 | loop fusion | flops 57216 | bytes 66308 | tf_op jit(solution)/shard_map/reduce_max | solution.py:589
  2.1 4.3 %gather_pages.1 = bf16[128,64,128]{2,1,0:T(8,128)(2,1)} custom-call(s32[64]{0:T(128)} %get-tuple-element.51.early_ref, s32[64]{0:T(128)} %get-tuple-element.52.late_ref, f32[128,64,128]{2,1,0:T(8,128)} %pool_hbm.1), custom_call_target="tpu_custom_call" | custom-call | flops 1048576 | bytes 6291456 | tf_op jit(solution)/shard_map/gather_pages/pallas_call | solution.py:64
  6.4 12.0 %all-to-all-start = ((bf16[128,64,128]{2,1,0:T(8,128)(2,1)}), bf16[128,64,128]{2,1,0:T(8,128)(2,1)}, u32[]{:S(2)}, u32[]{:S(2)}) async-start(bf16[128,64,128]{2,1,0:T(8,128)(2,1)} %gather_pages.1), calls=%async_computation | async-start | bytes 4194304 | tf_op jit(solution)/shard_map/all_to_all | solution.py:594
  18.4 1.6 %slice_bitcast_fusion = bf16[3,10240]{1,0:T(4,128)(2,1)} fusion(bf16[1,256,10240]{2,1,0:T(8,128)(2,1)} %c_ref.1), kind=kLoop, calls=%fused_computation.2 | loop fusion | bytes 122880 | tf_op jit(solution)/shard_map/squeeze | solution.py:597
  20.0 1.3 %collective-permute-start = (bf16[3,10240]{1,0:T(4,128)(2,1)}, bf16[3,10240]{1,0:T(4,128)(2,1)}, u32[]{:S(2)}, u32[]{:S(2)}) collective-permute-start(bf16[3,10240]{1,0:T(4,128)(2,1)} %slice_bitcast_fusion), channel_id=1, source_target_pairs={{0,1},{2,3},{4,5},{6,7},{8,9},{10,11},{12,13},{14,15},{16,17},{18,... | collective-permute-start | bytes 184328 | tf_op jit(solution)/shard_map/ppermute | solution.py:597
  21.3 0.6 pad_add_fusion.id_ref
  21.9 2.6 %step_tables.1 = (f32[256,128]{1,0:T(8,128)}, f32[128,256]{1,0:T(8,128)}, f32[256,128]{1,0:T(8,128)}, f32[8,128]{1,0:T(8,128)}) custom-call(s32[2]{0:T(128)} %pad_add_fusion.id_ref, s32[64]{0:T(128)} %count_ref.4, bf16[1,256,128]{2,1,0:T(8,128)(2,1)} %raw_ref, f32[1,128]{1,0:T(1,128)} %bitcast.22, f32[1,128]{1,0:T(1,128)} %bitcast.23), custom_call_target="tpu_custom_call" | custom-call | flops 50331648 | bytes 524288 | tf_op jit(solution)/shard_map/step_tables/pallas_call | solution.py:119
  24.6 0.0 collective-permute-done.before_ref
  24.6 8.8 %conv_half.2 = (bf16[256,4096]{1,0:T(8,128)(2,1)}, bf16[256,1024]{1,0:T(8,128)(2,1)}, bf16[4096,128]{1,0:T(8,128)(2,1)}, bf16[8,10240]{1,0:T(8,128)(2,1)}) custom-call(s32[2]{0:T(128)} %pad_add_fusion.id_ref, s32[64]{0:T(128)} %prefix_ref.3, s32[64]{0:T(128)} %count_ref.4, bf16[1,256,10240]{2,1,0:T(8,128)(2,1)} %c_ref.1, bf16[1,256,10240]{2,1,0:T(8,128)(2,1)} %c_ref.1, ...), custom_call_target="tpu_custom_call" | custom-call | flops 104857600 | bytes 5242880 | tf_op jit(solution)/shard_map/conv_half/pallas_call | solution.py:227
  33.4 1.8 %collective-permute-start.2 = (bf16[4096,128]{1,0:T(8,128)(2,1)}, bf16[4096,128]{1,0:T(8,128)(2,1)}, u32[]{:S(2)}, u32[]{:S(2)}) collective-permute-start(bf16[4096,128]{1,0:T(8,128)(2,1)} %get-tuple-element.42), channel_id=1, source_target_pairs={{0,1},{1,0},{2,3},{3,2},{4,5},{5,4},{6,7},{7,6},{8,9},{9,8},{10,11... | collective-permute-start | bytes 3145736 | tf_op jit(solution)/shard_map/ppermute | solution.py:22
  35.2 0.1 collective-permute-start.1
  35.3 0.6 iota_multiply_fusion
  35.9 9.0 %conv_half.3 = (bf16[256,4096]{1,0:T(8,128)(2,1)}, bf16[256,1024]{1,0:T(8,128)(2,1)}, bf16[4096,128]{1,0:T(8,128)(2,1)}, bf16[8,10240]{1,0:T(8,128)(2,1)}) custom-call(s32[2]{0:T(128)} %pad_add_fusion.id_ref, s32[64]{0:T(128)} %prefix_ref.3, s32[64]{0:T(128)} %count_ref.4, bf16[1,256,10240]{2,1,0:T(8,128)(2,1)} %c_ref.1, bf16[1,256,10240]{2,1,0:T(8,128)(2,1)} %c_ref.1, ...), custom_call_target="tpu_custom_call" | custom-call | flops 104857600 | bytes 5242880 | tf_op jit(solution)/shard_map/conv_half/pallas_call | solution.py:227
  44.9 0.0 collective-permute-done.1.theirs_ref
  44.9 0.0 collective-permute-done.2
  44.9 4.5 %outbound_pages.1 = bf16[128,72,128]{2,1,0:T(8,128)(2,1)} custom-call(s32[2]{0:T(128)} %pad_add_fusion.id_ref, s32[64]{0:T(128)} %prefix_ref.3, s32[64,128]{1,0:T(8,128)} %owner_ref.1, f32[8,128]{1,0:T(8,128)} %get-tuple-element.38.mine_ref, f32[8,128]{1,0:T(8,128)} %collective-permute-done.1.theirs_ref, bf16[64,64,128]{2,1,0:T(8,128)(2,1)} %bitcast.15, ...), custom_call_target="tpu_custom_call" | custom-call | flops 1572864 | bytes 3145728 | tf_op jit(solution)/shard_map/outbound_pages/pallas_call | solution.py:318
  49.4 0.0 all-to-all-done.in_ref
  49.4 10.2 %all-to-all-start.1 = ((bf16[128,72,128]{2,1,0:T(8,128)(2,1)}), bf16[128,72,128]{2,1,0:T(8,128)(2,1)}, u32[]{:S(2)}, u32[]{:S(2)}) async-start(bf16[128,72,128]{2,1,0:T(8,128)(2,1)} %outbound_pages.1), calls=%async_computation.1 | async-start | bytes 4718592 | tf_op jit(solution)/shard_map/all_to_all | solution.py:611
  59.6 5.1 %start_states.1 = (bf16[64,64,128]{2,1,0:T(8,128)(2,1)}, bf16[64,64,128]{2,1,0:T(8,128)(2,1)}) custom-call(s32[2]{0:T(128)} %pad_add_fusion.id_ref, s32[64]{0:T(128)} %prefix_ref.3, s32[64,128]{1,0:T(8,128)} %owner_ref.1, f32[8,128]{1,0:T(8,128)} %get-tuple-element.38.mine_ref, f32[8,128]{1,0:T(8,128)} %collective-permute-done.1.theirs_ref, ...), custom_call_target="tpu_custom_call" | custom-call | flops 2097152 | bytes 4194304 | tf_op jit(solution)/shard_map/start_states/pallas_call | solution.py:386
  64.7 1.2 %collective-permute-start.3 = (bf16[64,64,128]{2,1,0:T(8,128)(2,1)}, bf16[64,64,128]{2,1,0:T(8,128)(2,1)}, u32[]{:S(2)}, u32[]{:S(2)}) collective-permute-start(bf16[64,64,128]{2,1,0:T(8,128)(2,1)} %get-tuple-element.43), channel_id=1, source_target_pairs={{0,1},{1,0},{2,3},{3,2},{4,5},{5,4},{6,7},{7,6},{8,9},{9,8},{10,11... | collective-permute-start | bytes 3145736 | tf_op jit(solution)/shard_map/ppermute | solution.py:22
  65.9 0.3 collective-permute-start.4
  66.2 1.4 %maximum_reduce_fusion.dev_ref = s32[128]{0:T(128)} fusion(s32[64]{0:T(128)} %get-tuple-element.58, s32[64]{0:T(128)} %get-tuple-element.52.late_ref, s32[64]{0:T(128)} %get-tuple-element.57, s32[64]{0:T(128)} %get-tuple-element.51.early_ref), kind=kLoop, calls=%fused_computation.3 | loop fusion | flops 49024 | bytes 1536 | tf_op jit(solution)/shard_map/reduce_max | solution.py:634
  67.6 9.9 %mixer_half.2.rest_0_ = bf16[1,256,8192]{2,1,0:T(8,128)(2,1)} custom-call(s32[2]{0:T(128)} %pad_add_fusion.id_ref, s32[64]{0:T(128)} %count_ref.4, f32[128]{0:T(128)} %skip_ref.3, bf16[256,4096]{1,0:T(8,128)(2,1)} %get-tuple-element.44.x_ref, bf16[256,1024]{1,0:T(8,128)(2,1)} %get-tuple-element.45.bc_ref, f32[256,128]{1,0:T(8,128)} %get-tuple-element.35.cum_ref, ...), custom_call_target="tpu_custom_call" | custom-call | flops 805306368 | bytes 8388608 | tf_op jit(solution)/shard_map/mixer_half/pallas_call | solution.py:481
  77.4 1.2 %dynamic_slice.3 = s32[1]{0:T(128)} dynamic-slice(s32[64]{0:T(128)} %count_ref.4, s32[]{:T(128)S(6)} %select_n.27), dynamic_slice_sizes={1} | dynamic-slice | bytes 12 | tf_op jit(solution)/shard_map/dynamic_slice | solution.py:629
  79.3 0.0 collective-permute-done.4
  79.3 1.7 %fusion = bf16[1,3,10240]{2,1,0:T(4,128)(2,1)} fusion(bf16[8,10240]{1,0:T(8,128)(2,1)} %collective-permute-done.4, bf16[8,10240]{1,0:T(8,128)(2,1)} %get-tuple-element.50, pred[]{:T(512)S(6)} %eq.41), kind=kLoop, calls=%fused_computation.1 | loop fusion | flops 30720 | bytes 184321 | tf_op jit(solution)/shard_map/broadcast_in_dim | solution.py:641
  81.0 0.0 collective-permute-done.3
  81.0 9.8 %mixer_half.3 = bf16[1,256,8192]{2,1,0:T(8,128)(2,1)} custom-call(s32[2]{0:T(128)} %pad_add_fusion.id_ref, s32[64]{0:T(128)} %count_ref.4, f32[128]{0:T(128)} %skip_ref.3, bf16[256,4096]{1,0:T(8,128)(2,1)} %get-tuple-element.33.x_ref, bf16[256,1024]{1,0:T(8,128)(2,1)} %get-tuple-element.34.bc_ref, ...), custom_call_target="tpu_custom_call", output_to_operand_aliasing={{}: (10, {})} | custom-call | flops 805306368 | bytes 8388608 | tf_op jit(solution)/shard_map/mixer_half/pallas_call | solution.py:481
  90.8 1.7 %all-to-all-done.1.in_hbm = bf16[128,72,128]{2,1,0:T(8,128)(2,1)} async-done(((bf16[128,72,128]{2,1,0:T(8,128)(2,1)}), bf16[128,72,128]{2,1,0:T(8,128)(2,1)}, u32[]{:S(2)}, u32[]{:S(2)}) %all-to-all-start.1) | async-done | bytes 2359328 | tf_op jit(solution)/shard_map/all_to_all | solution.py:611
  92.6 5.6 %updated_pool.1 = f32[128,64,128]{2,1,0:T(8,128)} custom-call(s32[128]{0:T(128)} %maximum_reduce_fusion.dev_ref, f32[128,64,128]{2,1,0:T(8,128)} %pool_hbm.1, bf16[128,72,128]{2,1,0:T(8,128)(2,1)} %all-to-all-done.1.in_hbm), custom_call_target="tpu_custom_call" | custom-call | flops 2097152 | bytes 10485760 | tf_op jit(solution)/shard_map/updated_pool/pallas_call | solution.py:533
  (1 shorter events, 0.0 us)
Async XLA Ops:
  6.4 43.0 %all-to-all-start = ((bf16[128,64,128]{2,1,0:T(8,128)(2,1)}), bf16[128,64,128]{2,1,0:T(8,128)(2,1)}, u32[]{:S(2)}, u32[]{:S(2)}) async-start(bf16[128,64,128]{2,1,0:T(8,128)(2,1)} %gather_pages.1), calls=%async_computation | async-start | bytes 4194304 | tf_op jit(solution)/shard_map/all_to_all | solution.py:594
  20.0 4.6 %collective-permute-start = (bf16[3,10240]{1,0:T(4,128)(2,1)}, bf16[3,10240]{1,0:T(4,128)(2,1)}, u32[]{:S(2)}, u32[]{:S(2)}) collective-permute-start(bf16[3,10240]{1,0:T(4,128)(2,1)} %slice_bitcast_fusion), channel_id=1, source_target_pairs={{0,1},{2,3},{4,5},{6,7},{8,9},{10,11},{12,13},{14,15},{16,17},{18,... | collective-permute-start | bytes 184328 | tf_op jit(solution)/shard_map/ppermute | solution.py:597
  33.4 11.5 %collective-permute-start.2 = (bf16[4096,128]{1,0:T(8,128)(2,1)}, bf16[4096,128]{1,0:T(8,128)(2,1)}, u32[]{:S(2)}, u32[]{:S(2)}) collective-permute-start(bf16[4096,128]{1,0:T(8,128)(2,1)} %get-tuple-element.42), channel_id=1, source_target_pairs={{0,1},{1,0},{2,3},{3,2},{4,5},{5,4},{6,7},{7,6},{8,9},{9,8},{10,11... | collective-permute-start | bytes 3145736 | tf_op jit(solution)/shard_map/ppermute | solution.py:22
  35.2 9.7 %collective-permute-start.1 = (f32[8,128]{1,0:T(8,128)}, f32[8,128]{1,0:T(8,128)}, u32[]{:S(2)}, u32[]{:S(2)}) collective-permute-start(f32[8,128]{1,0:T(8,128)} %get-tuple-element.38.mine_ref), channel_id=1, source_target_pairs={{0,1},{1,0},{2,3},{3,2},{4,5},{5,4},{6,7},{7,6},{8,9},{9,8},{10,11... | collective-permute-start | bytes 12296 | tf_op jit(solution)/shard_map/ppermute | solution.py:22
  49.4 43.2 %all-to-all-start.1 = ((bf16[128,72,128]{2,1,0:T(8,128)(2,1)}), bf16[128,72,128]{2,1,0:T(8,128)(2,1)}, u32[]{:S(2)}, u32[]{:S(2)}) async-start(bf16[128,72,128]{2,1,0:T(8,128)(2,1)} %outbound_pages.1), calls=%async_computation.1 | async-start | bytes 4718592 | tf_op jit(solution)/shard_map/all_to_all | solution.py:611
  64.7 16.3 %collective-permute-start.3 = (bf16[64,64,128]{2,1,0:T(8,128)(2,1)}, bf16[64,64,128]{2,1,0:T(8,128)(2,1)}, u32[]{:S(2)}, u32[]{:S(2)}) collective-permute-start(bf16[64,64,128]{2,1,0:T(8,128)(2,1)} %get-tuple-element.43), channel_id=1, source_target_pairs={{0,1},{1,0},{2,3},{3,2},{4,5},{5,4},{6,7},{7,6},{8,9},{9,8},{10,11... | collective-permute-start | bytes 3145736 | tf_op jit(solution)/shard_map/ppermute | solution.py:22
  65.9 13.4 %collective-permute-start.4 = (bf16[8,10240]{1,0:T(8,128)(2,1)}, bf16[8,10240]{1,0:T(8,128)(2,1)}, u32[]{:S(2)}, u32[]{:S(2)}) collective-permute-start(bf16[8,10240]{1,0:T(8,128)(2,1)} %get-tuple-element.50), channel_id=1, source_target_pairs={{0,1},{1,0},{2,3},{3,2},{4,5},{5,4},{6,7},{7,6},{8,9},{9,8},{10,11... | collective-permute-start | bytes 491528 | tf_op jit(solution)/shard_map/ppermute | solution.py:22

commit v4 on v3

--- a/solution.py
+++ b/solution.py
@@ -41,12 +41,23 @@
     ]
 
 
-def gather_body(early_ref, late_ref, pool_ref, out_ref, page_ref, round_ref, in_sem, out_sem):
+def gather_body(
+    early_ref, late_ref, pool_ref, tokens_ref, out_ref, last_ref, page_ref, round_ref, deep_ref,
+    in_sem, out_sem, deep_sem,
+):
     devices = round_ref.shape[0]
+    deep = deep_ref.shape[0]
+    rim = last_ref.shape[0]
     ins = part_copies(pool_ref, page_ref, in_sem, PARTS)
     outs = part_copies(round_ref, out_ref, out_sem, PARTS)
+    rows = pltpu.make_async_copy(
+        tokens_ref.at[0, pl.ds(tokens_ref.shape[1] - deep, deep)], deep_ref, deep_sem
+    )
+    rows.start()
     for copy in ins:
         copy.start()
+    rows.wait()
+    last_ref[...] = deep_ref[...].astype(F32)[deep - rim :].astype(BF16)
     for copy in ins:
         copy.wait()
     for c in range(PARTS):
@@ -59,27 +70,33 @@
         copy.wait()
 
 
-def gather_pages(slot_early, slot_late, pool, devices):
+def gather_pages(slot_early, slot_late, pool, tokens, devices, rim):
     slots, rows, width = pool.shape
+    channels = tokens.shape[2]
     return pl.pallas_call(
         gather_body,
-        out_shape=jax.ShapeDtypeStruct((devices, rows, width), BF16),
+        out_shape=(
+            jax.ShapeDtypeStruct((devices, rows, width), BF16),
+            jax.ShapeDtypeStruct((rim, channels), BF16),
+        ),
         grid_spec=pltpu.PrefetchScalarGridSpec(
             num_scalar_prefetch=2,
             grid=(1,),
-            in_specs=[IN_HBM],
-            out_specs=IN_HBM,
+            in_specs=[IN_HBM, IN_HBM],
+            out_specs=[IN_HBM, pl.BlockSpec((rim, channels), lambda i, *s: (0, 0))],
             scratch_shapes=[
                 pltpu.VMEM((slots, rows, width), F32),
                 pltpu.VMEM((devices, rows, width), BF16),
+                pltpu.VMEM((16, channels), BF16),
                 pltpu.SemaphoreType.DMA((PARTS,)),
                 pltpu.SemaphoreType.DMA((PARTS,)),
+                pltpu.SemaphoreType.DMA,
             ],
         ),
         compiler_params=pltpu.CompilerParams(vmem_limit_bytes=GRANT),
         cost_estimate=cost(slots * rows * width, slots * rows * width * 6),
         name="gather_pages",
-    )(slot_early, slot_late, pool)
+    )(slot_early, slot_late, pool, tokens)
 
 
 def steps_body(id_ref, count_ref, raw_ref, bias_ref, alog_ref, cum_ref, shift_ref, ending_ref, decay_ref):
@@ -171,6 +188,7 @@
     lead = id_ref[1] == 0
     last = count_ref[id_ref[0]] - id_ref[1] * rows
     newest = 9 - taps + jnp.clip(last, 0, rows)
+    here = (count_ref[id_ref[0]] > rows) == (id_ref[1] == 1)
     if own:
 
         @pl.when(pl.program_id(0) == 0)
@@ -183,7 +201,7 @@
         rim = jnp.where(lead, cached, before_ref[:, lanes].astype(F32))
         rows_ref[slot, 9 - taps : 8] = rim
         rows_ref[slot, 8 : 8 + rows] = src[0, :, at : at + LANES].astype(F32)
-        tail_ref[:, lanes] = rows_ref[slot, pl.ds(newest, 8)].astype(BF16)
+        tail_ref[:, lanes] = jnp.where(here, rows_ref[slot, pl.ds(newest, 8)], 0.0).astype(BF16)
         total = bias_ref[:, lanes]
         weight = weight_ref[:, lanes]
         for k in range(taps):
@@ -275,65 +293,41 @@
     return pl.BlockSpec(decay.shape, lambda i, *s: (0, 0), memory_space=pltpu.SMEM)
 
 
-def outbound_body(
-    id_ref, prefix_ref, owner_ref, mine_ref, theirs_ref, own_hbm, recv_hbm, out_ref, own_ref, recv_ref,
-    page_ref, own_sem, recv_sem, sem,
-):
-    pages, rows, width = own_ref.shape
+def outbound_body(id_ref, prefix_ref, owner_ref, mine_ref, theirs_ref, own_ref, recv_ref, out_ref):
+    chunk, rows, width = own_ref.shape
+    pages = chunk * pl.num_programs(0)
     lead = id_ref[1] == 0
     keep = jnp.where(prefix_ref[id_ref[0]] > 0, 1.0, 0.0)
     top = lax.broadcasted_iota(jnp.int32, (TAIL, width), 0) == 0
-    own_in = part_copies(own_hbm, own_ref, own_sem, PARTS)
-    recv_in = part_copies(recv_hbm, recv_ref, recv_sem, PARTS)
-    for c in range(PARTS):
-        own_in[c].start()
-        recv_in[c].start()
-    outs = []
-    for c in range(PARTS):
-        own_in[c].wait()
-        recv_in[c].wait()
-        for k in range(pages // PARTS):
-            page = c * (pages // PARTS) + k
-            head = id_ref[1] * pages + page
-            mine, theirs = mine_ref[0, head], theirs_ref[0, head]
-            own_w = jnp.where(lead, theirs, 1.0)
-            recv_w = jnp.where(lead, 1.0, mine)
-            total = own_w * own_ref[page].astype(F32) + recv_w * recv_ref[page].astype(F32)
-            whole = jnp.full((TAIL, width), mine * theirs * keep, F32)
-            high = whole.astype(BF16).astype(F32)
-            page_ref[page, :rows] = total.astype(BF16)
-            page_ref[page, rows:] = jnp.where(top, high, whole - high).astype(BF16)
-        for k in range(pages // PARTS):
-            page = c * (pages // PARTS) + k
-            owner = owner_of(owner_ref, id_ref, page, pages)
-            copy = pltpu.make_async_copy(page_ref.at[page], out_ref.at[owner], sem.at[page])
-            copy.start()
-            outs.append(copy)
-    for copy in outs:
-        copy.wait()
+    for k in range(chunk):
+        page = pl.program_id(0) * chunk + k
+        head = id_ref[1] * pages + page
+        mine, theirs = mine_ref[0, head], theirs_ref[0, head]
+        own_w = jnp.where(lead, theirs, 1.0)
+        recv_w = jnp.where(lead, 1.0, mine)
+        total = own_w * own_ref[k].astype(F32) + recv_w * recv_ref[k].astype(F32)
+        whole = jnp.full((TAIL, width), mine * theirs * keep, F32)
+        high = whole.astype(BF16).astype(F32)
+        owner = owner_of(owner_ref, id_ref, page, pages)
+        out_ref[owner, :rows] = total.astype(BF16)
+        out_ref[owner, rows:] = jnp.where(top, high, whole - high).astype(BF16)
 
 
 def outbound_pages(ids, prefix, owners, mine, theirs, own, recv, devices):
     pages, rows, width = own.shape
+    chunk = pages // 2
     return pl.pallas_call(
         outbound_body,
         out_shape=jax.ShapeDtypeStruct((devices, rows + TAIL, width), BF16),
         grid_spec=pltpu.PrefetchScalarGridSpec(
             num_scalar_prefetch=2,
-            grid=(1,),
-            in_specs=[owner_block(owners), decay_block(mine), decay_block(theirs), IN_HBM, IN_HBM],
-            out_specs=IN_HBM,
-            scratch_shapes=[
-                pltpu.VMEM(own.shape, BF16),
-                pltpu.VMEM(own.shape, BF16),
-                pltpu.VMEM((pages, rows + TAIL, width), BF16),
-                pltpu.SemaphoreType.DMA((PARTS,)),
-                pltpu.SemaphoreType.DMA((PARTS,)),
-                pltpu.SemaphoreType.DMA((pages,)),
-            ],
+            grid=(pages // chunk,),
+            in_specs=[owner_block(owners), decay_block(mine), decay_block(theirs)]
+            + [pl.BlockSpec((chunk, rows, width), lambda i, *s: (i, 0, 0))] * 2,
+            out_specs=pl.BlockSpec((devices, rows + TAIL, width), lambda i, *s: (0, 0, 0)),
         ),
         compiler_params=pltpu.CompilerParams(vmem_limit_bytes=GRANT),
-        cost_estimate=cost(pages * rows * width * 3, pages * rows * width * 6),
+        cost_estimate=cost(pages * rows * width * 3, pages * rows * width * 8),
         name="outbound_pages",
     )(ids, prefix, owners, mine, theirs, own, recv)
 
@@ -587,14 +581,14 @@
     early = jnp.arange(2 * pages)[None, :] < pages
     slot_0 = jnp.max(jnp.where(matches & early, page_slot, -1), axis=1)
     slot_1 = jnp.max(jnp.where(matches & ~early, page_slot, -1), axis=1)
-    outgoing = gather_pages(slot_0, slot_1, state_pool, devices)
+    outgoing, last_rows = gather_pages(slot_0, slot_1, state_pool, conv_input, devices, rim)
     outgoing, conv_input, dt_raw, new_count, prefix_len, page_owner = lax.optimization_barrier(
         (outgoing, conv_input, dt_raw, new_count, prefix_len, page_owner)
     )
     incoming = lax.all_to_all(outgoing, ("req", "ctx"), split_axis=0, concat_axis=0, tiled=True)
 
     ids = jnp.stack([req_index, ctx_index]).astype(jnp.int32)
-    previous = lax.ppermute(conv_input[0, rows - rim :], "ctx", [(0, 1)])
+    previous = lax.ppermute(last_rows, "ctx", [(0, 1)])
     cum, shift, ending, decay_rows = step_tables(ids, new_count, dt_raw, dt_bias, a_log)
     other_decay = swapped(decay_rows)
 
@@ -611,8 +605,8 @@
     returned = lax.all_to_all(outbound, ("req", "ctx"), split_axis=0, concat_axis=0, tiled=True)
 
     start, send = start_states(*page_args, incoming, own_pages, recv_pages)
-    start, slot_0, slot_1, late_count, tail = lax.optimization_barrier(
-        (start, slot_0, slot_1, new_count, tail)
+    start, slot_0, slot_1, tail = lax.optimization_barrier(
+        (start, slot_0, slot_1, tail)
     )
     start_other = swapped(send)
     as_rows = lambda value: value.reshape(pages * page_rows, nstate)
@@ -625,11 +619,10 @@
         gate_input, norm_weight[None], mixed,
     )
 
-    other_tail = swapped(tail)
-    mine = (late_count[req_index] > rows) == (ctx_index == 1)
-    new_tail = jnp.where(mine, tail, other_tail)[:rim]
-    slot_ids = jnp.arange(slots, dtype=jnp.int32)[:, None]
-    request_ids = jnp.arange(requests, dtype=jnp.int32)[None, :]
+    new_tail = (tail + swapped(tail))[:rim]
+    slot_ids = lax.broadcasted_iota(jnp.int32, (slots, requests), 0)
+    request_ids = lax.broadcasted_iota(jnp.int32, (slots, requests), 1)
+    request_ids = jnp.where(slot_0[None, :] < -5, 0, request_ids)
     hits_0, hits_1 = slot_0[None, :] == slot_ids, slot_1[None, :] == slot_ids
     dev_of_slot = jnp.max(
         jnp.maximum(

time: 99.2 us -> 96.7 us (0.975)
  waiting for transfers between devices: 1.73 us -> 5.34 us
  local copies, waits for them, and re-layouts: 2.84 us -> 0 us
  starting transfers between devices: 26.9 us -> 24.5 us
    all_to_all x1, waiting for transfers between devices: 0.01 us -> 2.32 us  [local(): lax.all_to_all(outgoing, ('req', 'ctx'), split_axis=0, concat_axis=0, til...]
    all_to_all x1, starting transfers between devices: 10.2 us -> 7.9 us  [local(): lax.all_to_all(outbound, ('req', 'ctx'), split_axis=0, concat_axis=0, til...]
    squeeze x1 -> x0, local copies, waits for them, and re-layouts: 1.6 us -> none  [local(): previous = lax.ppermute(conv_input[0, rows - rim:], 'ctx', [(0, 1)])]
    all_to_all x1, waiting for transfers between devices: 1.71 us -> 3.01 us  [local(): lax.all_to_all(outbound, ('req', 'ctx'), split_axis=0, concat_axis=0, til...]
    dynamic_slice x1 -> x0, local copies, waits for them, and re-layouts: 1.24 us -> none  [local(): mine = (late_count[req_index] > rows) == (ctx_index == 1)]
  transfers between devices with their start and end apart: 7 -> 7, of which waited for: 1 -> 2; matrix products, arithmetic and copies ran while one was open for 7% -> 5% of each run, Pallas kernels for 51% -> 51%
where the time goes in v4:
time: 96.7 us; the launch traced here: 96 us
  Pallas kernels  59.4 us (61%)
  starting transfers between devices  24.5 us (25%)
  other arithmetic  5.83 us (6%)
  waiting for transfers between devices  5.34 us (6%)
    pallas_call x2, Pallas kernels, mixer_half(): pl.pallas_call(functools.partial(mixer_body, own), out_shape=jax.ShapeDty...  19.7 us
    pallas_call x2, Pallas kernels, conv_half(): pl.pallas_call(functools.partial(conv_body, own, (b_at, c_at)), out_shape...  17.5 us
    all_to_all x1, starting transfers between devices, local(): lax.all_to_all(outgoing, ('req', 'ctx'), split_axis=0, concat_axis=0, til...  12 us
    all_to_all x1, starting transfers between devices, local(): lax.all_to_all(outbound, ('req', 'ctx'), split_axis=0, concat_axis=0, til...  7.9 us
    pallas_call x1, Pallas kernels, updated_pool(): pl.pallas_call(pool_body, out_shape=jax.ShapeDtypeStruct(pool.shape, F32)...  5.63 us
    pallas_call x1, Pallas kernels, start_states(): pl.pallas_call(start_body, out_shape=(jax.ShapeDtypeStruct(own.shape, BF1...  5.07 us
    pallas_call x1, Pallas kernels, gather_pages(): pl.pallas_call(gather_body, out_shape=(jax.ShapeDtypeStruct((devices, row...  5.01 us
    pallas_call x1, Pallas kernels, outbound_pages(): pl.pallas_call(outbound_body, out_shape=jax.ShapeDtypeStruct((devices, ro...  3.86 us
  transfers between devices with their start and end apart: 7, of which 2 were waited for; matrix products, arithmetic and copies ran while one was open for 5% of the time, Pallas kernels for 51%

profile of v4, /device:TPU:1, one launch (start us, length us, event | category | flops | bytes accessed | tf_op | source)
XLA Modules:
  0.0 96.0 jit_solution(12264744646702002235)
XLA Ops:
  0.7 1.5 %select_reduce_fusion = (s32[64]{0:T(128)}, s32[64]{0:T(128)}) fusion(s32[64,128]{1,0:T(8,128)} %param.27, pred[128]{0:T(512)(128)(4,1)S(1)} %get-tuple-element.58, pred[128]{0:T(512)(128)(4,1)S(1)} %get-tuple-element.57, s32[64,128]{1,0:T(8,128)} %owner_ref.1, s32[]{:T(128)S(6)} %add.12), kind=kLoop, calls=%fused_computation.5 | loop fusion | flops 57216 | bytes 66308 | tf_op jit(solution)/shard_map/reduce_max | solution.py:583
  2.1 5.0 %gather_pages.1 = (bf16[128,64,128]{2,1,0:T(8,128)(2,1)}, bf16[3,10240]{1,0:T(4,128)(2,1)}) custom-call(s32[64]{0:T(128)} %get-tuple-element.53.early_ref, s32[64]{0:T(128)} %get-tuple-element.54.late_ref, f32[128,64,128]{2,1,0:T(8,128)} %pool_hbm.1, bf16[1,256,10240]{2,1,0:T(8,128)(2,1)} %c_ref.1), custom_call_target="tpu_custom_call" | custom-call | flops 1048576 | bytes 6291456 | tf_op jit(solution)/shard_map/gather_pages/pallas_call | solution.py:76
  7.2 12.0 %all-to-all-start = ((bf16[128,64,128]{2,1,0:T(8,128)(2,1)}), bf16[128,64,128]{2,1,0:T(8,128)(2,1)}, u32[]{:S(2)}, u32[]{:S(2)}) async-start(bf16[128,64,128]{2,1,0:T(8,128)(2,1)} %get-tuple-element.42), calls=%async_computation | async-start | bytes 4194304 | tf_op jit(solution)/shard_map/all_to_all | solution.py:588
  19.1 1.3 %collective-permute-start = (bf16[3,10240]{1,0:T(4,128)(2,1)}, bf16[3,10240]{1,0:T(4,128)(2,1)}, u32[]{:S(2)}, u32[]{:S(2)}) collective-permute-start(bf16[3,10240]{1,0:T(4,128)(2,1)} %get-tuple-element.33), channel_id=1, source_target_pairs={{0,1},{2,3},{4,5},{6,7},{8,9},{10,11},{12,13},{14,15},{16,17},{18,... | collective-permute-start | bytes 184328 | tf_op jit(solution)/shard_map/ppermute | solution.py:591
  20.4 0.7 pad_add_fusion.id_ref
  21.1 2.6 %step_tables.1 = (f32[256,128]{1,0:T(8,128)}, f32[128,256]{1,0:T(8,128)}, f32[256,128]{1,0:T(8,128)}, f32[8,128]{1,0:T(8,128)}) custom-call(s32[2]{0:T(128)} %pad_add_fusion.id_ref, s32[64]{0:T(128)} %count_ref.4, bf16[1,256,128]{2,1,0:T(8,128)(2,1)} %raw_ref, f32[1,128]{1,0:T(1,128)} %bitcast.19, f32[1,128]{1,0:T(1,128)} %bitcast.20), custom_call_target="tpu_custom_call" | custom-call | flops 50331648 | bytes 524288 | tf_op jit(solution)/shard_map/step_tables/pallas_call | solution.py:136
  23.7 0.0 collective-permute-done.before_ref
  23.7 8.7 %conv_half.2 = (bf16[256,4096]{1,0:T(8,128)(2,1)}, bf16[256,1024]{1,0:T(8,128)(2,1)}, bf16[4096,128]{1,0:T(8,128)(2,1)}, bf16[8,10240]{1,0:T(8,128)(2,1)}) custom-call(s32[2]{0:T(128)} %pad_add_fusion.id_ref, s32[64]{0:T(128)} %prefix_ref.3, s32[64]{0:T(128)} %count_ref.4, bf16[1,256,10240]{2,1,0:T(8,128)(2,1)} %c_ref.1, bf16[1,256,10240]{2,1,0:T(8,128)(2,1)} %c_ref.1, ...), custom_call_target="tpu_custom_call" | custom-call | flops 104857600 | bytes 5242880 | tf_op jit(solution)/shard_map/conv_half/pallas_call | solution.py:245
  32.4 1.8 %collective-permute-start.2 = (bf16[4096,128]{1,0:T(8,128)(2,1)}, bf16[4096,128]{1,0:T(8,128)(2,1)}, u32[]{:S(2)}, u32[]{:S(2)}) collective-permute-start(bf16[4096,128]{1,0:T(8,128)(2,1)} %get-tuple-element.45), channel_id=1, source_target_pairs={{0,1},{1,0},{2,3},{3,2},{4,5},{5,4},{6,7},{7,6},{8,9},{9,8},{10,11... | collective-permute-start | bytes 3145736 | tf_op jit(solution)/shard_map/ppermute | solution.py:22
  34.2 0.1 collective-permute-start.1
  34.3 8.8 %conv_half.3 = (bf16[256,4096]{1,0:T(8,128)(2,1)}, bf16[256,1024]{1,0:T(8,128)(2,1)}, bf16[4096,128]{1,0:T(8,128)(2,1)}, bf16[8,10240]{1,0:T(8,128)(2,1)}) custom-call(s32[2]{0:T(128)} %pad_add_fusion.id_ref, s32[64]{0:T(128)} %prefix_ref.3, s32[64]{0:T(128)} %count_ref.4, bf16[1,256,10240]{2,1,0:T(8,128)(2,1)} %c_ref.1, bf16[1,256,10240]{2,1,0:T(8,128)(2,1)} %c_ref.1, ...), custom_call_target="tpu_custom_call" | custom-call | flops 104857600 | bytes 5242880 | tf_op jit(solution)/shard_map/conv_half/pallas_call | solution.py:245
  43.1 0.0 collective-permute-done.1.theirs_ref
  43.1 0.0 collective-permute-done.2
  43.1 3.9 %outbound_pages.1 = bf16[128,72,128]{2,1,0:T(8,128)(2,1)} custom-call(s32[2]{0:T(128)} %pad_add_fusion.id_ref, s32[64]{0:T(128)} %prefix_ref.3, s32[64,128]{1,0:T(8,128)} %owner_ref.1, f32[8,128]{1,0:T(8,128)} %get-tuple-element.41.mine_ref, f32[8,128]{1,0:T(8,128)} %collective-permute-done.1.theirs_ref, bf16[64,64,128]{2,1,0:T(8,128)(2,1)} %bitcast.12, ...), custom_call_target="tpu_custom_call" | custom-call | flops 1572864 | bytes 4194304 | tf_op jit(solution)/shard_map/outbound_pages/pallas_call | solution.py:319
  47.0 2.3 %all-to-all-done.in_ref = bf16[128,64,128]{2,1,0:T(8,128)(2,1)} async-done(((bf16[128,64,128]{2,1,0:T(8,128)(2,1)}), bf16[128,64,128]{2,1,0:T(8,128)(2,1)}, u32[]{:S(2)}, u32[]{:S(2)}) %all-to-all-start) | async-done | bytes 2097184 | tf_op jit(solution)/shard_map/all_to_all | solution.py:588
  49.3 7.9 %all-to-all-start.1 = ((bf16[128,72,128]{2,1,0:T(8,128)(2,1)}), bf16[128,72,128]{2,1,0:T(8,128)(2,1)}, u32[]{:S(2)}, u32[]{:S(2)}) async-start(bf16[128,72,128]{2,1,0:T(8,128)(2,1)} %outbound_pages.1), calls=%async_computation.1 | async-start | bytes 4718592 | tf_op jit(solution)/shard_map/all_to_all | solution.py:605
  57.2 5.1 %start_states.1 = (bf16[64,64,128]{2,1,0:T(8,128)(2,1)}, bf16[64,64,128]{2,1,0:T(8,128)(2,1)}) custom-call(s32[2]{0:T(128)} %pad_add_fusion.id_ref, s32[64]{0:T(128)} %prefix_ref.3, s32[64,128]{1,0:T(8,128)} %owner_ref.1, f32[8,128]{1,0:T(8,128)} %get-tuple-element.41.mine_ref, f32[8,128]{1,0:T(8,128)} %collective-permute-done.1.theirs_ref, ...), custom_call_target="tpu_custom_call" | custom-call | flops 2097152 | bytes 4194304 | tf_op jit(solution)/shard_map/start_states/pallas_call | solution.py:380
  62.3 1.2 %collective-permute-start.3 = (bf16[64,64,128]{2,1,0:T(8,128)(2,1)}, bf16[64,64,128]{2,1,0:T(8,128)(2,1)}, u32[]{:S(2)}, u32[]{:S(2)}) collective-permute-start(bf16[64,64,128]{2,1,0:T(8,128)(2,1)} %get-tuple-element.46), channel_id=1, source_target_pairs={{0,1},{1,0},{2,3},{3,2},{4,5},{5,4},{6,7},{7,6},{8,9},{9,8},{10,11... | collective-permute-start | bytes 3145736 | tf_op jit(solution)/shard_map/ppermute | solution.py:22
  63.5 0.3 collective-permute-start.4
  63.8 0.7 broadcast_compare_fusion.1
  64.4 1.3 %maximum_reduce_fusion.dev_ref = s32[128]{0:T(128)} fusion(s32[64]{0:T(128)} %get-tuple-element.54.late_ref, s32[64]{0:T(128)} %get-tuple-element.53.early_ref, pred[64]{0:T(512)(128)(4,1)S(1)} %broadcast_compare_fusion.1), kind=kLoop, calls=%fused_computation.2 | loop fusion | flops 73600 | bytes 1088 | tf_op jit(solution)/shard_map/reduce_max | solution.py:627
  65.8 9.9 %mixer_half.2.rest_0_ = bf16[1,256,8192]{2,1,0:T(8,128)(2,1)} custom-call(s32[2]{0:T(128)} %pad_add_fusion.id_ref, s32[64]{0:T(128)} %count_ref.4, f32[128]{0:T(128)} %skip_ref.3, bf16[256,4096]{1,0:T(8,128)(2,1)} %get-tuple-element.47.x_ref, bf16[256,1024]{1,0:T(8,128)(2,1)} %get-tuple-element.48.bc_ref, f32[256,128]{1,0:T(8,128)} %get-tuple-element.38.cum_ref, ...), custom_call_target="tpu_custom_call" | custom-call | flops 805306368 | bytes 8388608 | tf_op jit(solution)/shard_map/mixer_half/pallas_call | solution.py:475
  75.7 0.0 collective-permute-done.4
  75.7 1.7 %fusion = bf16[1,3,10240]{2,1,0:T(4,128)(2,1)} fusion(bf16[8,10240]{1,0:T(8,128)(2,1)} %collective-permute-done.4, bf16[8,10240]{1,0:T(8,128)(2,1)} %get-tuple-element.52), kind=kLoop, calls=%fused_computation.1 | loop fusion | flops 30720 | bytes 184320 | tf_op jit(solution)/shard_map/broadcast_in_dim | solution.py:634
  77.3 0.0 collective-permute-done.3
  77.3 9.8 %mixer_half.3 = bf16[1,256,8192]{2,1,0:T(8,128)(2,1)} custom-call(s32[2]{0:T(128)} %pad_add_fusion.id_ref, s32[64]{0:T(128)} %count_ref.4, f32[128]{0:T(128)} %skip_ref.3, bf16[256,4096]{1,0:T(8,128)(2,1)} %get-tuple-element.36.x_ref, bf16[256,1024]{1,0:T(8,128)(2,1)} %get-tuple-element.37.bc_ref, ...), custom_call_target="tpu_custom_call", output_to_operand_aliasing={{}: (10, {})} | custom-call | flops 805306368 | bytes 8388608 | tf_op jit(solution)/shard_map/mixer_half/pallas_call | solution.py:475
  87.2 3.0 %all-to-all-done.1.in_hbm = bf16[128,72,128]{2,1,0:T(8,128)(2,1)} async-done(((bf16[128,72,128]{2,1,0:T(8,128)(2,1)}), bf16[128,72,128]{2,1,0:T(8,128)(2,1)}, u32[]{:S(2)}, u32[]{:S(2)}) %all-to-all-start.1) | async-done | bytes 2359328 | tf_op jit(solution)/shard_map/all_to_all | solution.py:605
  90.2 5.6 %updated_pool.1 = f32[128,64,128]{2,1,0:T(8,128)} custom-call(s32[128]{0:T(128)} %maximum_reduce_fusion.dev_ref, f32[128,64,128]{2,1,0:T(8,128)} %pool_hbm.1, bf16[128,72,128]{2,1,0:T(8,128)(2,1)} %all-to-all-done.1.in_hbm), custom_call_target="tpu_custom_call" | custom-call | flops 2097152 | bytes 10485760 | tf_op jit(solution)/shard_map/updated_pool/pallas_call | solution.py:527
  (1 shorter events, 0.0 us)
Async XLA Ops:
  7.2 42.1 %all-to-all-start = ((bf16[128,64,128]{2,1,0:T(8,128)(2,1)}), bf16[128,64,128]{2,1,0:T(8,128)(2,1)}, u32[]{:S(2)}, u32[]{:S(2)}) async-start(bf16[128,64,128]{2,1,0:T(8,128)(2,1)} %get-tuple-element.42), calls=%async_computation | async-start | bytes 4194304 | tf_op jit(solution)/shard_map/all_to_all | solution.py:588
  19.1 4.6 %collective-permute-start = (bf16[3,10240]{1,0:T(4,128)(2,1)}, bf16[3,10240]{1,0:T(4,128)(2,1)}, u32[]{:S(2)}, u32[]{:S(2)}) collective-permute-start(bf16[3,10240]{1,0:T(4,128)(2,1)} %get-tuple-element.33), channel_id=1, source_target_pairs={{0,1},{2,3},{4,5},{6,7},{8,9},{10,11},{12,13},{14,15},{16,17},{18,... | collective-permute-start | bytes 184328 | tf_op jit(solution)/shard_map/ppermute | solution.py:591
  32.4 10.7 %collective-permute-start.2 = (bf16[4096,128]{1,0:T(8,128)(2,1)}, bf16[4096,128]{1,0:T(8,128)(2,1)}, u32[]{:S(2)}, u32[]{:S(2)}) collective-permute-start(bf16[4096,128]{1,0:T(8,128)(2,1)} %get-tuple-element.45), channel_id=1, source_target_pairs={{0,1},{1,0},{2,3},{3,2},{4,5},{5,4},{6,7},{7,6},{8,9},{9,8},{10,11... | collective-permute-start | bytes 3145736 | tf_op jit(solution)/shard_map/ppermute | solution.py:22
  34.2 8.9 %collective-permute-start.1 = (f32[8,128]{1,0:T(8,128)}, f32[8,128]{1,0:T(8,128)}, u32[]{:S(2)}, u32[]{:S(2)}) collective-permute-start(f32[8,128]{1,0:T(8,128)} %get-tuple-element.41.mine_ref), channel_id=1, source_target_pairs={{0,1},{1,0},{2,3},{3,2},{4,5},{5,4},{6,7},{7,6},{8,9},{9,8},{10,11... | collective-permute-start | bytes 12296 | tf_op jit(solution)/shard_map/ppermute | solution.py:22
  49.3 40.9 %all-to-all-start.1 = ((bf16[128,72,128]{2,1,0:T(8,128)(2,1)}), bf16[128,72,128]{2,1,0:T(8,128)(2,1)}, u32[]{:S(2)}, u32[]{:S(2)}) async-start(bf16[128,72,128]{2,1,0:T(8,128)(2,1)} %outbound_pages.1), calls=%async_computation.1 | async-start | bytes 4718592 | tf_op jit(solution)/shard_map/all_to_all | solution.py:605
  62.3 15.0 %collective-permute-start.3 = (bf16[64,64,128]{2,1,0:T(8,128)(2,1)}, bf16[64,64,128]{2,1,0:T(8,128)(2,1)}, u32[]{:S(2)}, u32[]{:S(2)}) collective-permute-start(bf16[64,64,128]{2,1,0:T(8,128)(2,1)} %get-tuple-element.46), channel_id=1, source_target_pairs={{0,1},{1,0},{2,3},{3,2},{4,5},{5,4},{6,7},{7,6},{8,9},{9,8},{10,11... | collective-permute-start | bytes 3145736 | tf_op jit(solution)/shard_map/ppermute | solution.py:22
  63.5 12.2 %collective-permute-start.4 = (bf16[8,10240]{1,0:T(8,128)(2,1)}, bf16[8,10240]{1,0:T(8,128)(2,1)}, u32[]{:S(2)}, u32[]{:S(2)}) collective-permute-start(bf16[8,10240]{1,0:T(8,128)(2,1)} %get-tuple-element.52), channel_id=1, source_target_pairs={{0,1},{1,0},{2,3},{3,2},{4,5},{5,4},{6,7},{7,6},{8,9},{9,8},{10,11... | collective-permute-start | bytes 491528 | tf_op jit(solution)/shard_map/ppermute | solution.py:22

commit v5 on v4

--- a/solution.py
+++ b/solution.py
@@ -42,8 +42,8 @@
 
 
 def gather_body(
-    early_ref, late_ref, pool_ref, tokens_ref, out_ref, last_ref, page_ref, round_ref, deep_ref,
-    in_sem, out_sem, deep_sem,
+    early_ref, late_ref, pool_ref, tokens_ref, out_ref, last_hbm, page_ref, round_ref, deep_ref,
+    last_ref, in_sem, out_sem, deep_sem, last_sem,
 ):
     devices = round_ref.shape[0]
     deep = deep_ref.shape[0]
@@ -58,6 +58,8 @@
         copy.start()
     rows.wait()
     last_ref[...] = deep_ref[...].astype(F32)[deep - rim :].astype(BF16)
+    last = pltpu.make_async_copy(last_ref, last_hbm, last_sem)
+    last.start()
     for copy in ins:
         copy.wait()
     for c in range(PARTS):
@@ -66,6 +68,7 @@
             slot = (early_ref, late_ref)[device % 2][device // 2]
             round_ref[device] = page_ref[jnp.maximum(slot, 0)].astype(BF16)
         outs[c].start()
+    last.wait()
     for copy in outs:
         copy.wait()
 
@@ -83,13 +86,15 @@
             num_scalar_prefetch=2,
             grid=(1,),
             in_specs=[IN_HBM, IN_HBM],
-            out_specs=[IN_HBM, pl.BlockSpec((rim, channels), lambda i, *s: (0, 0))],
+            out_specs=[IN_HBM, IN_HBM],
             scratch_shapes=[
                 pltpu.VMEM((slots, rows, width), F32),
                 pltpu.VMEM((devices, rows, width), BF16),
                 pltpu.VMEM((16, channels), BF16),
+                pltpu.VMEM((rim, channels), BF16),
                 pltpu.SemaphoreType.DMA((PARTS,)),
                 pltpu.SemaphoreType.DMA((PARTS,)),
+                pltpu.SemaphoreType.DMA,
                 pltpu.SemaphoreType.DMA,
             ],
         ),

time: 96.7 us -> 96.1 us (level)
  no operation moved by 1% of the time
where the time goes in v5:
time: 96.1 us; the launch traced here: 95.3 us
  Pallas kernels  58.8 us (61%)
  starting transfers between devices  24.5 us (25%)
  other arithmetic  5.83 us (6%)
  waiting for transfers between devices  5.34 us (6%)
    pallas_call x2, Pallas kernels, mixer_half(): pl.pallas_call(functools.partial(mixer_body, own), out_shape=jax.ShapeDty...  19.7 us
    pallas_call x2, Pallas kernels, conv_half(): pl.pallas_call(functools.partial(conv_body, own, (b_at, c_at)), out_shape...  17.5 us
    all_to_all x1, starting transfers between devices, local(): lax.all_to_all(outgoing, ('req', 'ctx'), split_axis=0, concat_axis=0, til...  12 us
    all_to_all x1, starting transfers between devices, local(): lax.all_to_all(outbound, ('req', 'ctx'), split_axis=0, concat_axis=0, til...  7.89 us
    pallas_call x1, Pallas kernels, updated_pool(): pl.pallas_call(pool_body, out_shape=jax.ShapeDtypeStruct(pool.shape, F32)...  5.63 us
    pallas_call x1, Pallas kernels, start_states(): pl.pallas_call(start_body, out_shape=(jax.ShapeDtypeStruct(own.shape, BF1...  5.07 us
    pallas_call x1, Pallas kernels, gather_pages(): pl.pallas_call(gather_body, out_shape=(jax.ShapeDtypeStruct((devices, row...  4.39 us
    pallas_call x1, Pallas kernels, outbound_pages(): pl.pallas_call(outbound_body, out_shape=jax.ShapeDtypeStruct((devices, ro...  3.86 us
  transfers between devices with their start and end apart: 7, of which 2 were waited for; matrix products, arithmetic and copies ran while one was open for 5% of the time, Pallas kernels for 51%

profile of v5, /device:TPU:1, one launch (start us, length us, event | category | flops | bytes accessed | tf_op | source)
XLA Modules:
  0.0 95.3 jit_solution(1563337560864106281)
XLA Ops:
  0.7 1.5 %select_reduce_fusion = (s32[64]{0:T(128)}, s32[64]{0:T(128)}) fusion(s32[64,128]{1,0:T(8,128)} %param.27, pred[128]{0:T(512)(128)(4,1)S(1)} %get-tuple-element.58, pred[128]{0:T(512)(128)(4,1)S(1)} %get-tuple-element.57, s32[64,128]{1,0:T(8,128)} %owner_ref.1, s32[]{:T(128)S(6)} %add.12), kind=kLoop, calls=%fused_computation.5 | loop fusion | flops 57216 | bytes 66308 | tf_op jit(solution)/shard_map/reduce_max | solution.py:588
  2.1 4.4 %gather_pages.1 = (bf16[128,64,128]{2,1,0:T(8,128)(2,1)}, bf16[3,10240]{1,0:T(4,128)(2,1)}) custom-call(s32[64]{0:T(128)} %get-tuple-element.53.early_ref, s32[64]{0:T(128)} %get-tuple-element.54.late_ref, f32[128,64,128]{2,1,0:T(8,128)} %pool_hbm.1, bf16[1,256,10240]{2,1,0:T(8,128)(2,1)} %c_ref.1), custom_call_target="tpu_custom_call" | custom-call | flops 1048576 | bytes 6291456 | tf_op jit(solution)/shard_map/gather_pages/pallas_call | solution.py:79
  6.5 12.0 %all-to-all-start = ((bf16[128,64,128]{2,1,0:T(8,128)(2,1)}), bf16[128,64,128]{2,1,0:T(8,128)(2,1)}, u32[]{:S(2)}, u32[]{:S(2)}) async-start(bf16[128,64,128]{2,1,0:T(8,128)(2,1)} %get-tuple-element.42), calls=%async_computation | async-start | bytes 4194304 | tf_op jit(solution)/shard_map/all_to_all | solution.py:593
  18.5 1.3 %collective-permute-start = (bf16[3,10240]{1,0:T(4,128)(2,1)}, bf16[3,10240]{1,0:T(4,128)(2,1)}, u32[]{:S(2)}, u32[]{:S(2)}) collective-permute-start(bf16[3,10240]{1,0:T(4,128)(2,1)} %get-tuple-element.33), channel_id=1, source_target_pairs={{0,1},{2,3},{4,5},{6,7},{8,9},{10,11},{12,13},{14,15},{16,17},{18,... | collective-permute-start | bytes 184328 | tf_op jit(solution)/shard_map/ppermute | solution.py:596
  19.8 0.7 pad_add_fusion.id_ref
  20.5 2.6 %step_tables.1 = (f32[256,128]{1,0:T(8,128)}, f32[128,256]{1,0:T(8,128)}, f32[256,128]{1,0:T(8,128)}, f32[8,128]{1,0:T(8,128)}) custom-call(s32[2]{0:T(128)} %pad_add_fusion.id_ref, s32[64]{0:T(128)} %count_ref.4, bf16[1,256,128]{2,1,0:T(8,128)(2,1)} %raw_ref, f32[1,128]{1,0:T(1,128)} %bitcast.19, f32[1,128]{1,0:T(1,128)} %bitcast.20), custom_call_target="tpu_custom_call" | custom-call | flops 50331648 | bytes 524288 | tf_op jit(solution)/shard_map/step_tables/pallas_call | solution.py:141
  23.1 0.0 collective-permute-done.before_ref
  23.1 8.7 %conv_half.2 = (bf16[256,4096]{1,0:T(8,128)(2,1)}, bf16[256,1024]{1,0:T(8,128)(2,1)}, bf16[4096,128]{1,0:T(8,128)(2,1)}, bf16[8,10240]{1,0:T(8,128)(2,1)}) custom-call(s32[2]{0:T(128)} %pad_add_fusion.id_ref, s32[64]{0:T(128)} %prefix_ref.3, s32[64]{0:T(128)} %count_ref.4, bf16[1,256,10240]{2,1,0:T(8,128)(2,1)} %c_ref.1, bf16[1,256,10240]{2,1,0:T(8,128)(2,1)} %c_ref.1, ...), custom_call_target="tpu_custom_call" | custom-call | flops 104857600 | bytes 5242880 | tf_op jit(solution)/shard_map/conv_half/pallas_call | solution.py:250
  31.8 1.8 %collective-permute-start.2 = (bf16[4096,128]{1,0:T(8,128)(2,1)}, bf16[4096,128]{1,0:T(8,128)(2,1)}, u32[]{:S(2)}, u32[]{:S(2)}) collective-permute-start(bf16[4096,128]{1,0:T(8,128)(2,1)} %get-tuple-element.45), channel_id=1, source_target_pairs={{0,1},{1,0},{2,3},{3,2},{4,5},{5,4},{6,7},{7,6},{8,9},{9,8},{10,11... | collective-permute-start | bytes 3145736 | tf_op jit(solution)/shard_map/ppermute | solution.py:22
  33.6 0.1 collective-permute-start.1
  33.7 8.8 %conv_half.3 = (bf16[256,4096]{1,0:T(8,128)(2,1)}, bf16[256,1024]{1,0:T(8,128)(2,1)}, bf16[4096,128]{1,0:T(8,128)(2,1)}, bf16[8,10240]{1,0:T(8,128)(2,1)}) custom-call(s32[2]{0:T(128)} %pad_add_fusion.id_ref, s32[64]{0:T(128)} %prefix_ref.3, s32[64]{0:T(128)} %count_ref.4, bf16[1,256,10240]{2,1,0:T(8,128)(2,1)} %c_ref.1, bf16[1,256,10240]{2,1,0:T(8,128)(2,1)} %c_ref.1, ...), custom_call_target="tpu_custom_call" | custom-call | flops 104857600 | bytes 5242880 | tf_op jit(solution)/shard_map/conv_half/pallas_call | solution.py:250
  42.5 0.0 collective-permute-done.1.theirs_ref
  42.5 0.0 collective-permute-done.2
  42.5 3.9 %outbound_pages.1 = bf16[128,72,128]{2,1,0:T(8,128)(2,1)} custom-call(s32[2]{0:T(128)} %pad_add_fusion.id_ref, s32[64]{0:T(128)} %prefix_ref.3, s32[64,128]{1,0:T(8,128)} %owner_ref.1, f32[8,128]{1,0:T(8,128)} %get-tuple-element.41.mine_ref, f32[8,128]{1,0:T(8,128)} %collective-permute-done.1.theirs_ref, bf16[64,64,128]{2,1,0:T(8,128)(2,1)} %bitcast.12, ...), custom_call_target="tpu_custom_call" | custom-call | flops 1572864 | bytes 4194304 | tf_op jit(solution)/shard_map/outbound_pages/pallas_call | solution.py:324
  46.4 2.3 %all-to-all-done.in_ref = bf16[128,64,128]{2,1,0:T(8,128)(2,1)} async-done(((bf16[128,64,128]{2,1,0:T(8,128)(2,1)}), bf16[128,64,128]{2,1,0:T(8,128)(2,1)}, u32[]{:S(2)}, u32[]{:S(2)}) %all-to-all-start) | async-done | bytes 2097184 | tf_op jit(solution)/shard_map/all_to_all | solution.py:593
  48.7 7.9 %all-to-all-start.1 = ((bf16[128,72,128]{2,1,0:T(8,128)(2,1)}), bf16[128,72,128]{2,1,0:T(8,128)(2,1)}, u32[]{:S(2)}, u32[]{:S(2)}) async-start(bf16[128,72,128]{2,1,0:T(8,128)(2,1)} %outbound_pages.1), calls=%async_computation.1 | async-start | bytes 4718592 | tf_op jit(solution)/shard_map/all_to_all | solution.py:610
  56.6 5.1 %start_states.1 = (bf16[64,64,128]{2,1,0:T(8,128)(2,1)}, bf16[64,64,128]{2,1,0:T(8,128)(2,1)}) custom-call(s32[2]{0:T(128)} %pad_add_fusion.id_ref, s32[64]{0:T(128)} %prefix_ref.3, s32[64,128]{1,0:T(8,128)} %owner_ref.1, f32[8,128]{1,0:T(8,128)} %get-tuple-element.41.mine_ref, f32[8,128]{1,0:T(8,128)} %collective-permute-done.1.theirs_ref, ...), custom_call_target="tpu_custom_call" | custom-call | flops 2097152 | bytes 4194304 | tf_op jit(solution)/shard_map/start_states/pallas_call | solution.py:385
  61.7 1.2 %collective-permute-start.3 = (bf16[64,64,128]{2,1,0:T(8,128)(2,1)}, bf16[64,64,128]{2,1,0:T(8,128)(2,1)}, u32[]{:S(2)}, u32[]{:S(2)}) collective-permute-start(bf16[64,64,128]{2,1,0:T(8,128)(2,1)} %get-tuple-element.46), channel_id=1, source_target_pairs={{0,1},{1,0},{2,3},{3,2},{4,5},{5,4},{6,7},{7,6},{8,9},{9,8},{10,11... | collective-permute-start | bytes 3145736 | tf_op jit(solution)/shard_map/ppermute | solution.py:22
  62.9 0.3 collective-permute-start.4
  63.1 0.7 broadcast_compare_fusion.1
  63.8 1.3 %maximum_reduce_fusion.dev_ref = s32[128]{0:T(128)} fusion(s32[64]{0:T(128)} %get-tuple-element.54.late_ref, s32[64]{0:T(128)} %get-tuple-element.53.early_ref, pred[64]{0:T(512)(128)(4,1)S(1)} %broadcast_compare_fusion.1), kind=kLoop, calls=%fused_computation.2 | loop fusion | flops 73600 | bytes 1088 | tf_op jit(solution)/shard_map/reduce_max | solution.py:632
  65.2 9.9 %mixer_half.2.rest_0_ = bf16[1,256,8192]{2,1,0:T(8,128)(2,1)} custom-call(s32[2]{0:T(128)} %pad_add_fusion.id_ref, s32[64]{0:T(128)} %count_ref.4, f32[128]{0:T(128)} %skip_ref.3, bf16[256,4096]{1,0:T(8,128)(2,1)} %get-tuple-element.47.x_ref, bf16[256,1024]{1,0:T(8,128)(2,1)} %get-tuple-element.48.bc_ref, f32[256,128]{1,0:T(8,128)} %get-tuple-element.38.cum_ref, ...), custom_call_target="tpu_custom_call" | custom-call | flops 805306368 | bytes 8388608 | tf_op jit(solution)/shard_map/mixer_half/pallas_call | solution.py:480
  75.0 0.0 collective-permute-done.4
  75.0 1.7 %fusion = bf16[1,3,10240]{2,1,0:T(4,128)(2,1)} fusion(bf16[8,10240]{1,0:T(8,128)(2,1)} %collective-permute-done.4, bf16[8,10240]{1,0:T(8,128)(2,1)} %get-tuple-element.52), kind=kLoop, calls=%fused_computation.1 | loop fusion | flops 30720 | bytes 184320 | tf_op jit(solution)/shard_map/broadcast_in_dim | solution.py:639
  76.7 0.0 collective-permute-done.3
  76.7 9.8 %mixer_half.3 = bf16[1,256,8192]{2,1,0:T(8,128)(2,1)} custom-call(s32[2]{0:T(128)} %pad_add_fusion.id_ref, s32[64]{0:T(128)} %count_ref.4, f32[128]{0:T(128)} %skip_ref.3, bf16[256,4096]{1,0:T(8,128)(2,1)} %get-tuple-element.36.x_ref, bf16[256,1024]{1,0:T(8,128)(2,1)} %get-tuple-element.37.bc_ref, ...), custom_call_target="tpu_custom_call", output_to_operand_aliasing={{}: (10, {})} | custom-call | flops 805306368 | bytes 8388608 | tf_op jit(solution)/shard_map/mixer_half/pallas_call | solution.py:480
  86.5 3.0 %all-to-all-done.1.in_hbm = bf16[128,72,128]{2,1,0:T(8,128)(2,1)} async-done(((bf16[128,72,128]{2,1,0:T(8,128)(2,1)}), bf16[128,72,128]{2,1,0:T(8,128)(2,1)}, u32[]{:S(2)}, u32[]{:S(2)}) %all-to-all-start.1) | async-done | bytes 2359328 | tf_op jit(solution)/shard_map/all_to_all | solution.py:610
  89.5 5.6 %updated_pool.1 = f32[128,64,128]{2,1,0:T(8,128)} custom-call(s32[128]{0:T(128)} %maximum_reduce_fusion.dev_ref, f32[128,64,128]{2,1,0:T(8,128)} %pool_hbm.1, bf16[128,72,128]{2,1,0:T(8,128)(2,1)} %all-to-all-done.1.in_hbm), custom_call_target="tpu_custom_call" | custom-call | flops 2097152 | bytes 10485760 | tf_op jit(solution)/shard_map/updated_pool/pallas_call | solution.py:532
  (1 shorter events, 0.0 us)
Async XLA Ops:
  6.5 42.1 %all-to-all-start = ((bf16[128,64,128]{2,1,0:T(8,128)(2,1)}), bf16[128,64,128]{2,1,0:T(8,128)(2,1)}, u32[]{:S(2)}, u32[]{:S(2)}) async-start(bf16[128,64,128]{2,1,0:T(8,128)(2,1)} %get-tuple-element.42), calls=%async_computation | async-start | bytes 4194304 | tf_op jit(solution)/shard_map/all_to_all | solution.py:593
  18.5 4.6 %collective-permute-start = (bf16[3,10240]{1,0:T(4,128)(2,1)}, bf16[3,10240]{1,0:T(4,128)(2,1)}, u32[]{:S(2)}, u32[]{:S(2)}) collective-permute-start(bf16[3,10240]{1,0:T(4,128)(2,1)} %get-tuple-element.33), channel_id=1, source_target_pairs={{0,1},{2,3},{4,5},{6,7},{8,9},{10,11},{12,13},{14,15},{16,17},{18,... | collective-permute-start | bytes 184328 | tf_op jit(solution)/shard_map/ppermute | solution.py:596
  31.8 10.7 %collective-permute-start.2 = (bf16[4096,128]{1,0:T(8,128)(2,1)}, bf16[4096,128]{1,0:T(8,128)(2,1)}, u32[]{:S(2)}, u32[]{:S(2)}) collective-permute-start(bf16[4096,128]{1,0:T(8,128)(2,1)} %get-tuple-element.45), channel_id=1, source_target_pairs={{0,1},{1,0},{2,3},{3,2},{4,5},{5,4},{6,7},{7,6},{8,9},{9,8},{10,11... | collective-permute-start | bytes 3145736 | tf_op jit(solution)/shard_map/ppermute | solution.py:22
  33.6 8.9 %collective-permute-start.1 = (f32[8,128]{1,0:T(8,128)}, f32[8,128]{1,0:T(8,128)}, u32[]{:S(2)}, u32[]{:S(2)}) collective-permute-start(f32[8,128]{1,0:T(8,128)} %get-tuple-element.41.mine_ref), channel_id=1, source_target_pairs={{0,1},{1,0},{2,3},{3,2},{4,5},{5,4},{6,7},{7,6},{8,9},{9,8},{10,11... | collective-permute-start | bytes 12296 | tf_op jit(solution)/shard_map/ppermute | solution.py:22
  48.7 40.9 %all-to-all-start.1 = ((bf16[128,72,128]{2,1,0:T(8,128)(2,1)}), bf16[128,72,128]{2,1,0:T(8,128)(2,1)}, u32[]{:S(2)}, u32[]{:S(2)}) async-start(bf16[128,72,128]{2,1,0:T(8,128)(2,1)} %outbound_pages.1), calls=%async_computation.1 | async-start | bytes 4718592 | tf_op jit(solution)/shard_map/all_to_all | solution.py:610
  61.7 15.0 %collective-permute-start.3 = (bf16[64,64,128]{2,1,0:T(8,128)(2,1)}, bf16[64,64,128]{2,1,0:T(8,128)(2,1)}, u32[]{:S(2)}, u32[]{:S(2)}) collective-permute-start(bf16[64,64,128]{2,1,0:T(8,128)(2,1)} %get-tuple-element.46), channel_id=1, source_target_pairs={{0,1},{1,0},{2,3},{3,2},{4,5},{5,4},{6,7},{7,6},{8,9},{9,8},{10,11... | collective-permute-start | bytes 3145736 | tf_op jit(solution)/shard_map/ppermute | solution.py:22
  62.9 12.2 %collective-permute-start.4 = (bf16[8,10240]{1,0:T(8,128)(2,1)}, bf16[8,10240]{1,0:T(8,128)(2,1)}, u32[]{:S(2)}, u32[]{:S(2)}) collective-permute-start(bf16[8,10240]{1,0:T(8,128)(2,1)} %get-tuple-element.52), channel_id=1, source_target_pairs={{0,1},{1,0},{2,3},{3,2},{4,5},{5,4},{6,7},{7,6},{8,9},{9,8},{10,11... | collective-permute-start | bytes 491528 | tf_op jit(solution)/shard_map/ppermute | solution.py:22
